TPU v7x, 128 devices: a whole 4x4x4 slice. The times are simulated.
128 devices in a mesh: row: 8 (over x_lo, y), col: 16 (over x_hi, z, core).
Axes of the slice: x: 4 (x_hi: 2, x_lo: 2; x = x_hi * 2 + x_lo), y: 4, z: 4, core: 2. Of those that a mesh axis runs over, the one named last changes fastest.
Arguments:
- features: bfloat16 [262144, 256], P(('col', 'row')), may hold values from -6 to 6
- weight: bfloat16 [256, 256], replicated, may hold values from -0.375 to 0.375
- adj_rows: int32 [8, 16, 128], P('row', 'col'), may hold values from 0 to 255, as said below
- adj_cols: int32 [8, 16, 128], P('row', 'col'), may hold values from 0 to 127
- adj_blocks: bfloat16 [8, 16, 128, 128, 128], P('row', 'col'), as said below
- counts: int32 [8, 16], P('row', 'col'), may hold values from 1 to 128, as said below
- grad_out: bfloat16 [262144, 256], P(('col', 'row')), may hold values from -6 to 6
Outputs:
- out_col: bfloat16 [262144, 256], P(('col', 'row'))
- weight_grad: float32 [256, 256], replicated
Inputs may be any that keep to these rules, and one draw needn't show every extreme that they name: `adj_rows`: in every grid cell, slot k's block-row lies in [(k % 16) * 16, (k % 16 + 1) * 16), and no two slots of a cell share a block-row. At least one grid cell has all 128 slots live; live slots are the first counts of a cell. `adj_blocks`: each block holds nonnegative edge weights.
All inputs are finite; a program needn't handle non-finite values.
Results may differ from a plain program's by a relative error of at most 0.015.
Values may be sent and summed in bfloat16 or wider, within the bound.
No kernel may reach another device: no remote copies, remote signals or barrier semaphores. Data moves between devices by JAX's collectives and lax.ppermute only.
A program may use at most 128 MiB of HBM per device.

v0:
```python
import jax
import jax.numpy as jnp
from jax import lax
from jax.sharding import PartitionSpec as P

VBLK = 16


def group_products(col_blocks, slab_cols, blocks, live_count, first_slot, group):
    cols_here = lax.dynamic_slice_in_dim(slab_cols, first_slot, group)
    blocks_here = lax.dynamic_slice_in_dim(blocks, first_slot, group, 0)
    live_mask = first_slot + jnp.arange(group) < live_count
    picked = col_blocks[cols_here]
    products = jnp.einsum("kil,klf->kif", blocks_here, picked, preferred_element_type=jnp.float32)
    return jnp.where(live_mask[:, None, None], products, 0.0).astype(jnp.bfloat16)


def dense_partial(col_blocks, slab_rows, slab_cols, blocks, live_count, row_blocks, group):
    block_size = blocks.shape[-1]
    feat_width = col_blocks.shape[-1]
    turns = (live_count + group - 1) // group

    def one_group(group_idx, running):
        first_slot = group_idx * group
        rows_here = lax.dynamic_slice_in_dim(slab_rows, first_slot, group)
        products = group_products(col_blocks, slab_cols, blocks, live_count, first_slot, group)
        return running.at[rows_here].add(products)

    start_value = jnp.zeros((row_blocks, block_size, feat_width), jnp.bfloat16)
    running = lax.fori_loop(0, turns, one_group, start_value)
    return running.reshape(row_blocks * block_size, feat_width)


def derivative(preact, grad_rows):
    sigmoid_pre = jax.nn.sigmoid(preact)
    return (
        grad_rows.astype(jnp.float32) * sigmoid_pre * (1.0 + preact * (1.0 - sigmoid_pre))
    ).astype(jnp.bfloat16)


def on_device(features, weight, adj_rows, adj_cols, adj_blocks, counts, grad_out):
    feat_width = features.shape[1]
    local_rows = features.shape[0]
    owners = lax.axis_size("col")
    devices_all = lax.axis_size("row") * owners
    piece_rows = local_rows // devices_all
    block_size = adj_blocks.shape[-1]
    slot_total = adj_blocks.shape[2]
    group = min(32, slot_total)
    row_blocks = VBLK * owners
    slab = lax.all_gather(features, "row", axis=0, tiled=True)
    col_blocks = slab.reshape(-1, block_size, feat_width)
    slab_rows = adj_rows[0, 0]
    slab_cols = adj_cols[0, 0]
    blocks = adj_blocks[0, 0]
    live_count = counts[0, 0]
    partial_value = dense_partial(
        col_blocks, slab_rows, slab_cols, blocks, live_count, row_blocks, group
    )
    agg = (
        lax.psum_scatter(partial_value, "col", scatter_dimension=0, tiled=True)
        .astype(jnp.float32)
        .astype(jnp.bfloat16)
    )
    preact = jnp.dot(agg, weight, preferred_element_type=jnp.float32)
    out_row = jax.nn.silu(preact).astype(jnp.bfloat16)
    contract = (((0,), (0,)), ((), ()))
    moved = lax.all_to_all(
        out_row.reshape(devices_all, piece_rows, feat_width),
        ("row", "col"),
        split_axis=0,
        concat_axis=0,
        tiled=True,
    )
    out_col = moved.reshape(local_rows, feat_width)
    grad_row = lax.all_to_all(
        grad_out.reshape(devices_all, piece_rows, feat_width),
        ("row", "col"),
        split_axis=0,
        concat_axis=0,
        tiled=True,
    )
    grad_pre = derivative(preact, grad_row.reshape(local_rows, feat_width))
    weight_part = lax.dot_general(agg, grad_pre, contract, preferred_element_type=jnp.float32)
    weight_grad = lax.psum(weight_part, ("row", "col")) * (local_rows * devices_all) ** (-0.5)
    return (out_col, weight_grad)


def solution(mesh):
    placed = (
        P(("col", "row"), None),
        P(),
        P("row", "col", None),
        P("row", "col", None),
        P("row", "col", None, None, None),
        P("row", "col"),
        P(("col", "row"), None),
    )
    return jax.shard_map(
        on_device,
        mesh=mesh,
        in_specs=placed,
        out_specs=(P(("col", "row"), None), P()),
        check_vma=False,
    )
```

profile of v0, /device:TPU:1, one launch (start us, length us, event | category | flops | bytes accessed | tf_op | source)
XLA Modules:
  0.0 496.8 jit_solution(323156815200104506)
XLA Ops:
  8.6 96.2 %all-gather.2.cloned.1.call-done = bf16[16384,256]{1,0:T(8,128)(2,1)} async-done(((bf16[2048,256]{1,0:T(8,128)(2,1)}), bf16[16384,256]{1,0:T(8,128)(2,1)}) %all-gather.2.cloned.1.call-update) | async-done | bytes 8388624 | tf_op jit(solution)/shard_map/all_gather | solution.py:51
  104.8 6.0 %broadcast_in_dim.22 = bf16[256,128,256]{2,1,0:T(8,128)(2,1)} broadcast(bf16[]{:T(256)} %constant.35.clone.1), dimensions={} | broadcast | bytes 16777218 | tf_op jit(solution)/shard_map/broadcast_in_dim | solution.py:29
  110.8 72.4 %while.10 = (s32[]{:T(128)}, bf16[256,128,256]{2,1,0:T(8,128)(2,1)}, s32[]{:T(128)}, s32[128]{0:T(128)S(1)}, s32[]{:T(128)}, /*index=5*/bf16[128,128,128]{2,1,0:...) while((s32[]{:T(128)}, ...), condition=%wide.region_2.3_spmd, body=%wide.region_0.2_spmd.sunk | while | flops 271582464 | bytes 15733875 | solution.py:30
  110.9 5.4 %gather_fusion = bf16[32,128,256]{2,1,0:T(8,128)(2,1)} fusion(bf16[128,128,256]{2,1,0:T(8,128)(2,1)} %get-tuple-element.151, s32[1024]{0:T(1024)S(1)} %pad_clamp_fusion.2), kind=kCustom, calls=%fused_computation.clone.1 | custom fusion | bytes 4194432 | tf_op jit(solution)/shard_map/while/body/gather | solution.py:13
  117.0 2.6 select_convert_fusion.2
  119.6 9.3 %scatter_fusion = bf16[256,128,256]{2,1,0:T(8,128)(2,1)} fusion(bf16[256,128,256]{2,1,0:T(8,128)(2,1)} %get-tuple-element.133, s32[32]{0:T(128)S(1)} %get-tuple-element.118, bf16[32,128,256]{2,1,0:T(8,128)(2,1)S(1)} %select_convert_fusion.2), kind=kCustom, calls=%fused_computation.1.clone.1 | custom fusion | flops 1048576 | bytes 6291584 | tf_op jit(solution)/shard_map/while/body/scatter-add | solution.py:27
  129.0 5.4 %gather_fusion = bf16[32,128,256]{2,1,0:T(8,128)(2,1)} fusion(bf16[128,128,256]{2,1,0:T(8,128)(2,1)} %get-tuple-element.151, s32[1024]{0:T(1024)S(1)} %pad_clamp_fusion.2), kind=kCustom, calls=%fused_computation.clone.1 | custom fusion | bytes 4194432 | tf_op jit(solution)/shard_map/while/body/gather | solution.py:13
  135.0 2.6 select_convert_fusion.2
  137.7 9.4 %scatter_fusion = bf16[256,128,256]{2,1,0:T(8,128)(2,1)} fusion(bf16[256,128,256]{2,1,0:T(8,128)(2,1)} %get-tuple-element.133, s32[32]{0:T(128)S(1)} %get-tuple-element.118, bf16[32,128,256]{2,1,0:T(8,128)(2,1)S(1)} %select_convert_fusion.2), kind=kCustom, calls=%fused_computation.1.clone.1 | custom fusion | flops 1048576 | bytes 6291584 | tf_op jit(solution)/shard_map/while/body/scatter-add | solution.py:27
  147.2 5.4 %gather_fusion = bf16[32,128,256]{2,1,0:T(8,128)(2,1)} fusion(bf16[128,128,256]{2,1,0:T(8,128)(2,1)} %get-tuple-element.151, s32[1024]{0:T(1024)S(1)} %pad_clamp_fusion.2), kind=kCustom, calls=%fused_computation.clone.1 | custom fusion | bytes 4194432 | tf_op jit(solution)/shard_map/while/body/gather | solution.py:13
  153.2 2.6 select_convert_fusion.2
  155.9 9.3 %scatter_fusion = bf16[256,128,256]{2,1,0:T(8,128)(2,1)} fusion(bf16[256,128,256]{2,1,0:T(8,128)(2,1)} %get-tuple-element.133, s32[32]{0:T(128)S(1)} %get-tuple-element.118, bf16[32,128,256]{2,1,0:T(8,128)(2,1)S(1)} %select_convert_fusion.2), kind=kCustom, calls=%fused_computation.1.clone.1 | custom fusion | flops 1048576 | bytes 6291584 | tf_op jit(solution)/shard_map/while/body/scatter-add | solution.py:27
  165.3 5.4 %gather_fusion = bf16[32,128,256]{2,1,0:T(8,128)(2,1)} fusion(bf16[128,128,256]{2,1,0:T(8,128)(2,1)} %get-tuple-element.151, s32[1024]{0:T(1024)S(1)} %pad_clamp_fusion.2), kind=kCustom, calls=%fused_computation.clone.1 | custom fusion | bytes 4194432 | tf_op jit(solution)/shard_map/while/body/gather | solution.py:13
  171.3 2.6 select_convert_fusion.2
  174.0 9.3 %scatter_fusion = bf16[256,128,256]{2,1,0:T(8,128)(2,1)} fusion(bf16[256,128,256]{2,1,0:T(8,128)(2,1)} %get-tuple-element.133, s32[32]{0:T(128)S(1)} %get-tuple-element.118, bf16[32,128,256]{2,1,0:T(8,128)(2,1)S(1)} %select_convert_fusion.2), kind=kCustom, calls=%fused_computation.1.clone.1 | custom fusion | flops 1048576 | bytes 6291584 | tf_op jit(solution)/shard_map/while/body/scatter-add | solution.py:27
  183.3 1.2 copy-done.1
  184.5 25.6 %all_to_all.10 = bf16[128,16,256]{2,1,0:T(8,128)(2,1)S(1)} all-to-all(bf16[128,16,256]{2,1,0:T(8,128)(2,1)S(1)} %bitcast.24), channel_id=1, replica_groups=mesh['row'=8,'col'=16] {'row','col'}, dimensions={0} | all-to-all | bytes 2097152 | tf_op jit(solution)/shard_map/all_to_all | solution.py:76
  210.1 118.2 %reduce-scatter.2.cloned.1.call-done = bf16[2048,256]{1,0:T(8,128)(2,1)} async-done(((bf16[32768,256]{1,0:T(8,128)(2,1)}), bf16[2048,256]{1,0:T(8,128)(2,1)}) %reduce-scatter.2.cloned.1.call-update) | async-done | bytes 1048592 | tf_op jit(solution)/shard_map/reduce_scatter | solution.py:61
  328.4 3.4 fusion.3
  331.8 6.6 %all-to-all-start = ((bf16[128,16,256]{2,1,0:T(8,128)(2,1)}), bf16[128,16,256]{2,1,0:T(8,128)(2,1)S(1)}, u32[]{:S(2)}, u32[]{:S(2)}) async-start(bf16[128,16,256]{2,1,0:T(8,128)(2,1)} %bitcast.6), calls=%async_computation.1 | async-start | bytes 2097152 | tf_op jit(solution)/shard_map/all_to_all | solution.py:68
  338.5 1.2 fusion.4
  339.7 148.0 %all-reduce.2.cloned.1.call-done = f32[256,256]{1,0:T(8,128)} async-done(((f32[256,256]{1,0:T(8,128)}), f32[256,256]{1,0:T(8,128)}) %all-reduce.2.cloned.1.call-update) | async-done | bytes 262160 | tf_op jit(solution)/shard_map/psum | solution.py:85
  487.7 1.7 broadcast_multiply_fusion
  489.3 1.0 copy.19
  (28 shorter events, 3.8 us)
Async XLA Ops:
  7.2 321.2 %copy-start = (bf16[256,256]{1,0:T(8,128)(2,1)S(1)}, bf16[256,256]{1,0:T(8,128)(2,1)}, u32[]{:S(2)}) copy-start(bf16[256,256]{1,0:T(8,128)(2,1)} %param.10) | copy-start | bytes 393220
  7.2 97.6 %all-gather.2.cloned.1.call-start = ((), (), s32[]{:S(2)}) async-start(), calls=%async_computation.3 | async-start | bytes 9437184 | tf_op jit(solution)/shard_map/all_gather | solution.py:51
  7.9 320.5 %reduce-scatter.2.cloned.1.call-start = ((), (), s32[]{:S(2)}) async-start(), calls=%async_computation.4 | async-start | bytes 17825792 | tf_op jit(solution)/shard_map/reduce_scatter | solution.py:61
  104.8 6.0 %copy-start.3 = (s32[1,1,128]{2,1,0:T(1,128)S(1)}, s32[1,1,128]{2,1,0:T(1,128)}, u32[]{:S(2)}) copy-start(s32[1,1,128]{2,1,0:T(1,128)} %param.11) | copy-start | bytes 1540
  104.8 6.0 %copy-start.4 = (s32[1,1,128]{2,1,0:T(1,128)S(1)}, s32[1,1,128]{2,1,0:T(1,128)}, u32[]{:S(2)}) copy-start(s32[1,1,128]{2,1,0:T(1,128)} %param.12) | copy-start | bytes 1540
  183.3 1.2 copy-start.1
  331.8 6.7 %copy-start.2 = (bf16[2048,256]{1,0:T(8,128)(2,1)S(1)}, bf16[2048,256]{1,0:T(8,128)(2,1)}, u32[]{:S(2)}) copy-start(bf16[2048,256]{1,0:T(8,128)(2,1)} %reduce-scatter.2.cloned.1.call-done) | copy-start | bytes 3145732
  331.8 157.6 %all-to-all-start = ((bf16[128,16,256]{2,1,0:T(8,128)(2,1)}), bf16[128,16,256]{2,1,0:T(8,128)(2,1)S(1)}, u32[]{:S(2)}, u32[]{:S(2)}) async-start(bf16[128,16,256]{2,1,0:T(8,128)(2,1)} %bitcast.6), calls=%async_computation.1 | async-start | bytes 2097152 | tf_op jit(solution)/shard_map/all_to_all | solution.py:68
  338.4 149.3 %all-reduce.2.cloned.1.call-start = ((), (), s32[]{:S(2)}) async-start(), calls=%async_computation.5 | async-start | bytes 524288 | tf_op jit(solution)/shard_map/psum | solution.py:85
Sparse Core Ops, SparseCore 0:
  9.7 95.1 all-gather.1
  183.4 144.9 reduce-scatter.1
  344.6 143.0 all-reduce.1
where the time goes:
time: 498 us; the launch traced here: 497 us
  waiting for transfers between devices  363 us (73%)
  other arithmetic  41.9 us (8%)
  local copies, waits for them, and re-layouts  29.9 us (6%)
  blocking collectives  25.6 us (5%)
  matrix products  15 us (3%)
  between operations  14.4 us (3%)
  starting transfers between devices  6.76 us (1%)
    psum x1, waiting for transfers between devices, on_device(): lax.psum(weight_part, ('row', 'col')) * (local_rows * devices_all) ** (-0.5)  148 us
    reduce_scatter x1, waiting for transfers between devices, on_device(): lax.psum_scatter(partial_value, 'col', scatter_dimension=0, tiled=True)  118 us
    all_gather x1, waiting for transfers between devices, on_device(): slab = lax.all_gather(features, 'row', axis=0, tiled=True)  96.2 us
    scatter-add x4, other arithmetic, one_group(): return running.at[rows_here].add(products)  37.3 us
    all_to_all x1, blocking collectives, on_device(): lax.all_to_all(grad_out.reshape(devices_all, piece_rows, feat_width), ('r...  25.6 us
    gather x4, local copies, waits for them, and re-layouts, group_products(): picked = col_blocks[cols_here]  21.7 us
    dot_general x4, matrix products, group_products(): jnp.einsum('kil,klf->kif', blocks_here, picked, preferred_element_type=jn...  10.5 us
  transfers between devices with their start and end apart: 4, of which 3 were waited for; matrix products, arithmetic and copies ran while one was open for 1% of the time, Pallas kernels for 0%

commit v1 on v0

v1 whole, which is shorter than its diff:
```python
import functools

import jax
import jax.numpy as jnp
from jax import lax
from jax.experimental import pallas as pl
from jax.experimental.pallas import tpu as pltpu
from jax.sharding import Mesh, PartitionSpec as P

BS = 128
LANES = 128
OWNER_BLOCKS = 16
TURNS = 8
PEERS = 8
Z_ORDER = (2, 1, 3, 0)


def ring(size, step):
    return [(i, (i + step) % size) for i in range(size)]


def load_slab(pieces, slab, sems):
    copies = []
    start = 0
    for n, piece in enumerate(pieces):
        rows = piece.shape[0]
        copy = pltpu.make_async_copy(piece, slab.at[pl.ds(start, rows)], sems.at[n])
        copy.start()
        copies.append(copy)
        start += rows
    for copy in copies:
        copy.wait()


def product(adj_ref, slab, cols, slot, turn):
    start = pl.multiple_of(cols[slot] * BS, BS)
    return jnp.dot(
        adj_ref[turn, 0, 0], slab[pl.ds(start, BS), :], preferred_element_type=jnp.float32
    )


def other_core_kernel(n_pieces, cols, count, owners, core, adj_ref, *refs):
    pieces, (out_ref, slab, sems) = refs[:n_pieces], refs[n_pieces:]
    step = pl.program_id(0)

    @pl.when(step == 0)
    def _():
        load_slab(pieces, slab, sems)

    for turn in range(TURNS):
        slot = turn * 16 + owners[step] * 2 + 1 - core[0]

        @pl.when(slot < count[0])
        def _():
            out_ref[0, turn] = product(adj_ref, slab, cols, slot, turn).astype(out_ref.dtype)


def own_core_kernel(
    n_pieces, cols, rows, count, other_rows, other_count, owners, core, adj_ref, other_ref, *refs
):
    pieces, outs, (slab, sums, sems) = refs[:n_pieces], refs[n_pieces:-3], refs[-3:]
    step = pl.program_id(0)

    @pl.when(step == 0)
    def _():
        load_slab(pieces, slab, sems)

    sums[...] = jnp.zeros_like(sums)
    for turn in range(TURNS):
        slot = turn * 16 + owners[step] * 2 + core[0]

        @pl.when(slot < count[0])
        def _():
            sums[rows[slot]] = product(adj_ref, slab, cols, slot, turn).astype(sums.dtype)

    for turn in range(TURNS):
        slot = turn * 16 + owners[step] * 2 + core[0]

        @pl.when(slot < other_count[0])
        def _():
            row = other_rows[slot]
            total = sums[row].astype(jnp.float32) + other_ref[0, turn].astype(jnp.float32)
            sums[row] = total.astype(sums.dtype)

    half = OWNER_BLOCKS // 2
    for place in range(len(Z_ORDER)):

        @pl.when(step // 2 == place)
        def _():
            outs[2 * place][0] = sums[:half]
            outs[2 * place + 1][0] = sums[half:]


def slab_products(pieces, tables, adj):
    cols, rows, count, other_rows, other_count, owners, core = tables
    slab_rows = sum(piece.shape[0] for piece in pieces)
    n_pieces = len(pieces)
    any_spec = pl.BlockSpec(memory_space=pl.ANY)
    slab_scratch = pltpu.VMEM((slab_rows, LANES), jnp.bfloat16)
    sems = pltpu.SemaphoreType.DMA((n_pieces,))
    params = pltpu.CompilerParams(
        dimension_semantics=("arbitrary",), vmem_limit_bytes=32 * 1024 * 1024
    )
    cost = pl.CostEstimate(
        flops=2 * 64 * BS * BS * LANES, bytes_accessed=10 * 1024 * 1024, transcendentals=0
    )
    adj_block = (TURNS, 1, 1, BS, BS)
    other = pl.pallas_call(
        functools.partial(other_core_kernel, n_pieces),
        out_shape=jax.ShapeDtypeStruct((PEERS, TURNS, BS, LANES), jnp.bfloat16),
        grid_spec=pltpu.PrefetchScalarGridSpec(
            num_scalar_prefetch=4,
            grid=(PEERS,),
            in_specs=[
                pl.BlockSpec(adj_block, lambda g, cl, ct, ow, co: (0, ow[g], 1 - co[0], 0, 0)),
                *[any_spec] * n_pieces,
            ],
            out_specs=pl.BlockSpec((1, TURNS, BS, LANES), lambda g, *_: (g, 0, 0, 0)),
            scratch_shapes=[slab_scratch, sems],
        ),
        compiler_params=params,
        cost_estimate=cost,
        name="other_core",
    )(cols, count, owners, core, adj, *pieces)
    came = lax.ppermute(other, "core", ring(2, 1))
    half = OWNER_BLOCKS // 2
    out_shape, out_specs = [], []
    for place in range(len(Z_ORDER)):
        for _ in range(2):
            out_shape.append(jax.ShapeDtypeStruct((2, half, BS, LANES), jnp.bfloat16))
            out_specs.append(
                pl.BlockSpec(
                    (1, half, BS, LANES),
                    lambda g, *_, first=2 * place: (jnp.clip(g - first, 0, 1), 0, 0, 0),
                )
            )
    return pl.pallas_call(
        functools.partial(own_core_kernel, n_pieces),
        out_shape=out_shape,
        grid_spec=pltpu.PrefetchScalarGridSpec(
            num_scalar_prefetch=7,
            grid=(PEERS,),
            in_specs=[
                pl.BlockSpec(
                    adj_block, lambda g, cl, rw, ct, orw, oct, ow, co: (0, ow[g], co[0], 0, 0)
                ),
                pl.BlockSpec((1, TURNS, BS, LANES), lambda g, *_: (g, 0, 0, 0)),
                *[any_spec] * n_pieces,
            ],
            out_specs=out_specs,
            scratch_shapes=[
                slab_scratch,
                pltpu.VMEM((OWNER_BLOCKS, BS, LANES), jnp.bfloat16),
                sems,
            ],
        ),
        compiler_params=params,
        cost_estimate=cost,
        name="own_core",
    )(cols, rows, count, other_rows, other_count, owners, core, adj, came, *pieces)


def gather_first(own):
    up = lax.ppermute(own, "y", ring(4, 1))
    down = lax.ppermute(own, "y", ring(4, -1))
    side = lax.ppermute(own, "xl", ring(2, 1))
    return up, down, side


def gather_second(up, down, side):
    half = up.shape[0] // 2
    far_low = lax.ppermute(up[:half], "y", ring(4, 1))
    far_high = lax.ppermute(down[half:], "y", ring(4, -1))
    side_up = lax.ppermute(side, "y", ring(4, 1))
    side_down = lax.ppermute(side, "y", ring(4, -1))
    return far_low, far_high, side_up, side_down


def gather_third(side_up, side_down):
    half = side_up.shape[0] // 2
    return (
        lax.ppermute(side_up[:half], "y", ring(4, 1)),
        lax.ppermute(side_down[half:], "y", ring(4, -1)),
    )


def add(*terms):
    total = terms[0].astype(jnp.float32)
    for term in terms[1:]:
        total = total + term.astype(jnp.float32)
    return total.astype(jnp.bfloat16)


def reduce_to_owner(parts):
    far_low, far_high, next_low, next_high, prev_low, prev_high, own_low, own_high = parts
    up, down = ring(4, 1), ring(4, -1)
    via_low = lax.ppermute(far_low, "z", up)
    via_high = lax.ppermute(far_high, "z", down)
    got_high_1 = lax.ppermute(next_high, "z", up)
    got_low_1 = lax.ppermute(prev_low, "z", down)
    got_low_2 = lax.ppermute(add(next_low, via_low), "z", up)
    got_high_2 = lax.ppermute(add(prev_high, via_high), "z", down)
    side_low = lax.ppermute(add(own_low[1], got_low_1[1], got_low_2[1]), "xh", ring(2, 1))
    side_high = lax.ppermute(add(own_high[1], got_high_1[1], got_high_2[1]), "xh", ring(2, 1))
    low = add(own_low[0], got_low_1[0], got_low_2[0], side_low)
    high = add(own_high[0], got_high_1[0], got_high_2[0], side_high)
    return jnp.concatenate([low, high]).reshape(-1, LANES)


def derivative(preact, grad_rows):
    sigmoid_pre = jax.nn.sigmoid(preact)
    return (
        grad_rows.astype(jnp.float32) * sigmoid_pre * (1.0 + preact * (1.0 - sigmoid_pre))
    ).astype(jnp.bfloat16)


AXES = ("xl", "y", "xh", "z", "core")


def swap_all(rows, devices_all):
    return lax.all_to_all(
        rows.reshape(devices_all, -1, rows.shape[-1]), AXES, split_axis=0, concat_axis=0, tiled=True
    )


def on_device(features, weight, adj_rows, adj_cols, adj_blocks, counts, grad_out):
    local_rows, feat_width = features.shape
    devices_all = 128
    xl, y, xh, z, core = (lax.axis_index(name) for name in AXES)

    count = counts.reshape(1)
    slots = jnp.arange(adj_rows.shape[-1], dtype=jnp.int32)
    rows = adj_rows.reshape(-1) - (slots % 16) * OWNER_BLOCKS
    other_rows = lax.ppermute(rows, "core", ring(2, 1))
    other_count = lax.ppermute(count, "core", ring(2, 1))
    cols = adj_cols.reshape(-1)
    source = cols // OWNER_BLOCKS
    away = ((source // 4) ^ xl) * 4 + (source % 4 - y) % 4
    cols = away * OWNER_BLOCKS + cols % OWNER_BLOCKS
    owners = jnp.stack([(xh ^ dx) * 4 + (z + dz) % 4 for dz in Z_ORDER for dx in range(2)])
    tables = (cols, rows, count, other_rows, other_count, owners.astype(jnp.int32), core.reshape(1))
    adj = adj_blocks.reshape(TURNS, PEERS, 2, BS, BS)

    aggs = []
    after = None
    for part in range(feat_width // LANES):
        own = features[:, part * LANES : (part + 1) * LANES]
        if after is not None:
            own, _ = lax.optimization_barrier((own, after))
        up, down, side = gather_first(own)
        far_low, far_high, side_up, side_down = gather_second(up, down, side)
        after = (far_low, side_up)
        side_far_low, side_far_high = gather_third(side_up, side_down)
        pieces = (
            own, down, far_low, far_high, up,
            side, side_down, side_far_low, side_far_high, side_up,
        )
        aggs.append(reduce_to_owner(slab_products(pieces, tables, adj)))
    agg = jnp.concatenate(aggs, axis=1)

    grad_row = swap_all(grad_out, devices_all).reshape(local_rows, feat_width)
    preact = jnp.dot(agg, weight, preferred_element_type=jnp.float32)
    out_row = jax.nn.silu(preact).astype(jnp.bfloat16)
    out_col = swap_all(out_row, devices_all).reshape(local_rows, feat_width)
    grad_pre = derivative(preact, grad_row)
    contract = (((0,), (0,)), ((), ()))
    weight_part = lax.dot_general(agg, grad_pre, contract, preferred_element_type=jnp.float32)
    terms = swap_all(weight_part, devices_all)
    summed = jnp.sum(terms, axis=0) * (local_rows * devices_all) ** (-0.5)
    spread = jnp.broadcast_to(summed[None], (devices_all, *summed.shape))
    weight_grad = lax.all_to_all(spread, AXES, split_axis=0, concat_axis=0, tiled=True)
    return (out_col, weight_grad.reshape(feat_width, feat_width))


def solution(mesh):
    fine = Mesh(mesh.devices.reshape(2, 4, 2, 4, 2), AXES)
    row, col = ("xl", "y"), ("xh", "z", "core")
    placed = (
        P((*col, *row), None),
        P(),
        P(row, col, None),
        P(row, col, None),
        P(row, col, None, None, None),
        P(row, col),
        P((*col, *row), None),
    )
    return jax.shard_map(
        on_device,
        mesh=fine,
        in_specs=placed,
        out_specs=(P((*col, *row), None), P()),
        check_vma=False,
    )
```

time: 498 us -> 290 us (0.58)
  waiting for transfers between devices: 363 us -> 110 us
  starting transfers between devices: 6.76 us -> 71 us
  Pallas kernels: 0 us -> 46.7 us
  other arithmetic: 41.9 us -> 8.62 us
  local copies, waits for them, and re-layouts: 29.9 us -> 12.1 us
  between operations: 14.4 us -> 1.67 us
  blocking collectives: 25.6 us -> 36.9 us
  matrix products: 15 us -> 3.86 us
    psum x1 -> x0, waiting for transfers between devices: 148 us -> none  [on_device(): lax.psum(weight_part, ('row', 'col')) * (local_rows * devices_all) ** (-0.5)]
    reduce_scatter x1 -> x0, waiting for transfers between devices: 118 us -> none  [on_device(): lax.psum_scatter(partial_value, 'col', scatter_dimension=0, tiled=True)]
    all_gather x1 -> x0, waiting for transfers between devices: 96.2 us -> none  [on_device(): slab = lax.all_gather(features, 'row', axis=0, tiled=True)]
    ppermute x0 -> x38, waiting for transfers between devices: none -> 92 us  [the longest x2 14.9 us: gather_second(): side_up = lax.ppermute(side, 'y', ring(4, 1))]
    ppermute x0 -> x38, starting transfers between devices: none -> 52.5 us  [the longest x2 5.99 us: reduce_to_owner(): via_high = lax.ppermute(far_high, 'z', down)]
    pallas_call x0 -> x4, Pallas kernels: none -> 46.7 us  [the longest x2 26.5 us: slab_products(): pl.pallas_call(functools.partial(own_core_kernel, n_pieces), out_shape=ou...]
    scatter-add x4 -> x0, other arithmetic: 37.3 us -> none  [one_group(): return running.at[rows_here].add(products)]
    gather x4 -> x0, local copies, waits for them, and re-layouts: 21.7 us -> none  [group_products(): picked = col_blocks[cols_here]]
  transfers between devices with their start and end apart: 4 -> 40, of which waited for: 3 -> 16; matrix products, arithmetic and copies ran while one was open for 1% -> 4% of each run, Pallas kernels for 0% -> 16%
where the time goes in v1:
time: 290 us; the launch traced here: 291 us
  waiting for transfers between devices  110 us (38%)
  starting transfers between devices  71 us (24%)
  Pallas kernels  46.7 us (16%)
  blocking collectives  36.9 us (13%)
  local copies, waits for them, and re-layouts  12.1 us (4%)
  other arithmetic  8.62 us (3%)
  matrix products  3.86 us (1%)
    pallas_call x2, Pallas kernels, slab_products(): pl.pallas_call(functools.partial(own_core_kernel, n_pieces), out_shape=ou...  26.5 us
    all_to_all x1, blocking collectives, swap_all(): lax.all_to_all(rows.reshape(devices_all, -1, rows.shape[-1]), AXES, split...  21.6 us
    pallas_call x2, Pallas kernels, slab_products(): pl.pallas_call(functools.partial(other_core_kernel, n_pieces), out_shape=...  20.2 us
    all_to_all x2, starting transfers between devices, swap_all(): lax.all_to_all(rows.reshape(devices_all, -1, rows.shape[-1]), AXES, split...  18.4 us
    all_to_all x2, waiting for transfers between devices, swap_all(): lax.all_to_all(rows.reshape(devices_all, -1, rows.shape[-1]), AXES, split...  18.4 us
    all_to_all x1, blocking collectives, on_device(): lax.all_to_all(spread, AXES, split_axis=0, concat_axis=0, tiled=True)  15.4 us
    ppermute x2, waiting for transfers between devices, gather_second(): side_up = lax.ppermute(side, 'y', ring(4, 1))  14.9 us
    ppermute x2, waiting for transfers between devices, reduce_to_owner(): via_high = lax.ppermute(far_high, 'z', down)  13 us
  transfers between devices with their start and end apart: 40, of which 16 were waited for; matrix products, arithmetic and copies ran while one was open for 4% of the time, Pallas kernels for 16%

profile of v1, /device:TPU:1, one launch (start us, length us, event | category | flops | bytes accessed | tf_op | source)
XLA Modules:
  0.0 291.3 jit_solution(5161467914728190842)
XLA Ops:
  6.8 8.4 %collective-permute-done.6.refs_5_ = bf16[2048,128]{1,0:T(8,128)(2,1)S(1)} collective-permute-done((bf16[2048,128]{1,0:T(8,128)(2,1)S(1)}, bf16[2048,128]{1,0:T(8,128)(2,1)S(1)}, u32[]{:S(2)}, u32[]{:S(2)}) %collective-permute-start.6) | collective-permute-done | bytes 524320 | tf_op jit(solution)/shard_map/ppermute | solution.py:166
  22.5 6.6 %collective-permute-done.8.refs_9_ = bf16[2048,128]{1,0:T(8,128)(2,1)S(1)} collective-permute-done((bf16[2048,128]{1,0:T(8,128)(2,1)S(1)}, bf16[2048,128]{1,0:T(8,128)(2,1)S(1)}, u32[]{:S(2)}, u32[]{:S(2)}) %collective-permute-start.8) | collective-permute-done | bytes 524320 | tf_op jit(solution)/shard_map/ppermute | solution.py:174
  36.5 3.8 %collective-permute-done.9.refs_7_ = bf16[1024,128]{1,0:T(8,128)(2,1)} collective-permute-done((bf16[1024,128]{1,0:T(8,128)(2,1)}, bf16[1024,128]{1,0:T(8,128)(2,1)}, u32[]{:S(2)}, u32[]{:S(2)}) %collective-permute-start.9) | collective-permute-done | bytes 262176 | tf_op jit(solution)/shard_map/ppermute | solution.py:182
  43.5 10.1 %other_core.2 = bf16[8,8,128,128]{3,2,1,0:T(8,128)(2,1)S(1)} custom-call(s32[128]{0:T(128)S(1)} %fusion.13.cols, s32[1]{0:T(128)} %bitcast.60.count, s32[8]{0:T(128)S(1)} %stack.35.owners, s32[1]{0:T(128)} %bitcast.11.core, bf16[8,8,2,128,128]{4,3,2,1,0:T(8,128)(2,1)S(1)} %bitcast.64, bf16[2048,128]{1,0:T(8,128)(2,1)S(1)} %get-tuple-element.38.refs_0_, ...), custom_call_target="tpu_custom_call" | custom-call | flops 268435456 | bytes 10485760 | tf_op jit(solution)/shard_map/other_core/pallas_call | solution.py:108
  61.2 9.3 %collective-permute-done.21.refs_4_ = bf16[2048,128]{1,0:T(8,128)(2,1)S(1)} collective-permute-done((bf16[2048,128]{1,0:T(8,128)(2,1)S(1)}, bf16[2048,128]{1,0:T(8,128)(2,1)S(1)}, u32[]{:S(2)}, u32[]{:S(2)}) %collective-permute-start.21) | collective-permute-done | bytes 524320 | tf_op jit(solution)/shard_map/ppermute | solution.py:164
  73.4 8.4 %collective-permute-done.26.refs_9_ = bf16[2048,128]{1,0:T(8,128)(2,1)S(1)} collective-permute-done((bf16[2048,128]{1,0:T(8,128)(2,1)}, bf16[2048,128]{1,0:T(8,128)(2,1)S(1)}, u32[]{:S(2)}, u32[]{:S(2)}) %collective-permute-start.26) | collective-permute-done | bytes 524320 | tf_op jit(solution)/shard_map/ppermute | solution.py:174
  87.4 5.6 %collective-permute-done.27.refs_7_ = bf16[1024,128]{1,0:T(8,128)(2,1)S(1)} collective-permute-done((bf16[1024,128]{1,0:T(8,128)(2,1)S(1)}, bf16[1024,128]{1,0:T(8,128)(2,1)S(1)}, u32[]{:S(2)}, u32[]{:S(2)}) %collective-permute-start.27) | collective-permute-done | bytes 262176 | tf_op jit(solution)/shard_map/ppermute | solution.py:182
  93.0 10.1 %other_core.3 = bf16[8,8,128,128]{3,2,1,0:T(8,128)(2,1)S(1)} custom-call(s32[128]{0:T(128)S(1)} %fusion.13.cols, s32[1]{0:T(128)} %bitcast.62.count, s32[8]{0:T(128)S(1)} %stack.35.owners, s32[1]{0:T(128)} %bitcast.11.core, bf16[8,8,2,128,128]{4,3,2,1,0:T(8,128)(2,1)S(1)} %bitcast.65, bf16[2048,128]{1,0:T(8,128)(2,1)S(1)} %get-tuple-element.27.refs_0_, ...), custom_call_target="tpu_custom_call" | custom-call | flops 268435456 | bytes 10485760 | tf_op jit(solution)/shard_map/other_core/pallas_call | solution.py:108
  104.2 3.4 %collective-permute-done.1.other_count = s32[1]{0:T(128)} collective-permute-done((s32[1]{0:T(128)}, s32[1]{0:T(128)}, u32[]{:S(2)}, u32[]{:S(2)}) %collective-permute-start.1) | collective-permute-done | bytes 36 | tf_op jit(solution)/shard_map/ppermute | solution.py:235
  107.6 13.4 %own_core.2 = (bf16[2,8,128,128]{3,2,1,0:T(8,128)(2,1)S(1)}, bf16[2,8,128,128]{3,2,1,0:T(8,128)(2,1)S(1)}, bf16[2,8,128,128]{3,2,1,0:T(8,128)(2,1)S(1)}, bf16[2,...) custom-call(s32[128]{0:T(128)S(1)} %fusion.13.cols, ...), custom_call_target="tpu_custom_call" | custom-call | flops 268435456 | bytes 10485760 | tf_op jit(solution)/shard_map/own_core/pallas_call | solution.py:137
  125.3 10.4 %collective-permute-done.13 = bf16[2,8,128,128]{3,2,1,0:T(8,128)(2,1)S(1)} collective-permute-done((bf16[2,8,128,128]{3,2,1,0:T(8,128)(2,1)S(1)}, bf16[2,8,128,128]{3,2,1,0:T(8,128)(2,1)S(1)}, u32[]{:S(2)}, u32[]{:S(2)}) %collective-permute-start.13) | collective-permute-done | bytes 524320 | tf_op jit(solution)/shard_map/ppermute | solution.py:197
  140.3 13.1 %own_core.3 = (bf16[2,8,128,128]{3,2,1,0:T(8,128)(2,1)}, bf16[2,8,128,128]{3,2,1,0:T(8,128)(2,1)S(1)}, bf16[2,8,128,128]{3,2,1,0:T(8,128)(2,1)S(1)}, bf16[2,8,12...) custom-call(s32[128]{0:T(128)S(1)} %fusion.13.cols, ...), custom_call_target="tpu_custom_call" | custom-call | flops 268435456 | bytes 10485760 | tf_op jit(solution)/shard_map/own_core/pallas_call | solution.py:137
  155.9 14.1 %all-to-all-start.1 = ((bf16[128,16,256]{2,1,0:T(8,128)(2,1)}), bf16[128,16,256]{2,1,0:T(8,128)(2,1)}, u32[]{:S(2)}, u32[]{:S(2)}) async-start(bf16[128,16,256]{2,1,0:T(8,128)(2,1)} %bitcast.69), calls=%async_computation.1 | async-start | bytes 2097152 | tf_op jit(solution)/shard_map/all_to_all | solution.py:221
  170.0 3.3 %collective-permute-start.35 = (bf16[2,8,128,128]{3,2,1,0:T(8,128)(2,1)}, bf16[2,8,128,128]{3,2,1,0:T(8,128)(2,1)S(1)}, u32[]{:S(2)}, u32[]{:S(2)}) collective-permute-start(bf16[2,8,128,128]{3,2,1,0:T(8,128)(2,1)} %copy-done.13), channel_id=1, source_target_pairs={{0,6},{2,0},{4,2},{6,4},{1,7},{3,1},{5,3},{7,5},{8,14},{10,8},{12,... | collective-permute-start | bytes 1572872 | tf_op jit(solution)/shard_map/ppermute | solution.py:198
  181.4 13.0 %collective-permute-done.35 = bf16[2,8,128,128]{3,2,1,0:T(8,128)(2,1)S(1)} collective-permute-done((bf16[2,8,128,128]{3,2,1,0:T(8,128)(2,1)}, bf16[2,8,128,128]{3,2,1,0:T(8,128)(2,1)S(1)}, u32[]{:S(2)}, u32[]{:S(2)}) %collective-permute-start.35) | collective-permute-done | bytes 524320 | tf_op jit(solution)/shard_map/ppermute | solution.py:198
  200.3 5.2 %collective-permute-done.30 = bf16[2,8,128,128]{3,2,1,0:T(8,128)(2,1)S(1)} collective-permute-done((bf16[2,8,128,128]{3,2,1,0:T(8,128)(2,1)S(1)}, bf16[2,8,128,128]{3,2,1,0:T(8,128)(2,1)S(1)}, u32[]{:S(2)}, u32[]{:S(2)}) %collective-permute-start.30) | collective-permute-done | bytes 524320 | tf_op jit(solution)/shard_map/ppermute | solution.py:200
  205.5 3.2 %collective-permute-done.32 = bf16[2,8,128,128]{3,2,1,0:T(8,128)(2,1)S(1)} collective-permute-done((bf16[2,8,128,128]{3,2,1,0:T(8,128)(2,1)S(1)}, bf16[2,8,128,128]{3,2,1,0:T(8,128)(2,1)S(1)}, u32[]{:S(2)}, u32[]{:S(2)}) %collective-permute-start.32) | collective-permute-done | bytes 524320 | tf_op jit(solution)/shard_map/ppermute | solution.py:201
  211.5 5.3 %collective-permute-done.36 = bf16[2,8,128,128]{3,2,1,0:T(8,128)(2,1)S(1)} collective-permute-done((bf16[2,8,128,128]{3,2,1,0:T(8,128)(2,1)S(1)}, bf16[2,8,128,128]{3,2,1,0:T(8,128)(2,1)S(1)}, u32[]{:S(2)}, u32[]{:S(2)}) %collective-permute-start.36) | collective-permute-done | bytes 524320 | tf_op jit(solution)/shard_map/ppermute | solution.py:202
  220.2 5.1 %collective-permute-done.37 = bf16[8,128,128]{2,1,0:T(8,128)(2,1)S(1)} collective-permute-done((bf16[8,128,128]{2,1,0:T(8,128)(2,1)S(1)}, bf16[8,128,128]{2,1,0:T(8,128)(2,1)S(1)}, u32[]{:S(2)}, u32[]{:S(2)}) %collective-permute-start.37) | collective-permute-done | bytes 262176 | tf_op jit(solution)/shard_map/ppermute | solution.py:204
  225.5 3.4 %fusion.1 = (bf16[2048,256]{1,0:T(8,128)(2,1)S(1)}, bf16[2048,256]{1,0:T(8,128)(2,1)}) fusion(bf16[128,16,256]{2,1,0:T(8,128)(2,1)} %all-to-all-done.1, bf16[256,256]{1,0:T(8,128)(2,1)S(1)} %copy-done, bf16[2048,128]{1,0:T(8,128)(2,1)S(1)} %bitcast.72, bf16[2048,128]{1,0:T(8,128)(2,1)S(1)} %bitcast.70), kind=kOutput, calls=%fused_computation.2 | convolution fusion | flops 276824064 | bytes 4325376 | tf_op jit(solution)/shard_map/dot_general | solution.py:262
  229.6 21.6 %all_to_all.20 = f32[128,2,256]{2,1,0:T(2,128)S(1)} all-to-all(f32[128,2,256]{2,1,0:T(2,128)S(1)} %reshape.100), channel_id=1, replica_groups=mesh['xl'=2,'y'=4,'xh'=2,'z'=4,'core'=2] {'xl','y','xh','z','core'}, dimensions={0} | all-to-all | bytes 524288 | tf_op jit(solution)/shard_map/all_to_all | solution.py:221
  251.3 15.4 %all_to_all.21 = f32[128,2,256]{2,1,0:T(2,128)S(1)} all-to-all(f32[128,2,256]{2,1,0:T(2,128)S(1)} %broadcast_in_dim.2), channel_id=1, replica_groups=mesh['xl'=2,'y'=4,'xh'=2,'z'=4,'core'=2] {'xl','y','xh','z','core'}, dimensions={0} | all-to-all | bytes 524288 | tf_op jit(solution)/shard_map/all_to_all | solution.py:271
  266.7 4.3 %all-to-all-start = ((bf16[128,16,256]{2,1,0:T(8,128)(2,1)}), bf16[128,16,256]{2,1,0:T(8,128)(2,1)S(1)}, u32[]{:S(2)}, u32[]{:S(2)}) async-start(bf16[128,16,256]{2,1,0:T(8,128)(2,1)} %bitcast.23), calls=%async_computation | async-start | bytes 2097152 | tf_op jit(solution)/shard_map/all_to_all | solution.py:221
  272.0 18.4 %all-to-all-done = bf16[128,16,256]{2,1,0:T(8,128)(2,1)S(1)} async-done(((bf16[128,16,256]{2,1,0:T(8,128)(2,1)}), bf16[128,16,256]{2,1,0:T(8,128)(2,1)S(1)}, u32[]{:S(2)}, u32[]{:S(2)}) %all-to-all-start) | async-done | bytes 1048608 | tf_op jit(solution)/shard_map/all_to_all | solution.py:221
  (128 shorter events, 74.7 us)
Async XLA Ops:
  19.1 15.6 %collective-permute-start.4 = (bf16[1024,128]{1,0:T(8,128)(2,1)}, bf16[1024,128]{1,0:T(8,128)(2,1)S(1)}, u32[]{:S(2)}, u32[]{:S(2)}) collective-permute-start(bf16[1024,128]{1,0:T(8,128)(2,1)} %slice.136), channel_id=1, source_target_pairs={{0,16},{16,32},{32,48},{48,0},{1,17},{17,33},{33,49},{49,1},{2,18}... | collective-permute-start | bytes 786440 | tf_op jit(solution)/shard_map/ppermute | solution.py:172
  19.9 16.6 %collective-permute-start.5 = (bf16[1024,128]{1,0:T(8,128)(2,1)}, bf16[1024,128]{1,0:T(8,128)(2,1)}, u32[]{:S(2)}, u32[]{:S(2)}) collective-permute-start(bf16[1024,128]{1,0:T(8,128)(2,1)} %slice.137), channel_id=1, source_target_pairs={{0,48},{16,0},{32,16},{48,32},{1,49},{17,1},{33,17},{49,33},{2,50}... | collective-permute-start | bytes 786440 | tf_op jit(solution)/shard_map/ppermute | solution.py:173
  34.7 23.8 %collective-permute-start.24 = (bf16[2048,128]{1,0:T(8,128)(2,1)S(1)}, bf16[2048,128]{1,0:T(8,128)(2,1)}, u32[]{:S(2)}, u32[]{:S(2)}) collective-permute-start(bf16[2048,128]{1,0:T(8,128)(2,1)S(1)} %get-tuple-element.27.refs_0_), channel_id=1, source_target_pairs={{0,64},{64,0},{1,65},{65,1},{2,66},{66,2},{3,67},{67,3},{4,68},{68... | collective-permute-start | bytes 1572872 | tf_op jit(solution)/shard_map/ppermute | solution.py:166
  53.6 54.0 %collective-permute-start.11 = (bf16[8,8,128,128]{3,2,1,0:T(8,128)(2,1)S(1)}, bf16[8,8,128,128]{3,2,1,0:T(8,128)(2,1)S(1)}, u32[]{:S(2)}, u32[]{:S(2)}) collective-permute-start(bf16[8,8,128,128]{3,2,1,0:T(8,128)(2,1)S(1)} %other_core.2), channel_id=1, source_target_pairs={{0,1},{1,0},{2,3},{3,2},{4,5},{5,4},{6,7},{7,6},{8,9},{9,8},{10,11... | collective-permute-start | bytes 6291464 | tf_op jit(solution)/shard_map/ppermute | solution.py:125
  55.8 14.8 %collective-permute-start.20 = (bf16[2048,128]{1,0:T(8,128)(2,1)S(1)}, bf16[2048,128]{1,0:T(8,128)(2,1)S(1)}, u32[]{:S(2)}, u32[]{:S(2)}) collective-permute-start(bf16[2048,128]{1,0:T(8,128)(2,1)S(1)} %get-tuple-element.27.refs_0_), channel_id=1, source_target_pairs={{0,48},{16,0},{32,16},{48,32},{1,49},{17,1},{33,17},{49,33},{2,50}... | collective-permute-start | bytes 1572872 | tf_op jit(solution)/shard_map/ppermute | solution.py:165
  58.5 23.2 %collective-permute-start.26 = (bf16[2048,128]{1,0:T(8,128)(2,1)}, bf16[2048,128]{1,0:T(8,128)(2,1)S(1)}, u32[]{:S(2)}, u32[]{:S(2)}) collective-permute-start(bf16[2048,128]{1,0:T(8,128)(2,1)} %collective-permute-done.24.refs_5_), channel_id=1, source_target_pairs={{0,16},{16,32},{32,48},{48,0},{1,17},{17,33},{33,49},{49,1},{2,18}... | collective-permute-start | bytes 1572872 | tf_op jit(solution)/shard_map/ppermute | solution.py:174
  58.5 23.3 %collective-permute-start.25 = (bf16[2048,128]{1,0:T(8,128)(2,1)}, bf16[2048,128]{1,0:T(8,128)(2,1)S(1)}, u32[]{:S(2)}, u32[]{:S(2)}) collective-permute-start(bf16[2048,128]{1,0:T(8,128)(2,1)} %collective-permute-done.24.refs_5_), channel_id=1, source_target_pairs={{0,48},{16,0},{32,16},{48,32},{1,49},{17,1},{33,17},{49,33},{2,50}... | collective-permute-start | bytes 1572872 | tf_op jit(solution)/shard_map/ppermute | solution.py:175
  70.5 16.8 %collective-permute-start.22 = (bf16[1024,128]{1,0:T(8,128)(2,1)S(1)}, bf16[1024,128]{1,0:T(8,128)(2,1)S(1)}, u32[]{:S(2)}, u32[]{:S(2)}) collective-permute-start(bf16[1024,128]{1,0:T(8,128)(2,1)S(1)} %slice.148), channel_id=1, source_target_pairs={{0,16},{16,32},{32,48},{48,0},{1,17},{17,33},{33,49},{49,1},{2,18}... | collective-permute-start | bytes 786440 | tf_op jit(solution)/shard_map/ppermute | solution.py:172
  70.6 16.7 %collective-permute-start.23 = (bf16[1024,128]{1,0:T(8,128)(2,1)S(1)}, bf16[1024,128]{1,0:T(8,128)(2,1)S(1)}, u32[]{:S(2)}, u32[]{:S(2)}) collective-permute-start(bf16[1024,128]{1,0:T(8,128)(2,1)S(1)} %slice.149), channel_id=1, source_target_pairs={{0,48},{16,0},{32,16},{48,32},{1,49},{17,1},{33,17},{49,33},{2,50}... | collective-permute-start | bytes 786440 | tf_op jit(solution)/shard_map/ppermute | solution.py:173
  103.1 37.2 %collective-permute-start.29 = (bf16[8,8,128,128]{3,2,1,0:T(8,128)(2,1)S(1)}, bf16[8,8,128,128]{3,2,1,0:T(8,128)(2,1)S(1)}, u32[]{:S(2)}, u32[]{:S(2)}) collective-permute-start(bf16[8,8,128,128]{3,2,1,0:T(8,128)(2,1)S(1)} %other_core.3), channel_id=1, source_target_pairs={{0,1},{1,0},{2,3},{3,2},{4,5},{5,4},{6,7},{7,6},{8,9},{9,8},{10,11... | collective-permute-start | bytes 6291464 | tf_op jit(solution)/shard_map/ppermute | solution.py:125
  121.2 15.5 %collective-permute-start.17 = (bf16[2,8,128,128]{3,2,1,0:T(8,128)(2,1)S(1)}, bf16[2,8,128,128]{3,2,1,0:T(8,128)(2,1)S(1)}, u32[]{:S(2)}, u32[]{:S(2)}) collective-permute-start(bf16[2,8,128,128]{3,2,1,0:T(8,128)(2,1)S(1)} %get-tuple-element.26), channel_id=1, source_target_pairs={{0,6},{2,0},{4,2},{6,4},{1,7},{3,1},{5,3},{7,5},{8,14},{10,8},{12,... | collective-permute-start | bytes 1572872 | tf_op jit(solution)/shard_map/ppermute | solution.py:198
  123.8 46.2 %collective-permute-start.12 = (bf16[2,8,128,128]{3,2,1,0:T(8,128)(2,1)}, bf16[2,8,128,128]{3,2,1,0:T(8,128)(2,1)}, u32[]{:S(2)}, u32[]{:S(2)}) collective-permute-start(bf16[2,8,128,128]{3,2,1,0:T(8,128)(2,1)} %get-tuple-element.20), channel_id=1, source_target_pairs={{0,6},{2,0},{4,2},{6,4},{1,7},{3,1},{5,3},{7,5},{8,14},{10,8},{12,... | collective-permute-start | bytes 1572872 | tf_op jit(solution)/shard_map/ppermute | solution.py:200
  123.9 53.4 %collective-permute-start.16 = (bf16[2,8,128,128]{3,2,1,0:T(8,128)(2,1)}, bf16[2,8,128,128]{3,2,1,0:T(8,128)(2,1)}, u32[]{:S(2)}, u32[]{:S(2)}) collective-permute-start(bf16[2,8,128,128]{3,2,1,0:T(8,128)(2,1)} %get-tuple-element.24), channel_id=1, source_target_pairs={{0,2},{2,4},{4,6},{6,0},{1,3},{3,5},{5,7},{7,1},{8,10},{10,12},{12... | collective-permute-start | bytes 1572872 | tf_op jit(solution)/shard_map/ppermute | solution.py:199
  136.7 36.7 %collective-permute-start.14 = (bf16[2,8,128,128]{3,2,1,0:T(8,128)(2,1)}, bf16[2,8,128,128]{3,2,1,0:T(8,128)(2,1)}, u32[]{:S(2)}, u32[]{:S(2)}) collective-permute-start(bf16[2,8,128,128]{3,2,1,0:T(8,128)(2,1)} %add_convert_fusion.3), channel_id=1, source_target_pairs={{0,2},{2,4},{4,6},{6,0},{1,3},{3,5},{5,7},{7,1},{8,10},{10,12},{12... | collective-permute-start | bytes 1572872 | tf_op jit(solution)/shard_map/ppermute | solution.py:201
  137.6 39.7 %collective-permute-start.18 = (bf16[2,8,128,128]{3,2,1,0:T(8,128)(2,1)}, bf16[2,8,128,128]{3,2,1,0:T(8,128)(2,1)}, u32[]{:S(2)}, u32[]{:S(2)}) collective-permute-start(bf16[2,8,128,128]{3,2,1,0:T(8,128)(2,1)} %add_convert_fusion.2), channel_id=1, source_target_pairs={{0,6},{2,0},{4,2},{6,4},{1,7},{3,1},{5,3},{7,5},{8,14},{10,8},{12,... | collective-permute-start | bytes 1572872 | tf_op jit(solution)/shard_map/ppermute | solution.py:202
  155.9 23.2 %collective-permute-start.31 = (bf16[2,8,128,128]{3,2,1,0:T(8,128)(2,1)}, bf16[2,8,128,128]{3,2,1,0:T(8,128)(2,1)}, u32[]{:S(2)}, u32[]{:S(2)}) collective-permute-start(bf16[2,8,128,128]{3,2,1,0:T(8,128)(2,1)} %get-tuple-element.31), channel_id=1, source_target_pairs={{0,2},{2,4},{4,6},{6,0},{1,3},{3,5},{5,7},{7,1},{8,10},{10,12},{12... | collective-permute-start | bytes 1572872 | tf_op jit(solution)/shard_map/ppermute | solution.py:197
  155.9 69.6 %all-to-all-start.1 = ((bf16[128,16,256]{2,1,0:T(8,128)(2,1)}), bf16[128,16,256]{2,1,0:T(8,128)(2,1)}, u32[]{:S(2)}, u32[]{:S(2)}) async-start(bf16[128,16,256]{2,1,0:T(8,128)(2,1)} %bitcast.69), calls=%async_computation.1 | async-start | bytes 2097152 | tf_op jit(solution)/shard_map/all_to_all | solution.py:221
  170.0 24.4 %collective-permute-start.35 = (bf16[2,8,128,128]{3,2,1,0:T(8,128)(2,1)}, bf16[2,8,128,128]{3,2,1,0:T(8,128)(2,1)S(1)}, u32[]{:S(2)}, u32[]{:S(2)}) collective-permute-start(bf16[2,8,128,128]{3,2,1,0:T(8,128)(2,1)} %copy-done.13), channel_id=1, source_target_pairs={{0,6},{2,0},{4,2},{6,4},{1,7},{3,1},{5,3},{7,5},{8,14},{10,8},{12,... | collective-permute-start | bytes 1572872 | tf_op jit(solution)/shard_map/ppermute | solution.py:198
  174.5 22.1 %collective-permute-start.15 = (bf16[8,128,128]{2,1,0:T(8,128)(2,1)S(1)}, bf16[8,128,128]{2,1,0:T(8,128)(2,1)S(1)}, u32[]{:S(2)}, u32[]{:S(2)}) collective-permute-start(bf16[8,128,128]{2,1,0:T(8,128)(2,1)S(1)} %fusion.8), channel_id=1, source_target_pairs={{0,8},{8,0},{1,9},{9,1},{2,10},{10,2},{3,11},{11,3},{4,12},{12,4},... | collective-permute-start | bytes 786440 | tf_op jit(solution)/shard_map/ppermute | solution.py:203
  178.4 20.7 %collective-permute-start.19 = (bf16[8,128,128]{2,1,0:T(8,128)(2,1)S(1)}, bf16[8,128,128]{2,1,0:T(8,128)(2,1)S(1)}, u32[]{:S(2)}, u32[]{:S(2)}) collective-permute-start(bf16[8,128,128]{2,1,0:T(8,128)(2,1)S(1)} %fusion.9), channel_id=1, source_target_pairs={{0,8},{8,0},{1,9},{9,1},{2,10},{10,2},{3,11},{11,3},{4,12},{12,4},... | collective-permute-start | bytes 786440 | tf_op jit(solution)/shard_map/ppermute | solution.py:204
  178.8 26.8 %collective-permute-start.30 = (bf16[2,8,128,128]{3,2,1,0:T(8,128)(2,1)S(1)}, bf16[2,8,128,128]{3,2,1,0:T(8,128)(2,1)S(1)}, u32[]{:S(2)}, u32[]{:S(2)}) collective-permute-start(bf16[2,8,128,128]{3,2,1,0:T(8,128)(2,1)S(1)} %copy-done.12), channel_id=1, source_target_pairs={{0,6},{2,0},{4,2},{6,4},{1,7},{3,1},{5,3},{7,5},{8,14},{10,8},{12,... | collective-permute-start | bytes 1572872 | tf_op jit(solution)/shard_map/ppermute | solution.py:200
  179.1 32.4 %collective-permute-start.34 = (bf16[2,8,128,128]{3,2,1,0:T(8,128)(2,1)S(1)}, bf16[2,8,128,128]{3,2,1,0:T(8,128)(2,1)S(1)}, u32[]{:S(2)}, u32[]{:S(2)}) collective-permute-start(bf16[2,8,128,128]{3,2,1,0:T(8,128)(2,1)S(1)} %copy-done.10), channel_id=1, source_target_pairs={{0,2},{2,4},{4,6},{6,0},{1,3},{3,5},{5,7},{7,1},{8,10},{10,12},{12... | collective-permute-start | bytes 1572872 | tf_op jit(solution)/shard_map/ppermute | solution.py:199
  196.6 20.2 %collective-permute-start.36 = (bf16[2,8,128,128]{3,2,1,0:T(8,128)(2,1)S(1)}, bf16[2,8,128,128]{3,2,1,0:T(8,128)(2,1)S(1)}, u32[]{:S(2)}, u32[]{:S(2)}) collective-permute-start(bf16[2,8,128,128]{3,2,1,0:T(8,128)(2,1)S(1)} %add_convert_fusion), channel_id=1, source_target_pairs={{0,6},{2,0},{4,2},{6,4},{1,7},{3,1},{5,3},{7,5},{8,14},{10,8},{12,... | collective-permute-start | bytes 1572872 | tf_op jit(solution)/shard_map/ppermute | solution.py:202
  266.7 23.6 %all-to-all-start = ((bf16[128,16,256]{2,1,0:T(8,128)(2,1)}), bf16[128,16,256]{2,1,0:T(8,128)(2,1)S(1)}, u32[]{:S(2)}, u32[]{:S(2)}) async-start(bf16[128,16,256]{2,1,0:T(8,128)(2,1)} %bitcast.23), calls=%async_computation | async-start | bytes 2097152 | tf_op jit(solution)/shard_map/all_to_all | solution.py:221
  (32 other events, 595.5 us)

commit v2 on v1

v2 whole, which is shorter than its diff:
```python
import functools

import jax
import jax.numpy as jnp
from jax import lax
from jax.experimental import pallas as pl
from jax.experimental.pallas import tpu as pltpu
from jax.sharding import Mesh, PartitionSpec as P

BS = 128
LANES = 128
OWNER_BLOCKS = 16
TURNS = 8
PEERS = 8
Z_ORDER = (2, 1, 3, 0)


def ring(size, step):
    return [(i, (i + step) % size) for i in range(size)]


def load_slab(pieces, slab, sems):
    copies = []
    start = 0
    for n, piece in enumerate(pieces):
        rows = piece.shape[0]
        copy = pltpu.make_async_copy(piece, slab.at[pl.ds(start, rows)], sems.at[n])
        copy.start()
        copies.append(copy)
        start += rows
    for copy in copies:
        copy.wait()


def chip_kernel(n_pieces, tables, owners, core, adj_ref, other_adj_ref, *refs):
    pieces, outs, (slab, sums, sems) = refs[:n_pieces], refs[n_pieces:-3], refs[-3:]
    step = pl.program_id(0)

    @pl.when(step == 0)
    def _():
        load_slab(pieces, slab, sems)

    sums[...] = jnp.zeros_like(sums)

    def product(cell, slot, block):
        start = pl.multiple_of(tables[cell, 0, slot] * BS, BS)
        found = jnp.dot(block, slab[pl.ds(start, BS), :], preferred_element_type=jnp.float32)
        return jnp.where(slot < tables[cell, 2, 0], found, 0.0).astype(jnp.bfloat16)

    slots = [turn * 16 + owners[step] * 2 + core[0] for turn in range(TURNS)]
    for turn, slot in enumerate(slots):
        sums[tables[0, 1, slot]] = product(0, slot, adj_ref[turn, 0, 0])
    for turn, slot in enumerate(slots):
        row = tables[1, 1, slot]
        term = product(1, slot, other_adj_ref[turn, 0]).astype(jnp.float32)
        sums[row] = (sums[row].astype(jnp.float32) + term).astype(jnp.bfloat16)

    half = OWNER_BLOCKS // 2
    for place in range(len(Z_ORDER)):

        @pl.when(step // 2 == place)
        def _():
            outs[2 * place][0] = sums[:half]
            outs[2 * place + 1][0] = sums[half:]


def chip_sums(pieces, tables, owners, core, adj, other_adj):
    slab_rows = sum(piece.shape[0] for piece in pieces)
    n_pieces = len(pieces)
    half = OWNER_BLOCKS // 2
    out_shape, out_specs = [], []
    for place in range(len(Z_ORDER)):
        for _ in range(2):
            out_shape.append(jax.ShapeDtypeStruct((2, half, BS, LANES), jnp.bfloat16))
            out_specs.append(
                pl.BlockSpec(
                    (1, half, BS, LANES),
                    lambda g, *_, first=2 * place: (jnp.clip(g - first, 0, 1), 0, 0, 0),
                )
            )
    return pl.pallas_call(
        functools.partial(chip_kernel, n_pieces),
        out_shape=out_shape,
        grid_spec=pltpu.PrefetchScalarGridSpec(
            num_scalar_prefetch=3,
            grid=(PEERS,),
            in_specs=[
                pl.BlockSpec((TURNS, 1, 1, BS, BS), lambda g, tb, ow, co: (0, ow[g], co[0], 0, 0)),
                pl.BlockSpec((TURNS, 1, BS, BS), lambda g, tb, ow, co: (0, ow[g], 0, 0)),
                *[pl.BlockSpec(memory_space=pl.ANY)] * n_pieces,
            ],
            out_specs=out_specs,
            scratch_shapes=[
                pltpu.VMEM((slab_rows, LANES), jnp.bfloat16),
                pltpu.VMEM((OWNER_BLOCKS, BS, LANES), jnp.bfloat16),
                pltpu.SemaphoreType.DMA((n_pieces,)),
            ],
        ),
        compiler_params=pltpu.CompilerParams(
            dimension_semantics=("arbitrary",), vmem_limit_bytes=32 * 1024 * 1024
        ),
        cost_estimate=pl.CostEstimate(
            flops=12_000_000_000, bytes_accessed=16 * 1024 * 1024, transcendentals=0
        ),
        name="chip_sums",
    )(tables, owners, core, adj, other_adj, *pieces)


def gather_first(own):
    up = lax.ppermute(own, "y", ring(4, 1))
    down = lax.ppermute(own, "y", ring(4, -1))
    side = lax.ppermute(own, "xl", ring(2, 1))
    return up, down, side


def gather_second(up, down, side):
    half = up.shape[0] // 2
    far_low = lax.ppermute(up[:half], "y", ring(4, 1))
    far_high = lax.ppermute(down[half:], "y", ring(4, -1))
    side_up = lax.ppermute(side, "y", ring(4, 1))
    side_down = lax.ppermute(side, "y", ring(4, -1))
    return far_low, far_high, side_up, side_down


def gather_third(side_up, side_down):
    half = side_up.shape[0] // 2
    return (
        lax.ppermute(side_up[:half], "y", ring(4, 1)),
        lax.ppermute(side_down[half:], "y", ring(4, -1)),
    )


def add(*terms):
    total = terms[0].astype(jnp.float32)
    for term in terms[1:]:
        total = total + term.astype(jnp.float32)
    return total.astype(jnp.bfloat16)


def reduce_to_owner(parts):
    far_low, far_high, next_low, next_high, prev_low, prev_high, own_low, own_high = parts
    up, down = ring(4, 1), ring(4, -1)
    via_low = lax.ppermute(far_low, "z", up)
    via_high = lax.ppermute(far_high, "z", down)
    got_high_1 = lax.ppermute(next_high, "z", up)
    got_low_1 = lax.ppermute(prev_low, "z", down)
    got_low_2 = lax.ppermute(add(next_low, via_low), "z", up)
    got_high_2 = lax.ppermute(add(prev_high, via_high), "z", down)
    side_low = lax.ppermute(add(own_low[1], got_low_1[1], got_low_2[1]), "xh", ring(2, 1))
    side_high = lax.ppermute(add(own_high[1], got_high_1[1], got_high_2[1]), "xh", ring(2, 1))
    low = add(own_low[0], got_low_1[0], got_low_2[0], side_low)
    high = add(own_high[0], got_high_1[0], got_high_2[0], side_high)
    return jnp.concatenate([low, high]).reshape(-1, LANES)


def derivative(preact, grad_rows):
    sigmoid_pre = jax.nn.sigmoid(preact)
    return (
        grad_rows.astype(jnp.float32) * sigmoid_pre * (1.0 + preact * (1.0 - sigmoid_pre))
    ).astype(jnp.bfloat16)


AXES = ("xl", "y", "xh", "z", "core")


def swap_all(rows, devices_all):
    return lax.all_to_all(
        rows.reshape(devices_all, -1, rows.shape[-1]), AXES, split_axis=0, concat_axis=0, tiled=True
    )


def on_device(features, weight, adj_rows, adj_cols, adj_blocks, counts, grad_out):
    local_rows, feat_width = features.shape
    devices_all = 128
    xl, y, xh, z, core = (lax.axis_index(name) for name in AXES)
    swap_core = functools.partial(lax.ppermute, axis_name="core", perm=ring(2, 1))

    slots = jnp.arange(adj_rows.shape[-1], dtype=jnp.int32)
    rows = adj_rows.reshape(-1) - (slots % 16) * OWNER_BLOCKS
    cols = adj_cols.reshape(-1)
    source = cols // OWNER_BLOCKS
    away = ((source // 4) ^ xl) * 4 + (source % 4 - y) % 4
    cols = away * OWNER_BLOCKS + cols % OWNER_BLOCKS
    mine = jnp.stack([cols, rows, jnp.broadcast_to(counts.reshape(1), rows.shape)])
    theirs = swap_core(mine).at[0].add(slots.shape[0])
    tables = jnp.stack([mine, theirs])
    owners = jnp.stack([(xh ^ dx) * 4 + (z + dz) % 4 for dz in Z_ORDER for dx in range(2)])
    owners = owners.astype(jnp.int32)
    adj = adj_blocks.reshape(TURNS, PEERS, 2, BS, BS)
    other_adj = swap_core(lax.dynamic_index_in_dim(adj, 1 - core, 2, keepdims=False))

    aggs = []
    after = None
    for part in range(feat_width // LANES):
        own = features[:, part * LANES : (part + 1) * LANES]
        if after is not None:
            own, _ = lax.optimization_barrier((own, after))
        up, down, side = gather_first(own)
        if part == 0:
            grad_out, _ = lax.optimization_barrier((grad_out, up))
            grad_row = swap_all(grad_out, devices_all).reshape(local_rows, feat_width)
        far_low, far_high, side_up, side_down = gather_second(up, down, side)
        after = (far_low, side_up)
        side_far_low, side_far_high = gather_third(side_up, side_down)
        pieces = (
            own, down, far_low, far_high, up,
            side, side_down, side_far_low, side_far_high, side_up,
        )
        pieces = (*pieces, *[swap_core(piece) for piece in pieces])
        if part == 0:
            tables, grad_row = lax.optimization_barrier((tables, grad_row))
        parts = chip_sums(pieces, tables, owners, core.reshape(1), adj, other_adj)
        aggs.append(reduce_to_owner(parts))
    agg = jnp.concatenate(aggs, axis=1)

    preact = jnp.dot(agg, weight, preferred_element_type=jnp.float32)
    out_row = jax.nn.silu(preact).astype(jnp.bfloat16)
    grad_pre = derivative(preact, grad_row)
    contract = (((0,), (0,)), ((), ()))
    weight_part = lax.dot_general(agg, grad_pre, contract, preferred_element_type=jnp.float32)
    coarse = lax.reduce_precision(weight_part, 8, 7)
    terms = [coarse.astype(jnp.bfloat16), (weight_part - coarse).astype(jnp.bfloat16)]
    sent = jnp.concatenate([x.reshape(devices_all, -1, feat_width) for x in (out_row, *terms)], 1)
    came = lax.all_to_all(sent, AXES, split_axis=0, concat_axis=0, tiled=True)
    piece = local_rows // devices_all
    out_col = came[:, :piece].reshape(local_rows, feat_width)
    came = came[:, piece:].astype(jnp.float32)
    each = came.shape[1] // 2
    summed = jnp.sum(came[:, :each] + came[:, each:], axis=0) * (local_rows * devices_all) ** (-0.5)
    spread = jnp.broadcast_to(summed[None], (devices_all, *summed.shape))
    weight_grad = lax.all_to_all(spread, AXES, split_axis=0, concat_axis=0, tiled=True)
    return (out_col, weight_grad.reshape(feat_width, feat_width))


def solution(mesh):
    fine = Mesh(mesh.devices.reshape(2, 4, 2, 4, 2), AXES)
    row, col = ("xl", "y"), ("xh", "z", "core")
    placed = (
        P((*col, *row), None),
        P(),
        P(row, col, None),
        P(row, col, None),
        P(row, col, None, None, None),
        P(row, col),
        P((*col, *row), None),
    )
    return jax.shard_map(
        on_device,
        mesh=fine,
        in_specs=placed,
        out_specs=(P((*col, *row), None), P()),
        check_vma=False,
    )
```

time: 290 us -> 268 us (0.924)
  Pallas kernels: 46.7 us -> 17.8 us
  starting transfers between devices: 71 us -> 88.8 us
  waiting for transfers between devices: 110 us -> 96.5 us
  local copies, waits for them, and re-layouts: 12.1 us -> 24 us
  other arithmetic: 8.62 us -> 2.59 us
  blocking collectives: 36.9 us -> 32.9 us
    pallas_call x4 -> x2, Pallas kernels: 46.7 us -> 17.8 us  [chip_sums(): pl.pallas_call(functools.partial(chip_kernel, n_pieces), out_shape=out_sh...]
    ppermute x4 -> x22, starting transfers between devices: 3.33 us -> 24.4 us  [the longest x20 22.6 us: on_device(): pieces = (*pieces, *[swap_core(piece) for piece in pieces])]
    ppermute x2, waiting for transfers between devices: 3.21 us -> 21.9 us  [reduce_to_owner(): got_low_2 = lax.ppermute(add(next_low, via_low), 'z', up)]
    all_to_all x2 -> x1, waiting for transfers between devices: 18.4 us -> 0.01 us  [swap_all(): lax.all_to_all(rows.reshape(devices_all, -1, rows.shape[-1]), AXES, split...]
    ppermute x2, waiting for transfers between devices: 14.9 us -> 0.01 us  [gather_second(): side_up = lax.ppermute(side, 'y', ring(4, 1))]
    all_to_all x0 -> x1, waiting for transfers between devices: none -> 10.2 us  [on_device(): lax.all_to_all(spread, AXES, split_axis=0, concat_axis=0, tiled=True)]
    ppermute x2, waiting for transfers between devices: 4.24 us -> 14.3 us  [gather_second(): far_low = lax.ppermute(up[:half], 'y', ring(4, 1))]
    ppermute x2, waiting for transfers between devices: 0.01 us -> 9.63 us  [gather_first(): down = lax.ppermute(own, 'y', ring(4, -1))]
  transfers between devices with their start and end apart: 40 -> 58, of which waited for: 16 -> 20; matrix products, arithmetic and copies ran while one was open for 4% -> 4% of each run, Pallas kernels for 16% -> 7%
where the time goes in v2:
time: 268 us; the launch traced here: 267 us
  waiting for transfers between devices  96.5 us (36%)
  starting transfers between devices  88.8 us (33%)
  blocking collectives  32.9 us (12%)
  local copies, waits for them, and re-layouts  24 us (9%)
  Pallas kernels  17.8 us (7%)
  matrix products  3.07 us (1%)
    all_to_all x1, blocking collectives, on_device(): came = lax.all_to_all(sent, AXES, split_axis=0, concat_axis=0, tiled=True)  32.9 us
    ppermute x20, starting transfers between devices, on_device(): pieces = (*pieces, *[swap_core(piece) for piece in pieces])  22.6 us
    ppermute x2, waiting for transfers between devices, reduce_to_owner(): got_low_2 = lax.ppermute(add(next_low, via_low), 'z', up)  21.9 us
    pallas_call x2, Pallas kernels, chip_sums(): pl.pallas_call(functools.partial(chip_kernel, n_pieces), out_shape=out_sh...  17.8 us
    ppermute x2, waiting for transfers between devices, gather_second(): far_low = lax.ppermute(up[:half], 'y', ring(4, 1))  14.3 us
    unnamed x36, local copies, waits for them, and re-layouts  12.2 us
    all_to_all x1, starting transfers between devices, swap_all(): lax.all_to_all(rows.reshape(devices_all, -1, rows.shape[-1]), AXES, split...  11.2 us
    ppermute x2, waiting for transfers between devices, reduce_to_owner(): via_low = lax.ppermute(far_low, 'z', up)  10.4 us
  transfers between devices with their start and end apart: 58, of which 20 were waited for; matrix products, arithmetic and copies ran while one was open for 4% of the time, Pallas kernels for 7%

profile of v2, /device:TPU:1, one launch (start us, length us, event | category | flops | bytes accessed | tf_op | source)
XLA Modules:
  0.0 267.3 jit_solution(8679838494003087928)
XLA Ops:
  8.3 3.2 %dynamic-slice_bitcast_fusion = bf16[8,8,128,128]{3,2,1,0:T(8,128)(2,1)} fusion(bf16[8,8,2,128,128]{4,3,2,1,0:T(8,128)(2,1)} %bitcast.67, s32[]{:T(128)S(6)} %select_n.109), kind=kLoop, calls=%fused_computation.3 | loop fusion | bytes 4194308 | tf_op jit(solution)/shard_map/jit(dynamic_index_in_dim)/squeeze | solution.py:190
  12.3 2.9 %collective-permute-done.6.refs_5_ = bf16[2048,128]{1,0:T(8,128)(2,1)S(1)} collective-permute-done((bf16[2048,128]{1,0:T(8,128)(2,1)S(1)}, bf16[2048,128]{1,0:T(8,128)(2,1)S(1)}, u32[]{:S(2)}, u32[]{:S(2)}) %collective-permute-start.6) | collective-permute-done | bytes 524320 | tf_op jit(solution)/shard_map/ppermute | solution.py:112
  22.0 2.7 %collective-permute-start.5 = (bf16[1024,128]{1,0:T(8,128)(2,1)S(1)}, bf16[1024,128]{1,0:T(8,128)(2,1)S(1)}, u32[]{:S(2)}, u32[]{:S(2)}) collective-permute-start(bf16[1024,128]{1,0:T(8,128)(2,1)S(1)} %slice.171), channel_id=1, source_target_pairs={{0,48},{16,0},{32,16},{48,32},{1,49},{17,1},{33,17},{49,33},{2,50}... | collective-permute-start | bytes 786440 | tf_op jit(solution)/shard_map/ppermute | solution.py:119
  24.8 9.9 %collective-permute-done.4.refs_2_ = bf16[1024,128]{1,0:T(8,128)(2,1)S(1)} collective-permute-done((bf16[1024,128]{1,0:T(8,128)(2,1)S(1)}, bf16[1024,128]{1,0:T(8,128)(2,1)S(1)}, u32[]{:S(2)}, u32[]{:S(2)}) %collective-permute-start.4) | collective-permute-done | bytes 262176 | tf_op jit(solution)/shard_map/ppermute | solution.py:118
  50.1 11.2 %all-to-all-start = ((bf16[128,16,256]{2,1,0:T(8,128)(2,1)}), bf16[128,16,256]{2,1,0:T(8,128)(2,1)}, u32[]{:S(2)}, u32[]{:S(2)}) async-start(bf16[128,16,256]{2,1,0:T(8,128)(2,1)} %bitcast.70), calls=%async_computation | async-start | bytes 2097152 | tf_op jit(solution)/shard_map/all_to_all | solution.py:167
  67.8 7.6 %collective-permute-start.18 = (bf16[1024,128]{1,0:T(8,128)(2,1)}, bf16[1024,128]{1,0:T(8,128)(2,1)}, u32[]{:S(2)}, u32[]{:S(2)}) collective-permute-start(bf16[1024,128]{1,0:T(8,128)(2,1)} %collective-permute-done.9.refs_7_), channel_id=1, source_target_pairs={{0,1},{1,0},{2,3},{3,2},{4,5},{5,4},{6,7},{7,6},{8,9},{9,8},{10,11... | collective-permute-start | bytes 786440 | tf_op jit(solution)/shard_map/ppermute | solution.py:209
  75.4 9.6 %collective-permute-done.29.refs_1_ = bf16[2048,128]{1,0:T(8,128)(2,1)S(1)} collective-permute-done((bf16[2048,128]{1,0:T(8,128)(2,1)S(1)}, bf16[2048,128]{1,0:T(8,128)(2,1)S(1)}, u32[]{:S(2)}, u32[]{:S(2)}) %collective-permute-start.29) | collective-permute-done | bytes 524320 | tf_op jit(solution)/shard_map/ppermute | solution.py:111
  89.3 4.4 %collective-permute-done.31.refs_2_ = bf16[1024,128]{1,0:T(8,128)(2,1)} collective-permute-done((bf16[1024,128]{1,0:T(8,128)(2,1)}, bf16[1024,128]{1,0:T(8,128)(2,1)}, u32[]{:S(2)}, u32[]{:S(2)}) %collective-permute-start.31) | collective-permute-done | bytes 262176 | tf_op jit(solution)/shard_map/ppermute | solution.py:118
  106.6 9.4 %chip_sums.2 = (bf16[2,8,128,128]{3,2,1,0:T(8,128)(2,1)S(1)}, bf16[2,8,128,128]{3,2,1,0:T(8,128)(2,1)S(1)}, bf16[2,8,128,128]{3,2,1,0:T(8,128)(2,1)S(1)}, bf16[2...) custom-call(s32[2,3,128]{2,1,0:T(4,128)S(1)} %pad_add_fusion.tables,, ...), custom_call_target="tpu_custom_call" | custom-call | flops 12000000000 | bytes 16777216 | tf_op jit(solution)/shard_map/chip_sums/pallas_call | solution.py:81
  120.0 3.0 %collective-permute-start.26 = (bf16[2,8,128,128]{3,2,1,0:T(8,128)(2,1)S(1)}, bf16[2,8,128,128]{3,2,1,0:T(8,128)(2,1)S(1)}, u32[]{:S(2)}, u32[]{:S(2)}) collective-permute-start(bf16[2,8,128,128]{3,2,1,0:T(8,128)(2,1)S(1)} %get-tuple-element.43), channel_id=1, source_target_pairs={{0,6},{2,0},{4,2},{6,4},{1,7},{3,1},{5,3},{7,5},{8,14},{10,8},{12,... | collective-permute-start | bytes 1572872 | tf_op jit(solution)/shard_map/ppermute | solution.py:144
  129.0 2.7 %collective-permute-done.22 = bf16[2,8,128,128]{3,2,1,0:T(8,128)(2,1)S(1)} collective-permute-done((bf16[2,8,128,128]{3,2,1,0:T(8,128)(2,1)S(1)}, bf16[2,8,128,128]{3,2,1,0:T(8,128)(2,1)S(1)}, u32[]{:S(2)}, u32[]{:S(2)}) %collective-permute-start.22) | collective-permute-done | bytes 524320 | tf_op jit(solution)/shard_map/ppermute | solution.py:143
  135.4 3.5 %collective-permute-start.21 = (bf16[2,8,128,128]{3,2,1,0:T(8,128)(2,1)S(1)}, bf16[2,8,128,128]{3,2,1,0:T(8,128)(2,1)S(1)}, u32[]{:S(2)}, u32[]{:S(2)}) collective-permute-start(bf16[2,8,128,128]{3,2,1,0:T(8,128)(2,1)S(1)} %get-tuple-element.37), channel_id=1, source_target_pairs={{0,6},{2,0},{4,2},{6,4},{1,7},{3,1},{5,3},{7,5},{8,14},{10,8},{12,... | collective-permute-start | bytes 1572872 | tf_op jit(solution)/shard_map/ppermute | solution.py:146
  141.7 8.4 %chip_sums.3 = (bf16[2,8,128,128]{3,2,1,0:T(8,128)(2,1)S(1)}, bf16[2,8,128,128]{3,2,1,0:T(8,128)(2,1)S(1)}, bf16[2,8,128,128]{3,2,1,0:T(8,128)(2,1)S(1)}, bf16[2...) custom-call(s32[2,3,128]{2,1,0:T(4,128)S(1)} %pad_add_fusion.tables,, ...), custom_call_target="tpu_custom_call" | custom-call | flops 12000000000 | bytes 16777216 | tf_op jit(solution)/shard_map/chip_sums/pallas_call | solution.py:81
  150.2 3.4 %collective-permute-start.48 = (bf16[2,8,128,128]{3,2,1,0:T(8,128)(2,1)S(1)}, bf16[2,8,128,128]{3,2,1,0:T(8,128)(2,1)S(1)}, u32[]{:S(2)}, u32[]{:S(2)}) collective-permute-start(bf16[2,8,128,128]{3,2,1,0:T(8,128)(2,1)S(1)} %get-tuple-element.46), channel_id=1, source_target_pairs={{0,6},{2,0},{4,2},{6,4},{1,7},{3,1},{5,3},{7,5},{8,14},{10,8},{12,... | collective-permute-start | bytes 1572872 | tf_op jit(solution)/shard_map/ppermute | solution.py:146
  153.7 10.9 %collective-permute-done.23 = bf16[2,8,128,128]{3,2,1,0:T(8,128)(2,1)S(1)} collective-permute-done((bf16[2,8,128,128]{3,2,1,0:T(8,128)(2,1)S(1)}, bf16[2,8,128,128]{3,2,1,0:T(8,128)(2,1)S(1)}, u32[]{:S(2)}, u32[]{:S(2)}) %collective-permute-start.23) | collective-permute-done | bytes 524320 | tf_op jit(solution)/shard_map/ppermute | solution.py:147
  168.0 7.8 %collective-permute-done.49 = bf16[2,8,128,128]{3,2,1,0:T(8,128)(2,1)S(1)} collective-permute-done((bf16[2,8,128,128]{3,2,1,0:T(8,128)(2,1)S(1)}, bf16[2,8,128,128]{3,2,1,0:T(8,128)(2,1)S(1)}, u32[]{:S(2)}, u32[]{:S(2)}) %collective-permute-start.49) | collective-permute-done | bytes 524320 | tf_op jit(solution)/shard_map/ppermute | solution.py:143
  177.6 6.3 %collective-permute-done.53 = bf16[2,8,128,128]{3,2,1,0:T(8,128)(2,1)S(1)} collective-permute-done((bf16[2,8,128,128]{3,2,1,0:T(8,128)(2,1)S(1)}, bf16[2,8,128,128]{3,2,1,0:T(8,128)(2,1)S(1)}, u32[]{:S(2)}, u32[]{:S(2)}) %collective-permute-start.53) | collective-permute-done | bytes 524320 | tf_op jit(solution)/shard_map/ppermute | solution.py:144
  184.1 3.5 %collective-permute-start.54 = (bf16[2,8,128,128]{3,2,1,0:T(8,128)(2,1)S(1)}, bf16[2,8,128,128]{3,2,1,0:T(8,128)(2,1)S(1)}, u32[]{:S(2)}, u32[]{:S(2)}) collective-permute-start(bf16[2,8,128,128]{3,2,1,0:T(8,128)(2,1)S(1)} %add_convert_fusion), channel_id=1, source_target_pairs={{0,6},{2,0},{4,2},{6,4},{1,7},{3,1},{5,3},{7,5},{8,14},{10,8},{12,... | collective-permute-start | bytes 1572872 | tf_op jit(solution)/shard_map/ppermute | solution.py:148
  187.9 11.0 %collective-permute-done.50 = bf16[2,8,128,128]{3,2,1,0:T(8,128)(2,1)S(1)} collective-permute-done((bf16[2,8,128,128]{3,2,1,0:T(8,128)(2,1)S(1)}, bf16[2,8,128,128]{3,2,1,0:T(8,128)(2,1)S(1)}, u32[]{:S(2)}, u32[]{:S(2)}) %collective-permute-start.50) | collective-permute-done | bytes 524320 | tf_op jit(solution)/shard_map/ppermute | solution.py:147
  202.5 4.7 %collective-permute-done.51 = bf16[8,128,128]{2,1,0:T(8,128)(2,1)S(1)} collective-permute-done((bf16[8,128,128]{2,1,0:T(8,128)(2,1)S(1)}, bf16[8,128,128]{2,1,0:T(8,128)(2,1)S(1)}, u32[]{:S(2)}, u32[]{:S(2)}) %collective-permute-start.51) | collective-permute-done | bytes 262176 | tf_op jit(solution)/shard_map/ppermute | solution.py:149
  207.4 5.5 %collective-permute-done.55 = bf16[8,128,128]{2,1,0:T(8,128)(2,1)S(1)} collective-permute-done((bf16[8,128,128]{2,1,0:T(8,128)(2,1)S(1)}, bf16[8,128,128]{2,1,0:T(8,128)(2,1)S(1)}, u32[]{:S(2)}, u32[]{:S(2)}) %collective-permute-start.55) | collective-permute-done | bytes 262176 | tf_op jit(solution)/shard_map/ppermute | solution.py:150
  216.7 32.9 %all_to_all.15 = bf16[128,20,256]{2,1,0:T(8,128)(2,1)S(1)} all-to-all(bf16[128,20,256]{2,1,0:T(8,128)(2,1)S(1)} %pad_maximum_fusion), channel_id=1, replica_groups=mesh['xl'=2,'y'=4,'xh'=2,'z'=4,'core'=2] {'xl','y','xh','z','core'}, dimensions={0} | all-to-all | bytes 2621440 | tf_op jit(solution)/shard_map/all_to_all | solution.py:224
  250.7 4.5 %all-to-all-start.2 = ((f32[128,2,256]{2,1,0:T(2,128)}), f32[128,2,256]{2,1,0:T(2,128)S(1)}, u32[]{:S(2)}, u32[]{:S(2)}) async-start(f32[128,2,256]{2,1,0:T(2,128)} %broadcast_in_dim.2), calls=%async_computation.2 | async-start | bytes 524288 | tf_op jit(solution)/shard_map/all_to_all | solution.py:231
  256.3 10.2 %all-to-all-done.2 = f32[128,2,256]{2,1,0:T(2,128)S(1)} async-done(((f32[128,2,256]{2,1,0:T(2,128)}), f32[128,2,256]{2,1,0:T(2,128)S(1)}, u32[]{:S(2)}, u32[]{:S(2)}) %all-to-all-start.2) | async-done | bytes 262176 | tf_op jit(solution)/shard_map/all_to_all | solution.py:231
  (173 shorter events, 86.4 us)
Async XLA Ops:
  11.5 83.3 %collective-permute-start.2 = (bf16[8,8,128,128]{3,2,1,0:T(8,128)(2,1)}, bf16[8,8,128,128]{3,2,1,0:T(8,128)(2,1)}, u32[]{:S(2)}, u32[]{:S(2)}) collective-permute-start(bf16[8,8,128,128]{3,2,1,0:T(8,128)(2,1)} %dynamic-slice_bitcast_fusion), channel_id=1, source_target_pairs={{0,1},{1,0},{2,3},{3,2},{4,5},{5,4},{6,7},{7,6},{8,9},{9,8},{10,11... | collective-permute-start | bytes 6291464 | tf_op jit(solution)/shard_map/ppermute | solution.py:190
  15.2 25.3 %collective-permute-start.8 = (bf16[2048,128]{1,0:T(8,128)(2,1)S(1)}, bf16[2048,128]{1,0:T(8,128)(2,1)}, u32[]{:S(2)}, u32[]{:S(2)}) collective-permute-start(bf16[2048,128]{1,0:T(8,128)(2,1)S(1)} %collective-permute-done.6.refs_5_), channel_id=1, source_target_pairs={{0,16},{16,32},{32,48},{48,0},{1,17},{17,33},{33,49},{49,1},{2,18}... | collective-permute-start | bytes 1572872 | tf_op jit(solution)/shard_map/ppermute | solution.py:120
  20.5 20.1 %collective-permute-start.7 = (bf16[2048,128]{1,0:T(8,128)(2,1)S(1)}, bf16[2048,128]{1,0:T(8,128)(2,1)}, u32[]{:S(2)}, u32[]{:S(2)}) collective-permute-start(bf16[2048,128]{1,0:T(8,128)(2,1)S(1)} %collective-permute-done.6.refs_5_), channel_id=1, source_target_pairs={{0,48},{16,0},{32,16},{48,32},{1,49},{17,1},{33,17},{49,33},{2,50}... | collective-permute-start | bytes 1572872 | tf_op jit(solution)/shard_map/ppermute | solution.py:121
  22.0 17.3 %collective-permute-start.5 = (bf16[1024,128]{1,0:T(8,128)(2,1)S(1)}, bf16[1024,128]{1,0:T(8,128)(2,1)S(1)}, u32[]{:S(2)}, u32[]{:S(2)}) collective-permute-start(bf16[1024,128]{1,0:T(8,128)(2,1)S(1)} %slice.171), channel_id=1, source_target_pairs={{0,48},{16,0},{32,16},{48,32},{1,49},{17,1},{33,17},{49,33},{2,50}... | collective-permute-start | bytes 786440 | tf_op jit(solution)/shard_map/ppermute | solution.py:119
  40.6 20.8 %collective-permute-start.12 = (bf16[2048,128]{1,0:T(8,128)(2,1)S(1)}, bf16[2048,128]{1,0:T(8,128)(2,1)}, u32[]{:S(2)}, u32[]{:S(2)}) collective-permute-start(bf16[2048,128]{1,0:T(8,128)(2,1)S(1)} %collective-permute-done.3.refs_1_), channel_id=1, source_target_pairs={{0,1},{1,0},{2,3},{3,2},{4,5},{5,4},{6,7},{7,6},{8,9},{9,8},{10,11... | collective-permute-start | bytes 1572872 | tf_op jit(solution)/shard_map/ppermute | solution.py:209
  45.8 16.7 %collective-permute-start.9 = (bf16[1024,128]{1,0:T(8,128)(2,1)}, bf16[1024,128]{1,0:T(8,128)(2,1)}, u32[]{:S(2)}, u32[]{:S(2)}) collective-permute-start(bf16[1024,128]{1,0:T(8,128)(2,1)} %slice.172), channel_id=1, source_target_pairs={{0,16},{16,32},{32,48},{48,0},{1,17},{17,33},{33,49},{49,1},{2,18}... | collective-permute-start | bytes 786440 | tf_op jit(solution)/shard_map/ppermute | solution.py:128
  50.1 36.7 %all-to-all-start = ((bf16[128,16,256]{2,1,0:T(8,128)(2,1)}), bf16[128,16,256]{2,1,0:T(8,128)(2,1)}, u32[]{:S(2)}, u32[]{:S(2)}) async-start(bf16[128,16,256]{2,1,0:T(8,128)(2,1)} %bitcast.70), calls=%async_computation | async-start | bytes 2097152 | tf_op jit(solution)/shard_map/all_to_all | solution.py:167
  62.7 22.4 %collective-permute-start.29 = (bf16[2048,128]{1,0:T(8,128)(2,1)S(1)}, bf16[2048,128]{1,0:T(8,128)(2,1)S(1)}, u32[]{:S(2)}, u32[]{:S(2)}) collective-permute-start(bf16[2048,128]{1,0:T(8,128)(2,1)S(1)} %get-tuple-element.44.refs_0_), channel_id=1, source_target_pairs={{0,48},{16,0},{32,16},{48,32},{1,49},{17,1},{33,17},{49,33},{2,50}... | collective-permute-start | bytes 1572872 | tf_op jit(solution)/shard_map/ppermute | solution.py:111
  66.4 20.5 %collective-permute-start.33 = (bf16[2048,128]{1,0:T(8,128)(2,1)S(1)}, bf16[2048,128]{1,0:T(8,128)(2,1)}, u32[]{:S(2)}, u32[]{:S(2)}) collective-permute-start(bf16[2048,128]{1,0:T(8,128)(2,1)S(1)} %get-tuple-element.44.refs_0_), channel_id=1, source_target_pairs={{0,64},{64,0},{1,65},{65,1},{2,66},{66,2},{3,67},{67,3},{4,68},{68... | collective-permute-start | bytes 1572872 | tf_op jit(solution)/shard_map/ppermute | solution.py:112
  67.8 20.0 %collective-permute-start.18 = (bf16[1024,128]{1,0:T(8,128)(2,1)}, bf16[1024,128]{1,0:T(8,128)(2,1)}, u32[]{:S(2)}, u32[]{:S(2)}) collective-permute-start(bf16[1024,128]{1,0:T(8,128)(2,1)} %collective-permute-done.9.refs_7_), channel_id=1, source_target_pairs={{0,1},{1,0},{2,3},{3,2},{4,5},{5,4},{6,7},{7,6},{8,9},{9,8},{10,11... | collective-permute-start | bytes 786440 | tf_op jit(solution)/shard_map/ppermute | solution.py:209
  86.9 29.1 %collective-permute-start.38 = (bf16[2048,128]{1,0:T(8,128)(2,1)S(1)}, bf16[2048,128]{1,0:T(8,128)(2,1)S(1)}, u32[]{:S(2)}, u32[]{:S(2)}) collective-permute-start(bf16[2048,128]{1,0:T(8,128)(2,1)S(1)} %get-tuple-element.44.refs_0_), channel_id=1, source_target_pairs={{0,1},{1,0},{2,3},{3,2},{4,5},{5,4},{6,7},{7,6},{8,9},{9,8},{10,11... | collective-permute-start | bytes 1572872 | tf_op jit(solution)/shard_map/ppermute | solution.py:209
  87.8 28.3 %collective-permute-start.32 = (bf16[1024,128]{1,0:T(8,128)(2,1)S(1)}, bf16[1024,128]{1,0:T(8,128)(2,1)S(1)}, u32[]{:S(2)}, u32[]{:S(2)}) collective-permute-start(bf16[1024,128]{1,0:T(8,128)(2,1)S(1)} %slice.183), channel_id=1, source_target_pairs={{0,48},{16,0},{32,16},{48,32},{1,49},{17,1},{33,17},{49,33},{2,50}... | collective-permute-start | bytes 786440 | tf_op jit(solution)/shard_map/ppermute | solution.py:119
  88.9 27.8 %collective-permute-start.35 = (bf16[2048,128]{1,0:T(8,128)(2,1)}, bf16[2048,128]{1,0:T(8,128)(2,1)S(1)}, u32[]{:S(2)}, u32[]{:S(2)}) collective-permute-start(bf16[2048,128]{1,0:T(8,128)(2,1)} %collective-permute-done.33.refs_5_), channel_id=1, source_target_pairs={{0,16},{16,32},{32,48},{48,0},{1,17},{17,33},{33,49},{49,1},{2,18}... | collective-permute-start | bytes 1572872 | tf_op jit(solution)/shard_map/ppermute | solution.py:120
  93.7 26.4 %collective-permute-start.34 = (bf16[2048,128]{1,0:T(8,128)(2,1)}, bf16[2048,128]{1,0:T(8,128)(2,1)S(1)}, u32[]{:S(2)}, u32[]{:S(2)}) collective-permute-start(bf16[2048,128]{1,0:T(8,128)(2,1)} %collective-permute-done.33.refs_5_), channel_id=1, source_target_pairs={{0,48},{16,0},{32,16},{48,32},{1,49},{17,1},{33,17},{49,33},{2,50}... | collective-permute-start | bytes 1572872 | tf_op jit(solution)/shard_map/ppermute | solution.py:121
  94.8 21.8 %collective-permute-start.40 = (bf16[1024,128]{1,0:T(8,128)(2,1)}, bf16[1024,128]{1,0:T(8,128)(2,1)S(1)}, u32[]{:S(2)}, u32[]{:S(2)}) collective-permute-start(bf16[1024,128]{1,0:T(8,128)(2,1)} %collective-permute-done.31.refs_2_), channel_id=1, source_target_pairs={{0,1},{1,0},{2,3},{3,2},{4,5},{5,4},{6,7},{7,6},{8,9},{9,8},{10,11... | collective-permute-start | bytes 786440 | tf_op jit(solution)/shard_map/ppermute | solution.py:209
  138.9 25.8 %collective-permute-start.25 = (bf16[2,8,128,128]{3,2,1,0:T(8,128)(2,1)S(1)}, bf16[2,8,128,128]{3,2,1,0:T(8,128)(2,1)S(1)}, u32[]{:S(2)}, u32[]{:S(2)}) collective-permute-start(bf16[2,8,128,128]{3,2,1,0:T(8,128)(2,1)S(1)} %get-tuple-element.41), channel_id=1, source_target_pairs={{0,2},{2,4},{4,6},{6,0},{1,3},{3,5},{5,7},{7,1},{8,10},{10,12},{12... | collective-permute-start | bytes 1572872 | tf_op jit(solution)/shard_map/ppermute | solution.py:145
  138.9 25.7 %collective-permute-start.23 = (bf16[2,8,128,128]{3,2,1,0:T(8,128)(2,1)S(1)}, bf16[2,8,128,128]{3,2,1,0:T(8,128)(2,1)S(1)}, u32[]{:S(2)}, u32[]{:S(2)}) collective-permute-start(bf16[2,8,128,128]{3,2,1,0:T(8,128)(2,1)S(1)} %add_convert_fusion.3), channel_id=1, source_target_pairs={{0,2},{2,4},{4,6},{6,0},{1,3},{3,5},{5,7},{7,1},{8,10},{10,12},{12... | collective-permute-start | bytes 1572872 | tf_op jit(solution)/shard_map/ppermute | solution.py:147
  139.0 27.2 %collective-permute-start.27 = (bf16[2,8,128,128]{3,2,1,0:T(8,128)(2,1)S(1)}, bf16[2,8,128,128]{3,2,1,0:T(8,128)(2,1)S(1)}, u32[]{:S(2)}, u32[]{:S(2)}) collective-permute-start(bf16[2,8,128,128]{3,2,1,0:T(8,128)(2,1)S(1)} %add_convert_fusion.2), channel_id=1, source_target_pairs={{0,6},{2,0},{4,2},{6,4},{1,7},{3,1},{5,3},{7,5},{8,14},{10,8},{12,... | collective-permute-start | bytes 1572872 | tf_op jit(solution)/shard_map/ppermute | solution.py:148
  150.1 25.7 %collective-permute-start.49 = (bf16[2,8,128,128]{3,2,1,0:T(8,128)(2,1)S(1)}, bf16[2,8,128,128]{3,2,1,0:T(8,128)(2,1)S(1)}, u32[]{:S(2)}, u32[]{:S(2)}) collective-permute-start(bf16[2,8,128,128]{3,2,1,0:T(8,128)(2,1)S(1)} %get-tuple-element.48), channel_id=1, source_target_pairs={{0,2},{2,4},{4,6},{6,0},{1,3},{3,5},{5,7},{7,1},{8,10},{10,12},{12... | collective-permute-start | bytes 1572872 | tf_op jit(solution)/shard_map/ppermute | solution.py:143
  150.2 37.7 %collective-permute-start.48 = (bf16[2,8,128,128]{3,2,1,0:T(8,128)(2,1)S(1)}, bf16[2,8,128,128]{3,2,1,0:T(8,128)(2,1)S(1)}, u32[]{:S(2)}, u32[]{:S(2)}) collective-permute-start(bf16[2,8,128,128]{3,2,1,0:T(8,128)(2,1)S(1)} %get-tuple-element.46), channel_id=1, source_target_pairs={{0,6},{2,0},{4,2},{6,4},{1,7},{3,1},{5,3},{7,5},{8,14},{10,8},{12,... | collective-permute-start | bytes 1572872 | tf_op jit(solution)/shard_map/ppermute | solution.py:146
  164.6 19.4 %collective-permute-start.53 = (bf16[2,8,128,128]{3,2,1,0:T(8,128)(2,1)S(1)}, bf16[2,8,128,128]{3,2,1,0:T(8,128)(2,1)S(1)}, u32[]{:S(2)}, u32[]{:S(2)}) collective-permute-start(bf16[2,8,128,128]{3,2,1,0:T(8,128)(2,1)S(1)} %get-tuple-element.52), channel_id=1, source_target_pairs={{0,6},{2,0},{4,2},{6,4},{1,7},{3,1},{5,3},{7,5},{8,14},{10,8},{12,... | collective-permute-start | bytes 1572872 | tf_op jit(solution)/shard_map/ppermute | solution.py:144
  164.7 36.3 %collective-permute-start.52 = (bf16[2,8,128,128]{3,2,1,0:T(8,128)(2,1)S(1)}, bf16[2,8,128,128]{3,2,1,0:T(8,128)(2,1)S(1)}, u32[]{:S(2)}, u32[]{:S(2)}) collective-permute-start(bf16[2,8,128,128]{3,2,1,0:T(8,128)(2,1)S(1)} %get-tuple-element.50), channel_id=1, source_target_pairs={{0,2},{2,4},{4,6},{6,0},{1,3},{3,5},{5,7},{7,1},{8,10},{10,12},{12... | collective-permute-start | bytes 1572872 | tf_op jit(solution)/shard_map/ppermute | solution.py:145
  166.2 17.9 %collective-permute-start.24 = (bf16[8,128,128]{2,1,0:T(8,128)(2,1)S(1)}, bf16[8,128,128]{2,1,0:T(8,128)(2,1)S(1)}, u32[]{:S(2)}, u32[]{:S(2)}) collective-permute-start(bf16[8,128,128]{2,1,0:T(8,128)(2,1)S(1)} %fusion.7), channel_id=1, source_target_pairs={{0,8},{8,0},{1,9},{9,1},{2,10},{10,2},{3,11},{11,3},{4,12},{12,4},... | collective-permute-start | bytes 786440 | tf_op jit(solution)/shard_map/ppermute | solution.py:149
  184.1 16.9 %collective-permute-start.54 = (bf16[2,8,128,128]{3,2,1,0:T(8,128)(2,1)S(1)}, bf16[2,8,128,128]{3,2,1,0:T(8,128)(2,1)S(1)}, u32[]{:S(2)}, u32[]{:S(2)}) collective-permute-start(bf16[2,8,128,128]{3,2,1,0:T(8,128)(2,1)S(1)} %add_convert_fusion), channel_id=1, source_target_pairs={{0,6},{2,0},{4,2},{6,4},{1,7},{3,1},{5,3},{7,5},{8,14},{10,8},{12,... | collective-permute-start | bytes 1572872 | tf_op jit(solution)/shard_map/ppermute | solution.py:148
  (52 other events, 676.4 us)

commit v3 on v2

v3 whole, which is shorter than its diff:
```python
import functools

import jax
import jax.numpy as jnp
from jax import lax
from jax.experimental import pallas as pl
from jax.experimental.pallas import tpu as pltpu
from jax.sharding import Mesh, PartitionSpec as P

BS = 128
WIDTH = 256
OWNER_BLOCKS = 16
LOW = 9
SIDE_FIRST = 10
TURNS = 8
PEERS = 8
CB = 128


def ring(size, step):
    return [(i, (i + step) % size) for i in range(size)]


def permute(value, axis, step):
    return lax.ppermute(value, axis, ring(lax.axis_size(axis), step))


def load_slab(layout, pieces, slab, sems):
    copies = []
    for n, (piece, start, rows, place) in enumerate(layout):
        source = pieces[piece].at[pl.ds(start, rows)]
        copy = pltpu.make_async_copy(source, slab.at[pl.ds(place, rows)], sems.at[n])
        copy.start()
        copies.append(copy)
    for copy in copies:
        copy.wait()


def chip_kernel(
    layout, n_pieces, stores, tables, owners, core, adj_ref, other_adj_ref, *refs
):
    pieces, outs, (slab, sums, sems) = refs[:n_pieces], refs[n_pieces:-3], refs[-3:]
    step = pl.program_id(0)

    @pl.when(step == 0)
    def _():
        load_slab(layout, pieces, slab, sems)

    sums[...] = jnp.zeros_like(sums)

    def product(cell, slot, block):
        start = pl.multiple_of(tables[cell, 0, slot] * BS, BS)
        found = jnp.dot(block, slab[pl.ds(start, BS), :], preferred_element_type=jnp.float32)
        return jnp.where(slot < tables[cell, 2, 0], found, 0.0).astype(jnp.bfloat16)

    slots = [turn * 16 + owners[step] * 2 + core[0] for turn in range(TURNS)]
    for turn, slot in enumerate(slots):
        sums[tables[0, 1, slot]] = product(0, slot, adj_ref[turn, 0, 0])
    for turn, slot in enumerate(slots):
        row = tables[1, 1, slot]
        term = product(1, slot, other_adj_ref[turn, 0]).astype(jnp.float32)
        sums[row] = (sums[row].astype(jnp.float32) + term).astype(jnp.bfloat16)

    for out, (first, last, start, stop, every) in zip(outs, stores):

        @pl.when((step >= first) & (step < last) & ((step - first) % every == 0))
        def _():
            out[0] = sums[start:stop]


def chip_sums(gathered, distances, tables, owners, core, adj, other_adj):
    layout, pieces = gathered
    steps = 2 * len(distances)
    high = OWNER_BLOCKS - LOW
    shapes, specs, stores = [], [], []

    def output(count, blocks, place, store):
        shapes.append(jax.ShapeDtypeStruct((count, blocks, BS, WIDTH), jnp.bfloat16))
        specs.append(pl.BlockSpec((1, blocks, BS, WIDTH), lambda g, *_: (place(g), 0, 0, 0)))
        stores.append(store)

    for n, distance in enumerate(distances):
        cuts = (0, LOW // 2, LOW) if distance == 2 else (0, LOW)
        for start, stop in zip(cuts, cuts[1:]):
            output(
                2,
                stop - start,
                lambda g, first=2 * n: jnp.clip(g - first, 0, 1),
                (2 * n, 2 * n + 2, start, stop, 1),
            )
    for side in range(2):
        output(len(distances), high, lambda g: g // 2, (side, steps, LOW, OWNER_BLOCKS, 2))
    return pl.pallas_call(
        functools.partial(chip_kernel, layout, len(pieces), stores),
        out_shape=shapes,
        grid_spec=pltpu.PrefetchScalarGridSpec(
            num_scalar_prefetch=3,
            grid=(steps,),
            in_specs=[
                pl.BlockSpec((TURNS, 1, 1, BS, BS), lambda g, tb, ow, co: (0, ow[g], co[0], 0, 0)),
                pl.BlockSpec((TURNS, 1, BS, BS), lambda g, tb, ow, co: (0, ow[g], 0, 0)),
                *[pl.BlockSpec(memory_space=pl.ANY)] * len(pieces),
            ],
            out_specs=specs,
            scratch_shapes=[
                pltpu.VMEM((2 * CB * BS, WIDTH), jnp.bfloat16),
                pltpu.VMEM((OWNER_BLOCKS, BS, WIDTH), jnp.bfloat16),
                pltpu.SemaphoreType.DMA((len(layout),)),
            ],
        ),
        compiler_params=pltpu.CompilerParams(
            dimension_semantics=("arbitrary",), vmem_limit_bytes=60 * 1024 * 1024
        ),
        cost_estimate=pl.CostEstimate(
            flops=2_000_000_000 * (3 + steps), bytes_accessed=1024, transcendentals=0
        ),
        name="chip_sums",
    )(tables, owners(distances), core, adj, other_adj, *pieces)


def copy_rows_kernel(plans, n_sources, *refs):
    n_outs = len(plans)
    sources, outs, held = refs[:n_sources], refs[n_sources:-n_outs - 1], refs[-n_outs - 1 : -1]
    sems = refs[-1]
    loads, stores = [], []
    for out, buffer, plan in zip(outs, held, plans):
        place = 0
        for source, start, stop in plan:
            here, n = pl.ds(place, stop - start), len(loads)
            there = sources[source].at[pl.ds(start, stop - start)]
            loads.append(pltpu.make_async_copy(there, buffer.at[here], sems.at[0, n]))
            stores.append(pltpu.make_async_copy(buffer.at[here], out.at[here], sems.at[1, n]))
            place += stop - start
    for load in loads:
        load.start()
    for load, store in zip(loads, stores):
        load.wait()
        store.start()
    for store in stores:
        store.wait()


def copy_rows(sources, *plans):
    sizes = [(sum(stop - start for _, start, stop in plan), WIDTH) for plan in plans]
    dtype = sources[0].dtype
    any_spec = pl.BlockSpec(memory_space=pl.ANY)
    return pl.pallas_call(
        functools.partial(copy_rows_kernel, plans, len(sources)),
        out_shape=[jax.ShapeDtypeStruct(size, dtype) for size in sizes],
        in_specs=[any_spec] * len(sources),
        out_specs=[any_spec] * len(plans),
        scratch_shapes=[
            *[pltpu.VMEM(size, dtype) for size in sizes],
            pltpu.SemaphoreType.DMA((2, sum(len(plan) for plan in plans))),
        ],
        compiler_params=pltpu.CompilerParams(vmem_limit_bytes=60 * 1024 * 1024),
        name="copy_rows",
    )(*sources)


def together(*values):
    return lax.optimization_barrier(values)


def gather(own, shared, others):
    n = own.shape[0]
    half, first = n // 2, SIDE_FIRST * BS
    last, cut = n - first, SIDE_FIRST // 2 * BS
    up, down, side = permute(own, "y", 1), permute(own, "y", -1), permute(own, "xl", 1)
    shared = [permute(value, "core", 1) for value in shared]
    up, down, side, shared = together(up, down, side, shared)
    go_up, go_down, go_across = copy_rows(
        (up, down, side),
        ((0, 0, half), (2, 0, first)),
        ((1, half, n), (2, 0, first)),
        ((0, first, n), (1, first, n)),
    )
    via_up, via_down = permute(go_up, "y", 1), permute(go_down, "y", -1)
    across = permute(go_across, "xl", 1)
    others = others(up)
    via_up, via_down, across, others = together(via_up, via_down, across, others)
    ends = copy_rows(
        (via_up, via_down),
        ((0, half, half + cut),),
        ((1, half + cut, half + first),),
        ((1, first - half, half),),
    )
    end_up = permute(ends[0], "y", 1)
    end_down = permute(ends[1], "y", -1)
    end_across = permute(ends[2], "xl", 1)
    early = [own, up, down, side, via_up, via_down, across]
    late = [end_up, end_down, end_across]
    parts = [
        [(0, n, 0)],
        [(0, n, 3 * n)],
        [(0, n, n)],
        [(0, n, 4 * n)],
        [(0, half, 2 * n), (half, first, 7 * n)],
        [(0, half, 2 * n + half), (half, first, 5 * n)],
        [(0, last, 7 * n + first), (last, last, 5 * n + first)],
        [(0, cut, 6 * n)],
        [(0, first - cut, 6 * n + cut)],
        [(0, last, 6 * n + first)],
    ]
    pieces = early + late
    pieces += [permute(x, "core", 1) for x in pieces]
    layout = [(i, *part) for i, each in enumerate(parts) for part in each]
    layout += [(len(parts) + i, start, rows, place + 8 * n) for i, start, rows, place in layout]
    return layout, pieces, shared, others


def add(*terms):
    total = terms[0].astype(jnp.float32)
    for term in terms[1:]:
        total = total + term.astype(jnp.float32)
    return total.astype(jnp.bfloat16)


def reduce_to_owner(far, near):
    far_a, far_b, keep, give = far
    via_a = permute(far_a, "z", 1)
    via_b = permute(far_b, "z", -1)
    came = permute(give, "xh", 1)
    via_a, via_b, came, near = together(via_a, via_b, came, near)
    cut = came.shape[1] // 2
    high_a = permute(add(keep[0, :cut], came[0, :cut]), "z", 1)
    high_b = permute(add(keep[0, cut:], came[0, cut:]), "z", -1)
    up, down, own, keep, give = near
    part = via_a.shape[1]
    up = lax.dynamic_update_slice(up, add(up[:, :part], via_a), (0, 0, 0, 0))
    down = lax.dynamic_update_slice(down, add(down[:, part:], via_b), (0, part, 0, 0))
    came = permute(give, "xh", 1)
    up, down, came, high_a, high_b = together(
        permute(up, "z", 1), permute(down, "z", -1), came, high_a, high_b
    )
    low_side = permute(add(own[1], up[1], down[1]), "xh", 1)
    high = [add(keep[n], came[n]) for n in range(2)]
    high_up = jnp.concatenate([add(high[0][:cut], high_a), high[0][cut:]])
    high_down = jnp.concatenate([high[1][:cut], add(high[1][cut:], high_b)])
    low_side, high_up, high_down = together(
        low_side, permute(high_up, "z", 1), permute(high_down, "z", -1)
    )
    high = add(keep[2], came[2], high_up, high_down)
    return jnp.concatenate([add(own[0], up[0], down[0], low_side), high]).reshape(-1, WIDTH)


def derivative(preact, grad_rows):
    sigmoid_pre = jax.nn.sigmoid(preact)
    return (
        grad_rows.astype(jnp.float32) * sigmoid_pre * (1.0 + preact * (1.0 - sigmoid_pre))
    ).astype(jnp.bfloat16)


AXES = ("xl", "y", "xh", "z", "core")


def swap_all(rows, devices_all):
    return lax.all_to_all(
        rows.reshape(devices_all, -1, rows.shape[-1]), AXES, split_axis=0, concat_axis=0, tiled=True
    )


def on_device(features, weight, adj_rows, adj_cols, adj_blocks, counts, grad_out):
    local_rows, feat_width = features.shape
    devices_all = 128
    xl, y, xh, z, core = (lax.axis_index(name) for name in AXES)

    slots = jnp.arange(adj_rows.shape[-1], dtype=jnp.int32)
    rows = adj_rows.reshape(-1) - (slots % 16) * OWNER_BLOCKS
    cols = adj_cols.reshape(-1)
    source = cols // OWNER_BLOCKS
    away = ((source // 4) ^ xl) * 4 + (source % 4 - y) % 4
    cols = away * OWNER_BLOCKS + cols % OWNER_BLOCKS
    mine = jnp.stack([cols, rows, jnp.broadcast_to(counts.reshape(1), rows.shape)])

    def owners(distances):
        chips = [(xh ^ dx) * 4 + (z + dz) % 4 for dz in distances for dx in range(2)]
        return jnp.stack(chips).astype(jnp.int32)

    adj = adj_blocks.reshape(TURNS, PEERS, 2, BS, BS)
    other_adj = lax.dynamic_index_in_dim(adj, 1 - core, 2, keepdims=False)

    def tied(value, *others):
        return lax.optimization_barrier((value, others))[0]

    sub_rows = local_rows // devices_all

    def grads_first(after):
        grads = tied(grad_out, after).reshape(2, 4, 16, sub_rows, feat_width)
        grads = grads.transpose(0, 2, 1, 3, 4).reshape(32, 4, sub_rows, feat_width)
        return lax.all_to_all(grads, ("xl", "xh", "z", "core"), 0, 0, tiled=True)

    def grads_last(grads, after):
        grads = tied(grads, after).transpose(1, 0, 2, 3)
        grads = lax.all_to_all(grads, "y", 0, 0, tiled=True)
        grads = grads.reshape(4, 2, 16, sub_rows, feat_width).transpose(1, 0, 2, 3, 4)
        return grads.reshape(local_rows, feat_width)

    layout, pieces, (theirs, other_adj), grads = gather(features, (mine, other_adj), grads_first)
    tables = jnp.stack([mine, theirs.at[0].add(CB)])
    products = functools.partial(
        chip_sums, tables=tables, owners=owners, core=core.reshape(1), adj=adj, other_adj=other_adj
    )
    far = products((layout, pieces), (2,))

    near = products((layout, pieces), (1, 3, 0))
    agg = reduce_to_owner(far, near)
    grad_row = grads_last(grads, near)

    preact = jnp.dot(agg, weight, preferred_element_type=jnp.float32)
    out_row = jax.nn.silu(preact).astype(jnp.bfloat16)
    grad_pre = derivative(preact, grad_row)
    contract = (((0,), (0,)), ((), ()))
    weight_part = lax.dot_general(agg, grad_pre, contract, preferred_element_type=jnp.float32)
    coarse = lax.reduce_precision(weight_part, 8, 7)
    terms = [coarse.astype(jnp.bfloat16), (weight_part - coarse).astype(jnp.bfloat16)]
    lanes = [out_row[:, :BS], out_row[:, BS:], *terms]
    sent = jnp.concatenate([x.reshape(devices_all, -1, BS) for x in lanes], axis=1)
    came = lax.all_to_all(sent, AXES, split_axis=0, concat_axis=0, tiled=True)
    piece = local_rows // devices_all
    out_col = jnp.concatenate([came[:, :piece], came[:, piece : 2 * piece]], axis=2)
    out_col = out_col.reshape(local_rows, feat_width)
    came = came[:, 2 * piece :].astype(jnp.float32)
    each = came.shape[1] // 2
    summed = jnp.sum(came[:, :each] + came[:, each:], axis=0) * (local_rows * devices_all) ** (-0.5)
    summed = summed.reshape(-1, feat_width)
    spread = jnp.broadcast_to(summed[None], (devices_all, *summed.shape))
    weight_grad = lax.all_to_all(spread, AXES, split_axis=0, concat_axis=0, tiled=True)
    return (out_col, weight_grad.reshape(feat_width, feat_width))


def solution(mesh):
    fine = Mesh(mesh.devices.reshape(2, 4, 2, 4, 2), AXES)
    row, col = ("xl", "y"), ("xh", "z", "core")
    placed = (
        P((*col, *row), None),
        P(),
        P(row, col, None),
        P(row, col, None),
        P(row, col, None, None, None),
        P(row, col),
        P((*col, *row), None),
    )
    return jax.shard_map(
        on_device,
        mesh=fine,
        in_specs=placed,
        out_specs=(P((*col, *row), None), P()),
        check_vma=False,
    )
```

time: 268 us -> 235 us (0.88)
  starting transfers between devices: 88.8 us -> 54.2 us
  local copies, waits for them, and re-layouts: 24 us -> 9.29 us
  other arithmetic: 2.59 us -> 16.9 us
  Pallas kernels: 17.8 us -> 30.8 us
  waiting for transfers between devices: 96.5 us -> 86.2 us
    ppermute x56 -> x32, starting transfers between devices: 73.1 us -> 38.1 us  [permute(): return lax.ppermute(value, axis, ring(lax.axis_size(axis), step))]
    ppermute x56 -> x32, waiting for transfers between devices: 86.3 us -> 70.7 us  [permute(): return lax.ppermute(value, axis, ring(lax.axis_size(axis), step))]
    pallas_call x2 -> x4, Pallas kernels: 17.8 us -> 30.8 us  [the longest x2 25.3 us: chip_sums(): pl.pallas_call(functools.partial(chip_kernel, layout, len(pieces), stores...]
    unnamed x36 -> x22, local copies, waits for them, and re-layouts: 12.2 us -> 1.19 us
    slice x10 -> x4, local copies, waits for them, and re-layouts: 6.54 us -> 0.29 us  [the longest x1 0.18 us: on_device(): came[:, :piece]]
    convert_element_type x12 -> x8, other arithmetic: 1.66 us -> 7.89 us  [add(): return total.astype(jnp.bfloat16)]
    all_to_all x1 -> x2, waiting for transfers between devices: 0.01 us -> 5.5 us  [the longest x1 5.49 us: grads_first(): return lax.all_to_all(grads, ('xl', 'xh', 'z', 'core'), 0, 0, tiled=True)]
    dynamic_update_slice x0 -> x2, other arithmetic: none -> 4.15 us  [the longest x1 2.19 us: reduce_to_owner(): lax.dynamic_update_slice(down, add(down[:, part:], via_b), (0, part, 0, 0))]
  transfers between devices with their start and end apart: 58 -> 35, of which waited for: 20 -> 14; matrix products, arithmetic and copies ran while one was open for 4% -> 7% of each run, Pallas kernels for 7% -> 7%
where the time goes in v3:
time: 235 us; the launch traced here: 234 us
  waiting for transfers between devices  86.2 us (37%)
  starting transfers between devices  54.2 us (23%)
  blocking collectives  33.7 us (14%)
  Pallas kernels  30.8 us (13%)
  other arithmetic  16.9 us (7%)
  local copies, waits for them, and re-layouts  9.29 us (4%)
    ppermute x32, waiting for transfers between devices, permute(): return lax.ppermute(value, axis, ring(lax.axis_size(axis), step))  70.7 us
    ppermute x32, starting transfers between devices, permute(): return lax.ppermute(value, axis, ring(lax.axis_size(axis), step))  38.1 us
    all_to_all x1, blocking collectives, on_device(): came = lax.all_to_all(sent, AXES, split_axis=0, concat_axis=0, tiled=True)  33.7 us
    pallas_call x2, Pallas kernels, chip_sums(): pl.pallas_call(functools.partial(chip_kernel, layout, len(pieces), stores...  25.3 us
    all_to_all x1, waiting for transfers between devices, on_device(): lax.all_to_all(spread, AXES, split_axis=0, concat_axis=0, tiled=True)  9.95 us
    all_to_all x1, starting transfers between devices, grads_first(): return lax.all_to_all(grads, ('xl', 'xh', 'z', 'core'), 0, 0, tiled=True)  8.04 us
    convert_element_type x8, other arithmetic, add(): return total.astype(jnp.bfloat16)  7.89 us
    all_to_all x1, waiting for transfers between devices, grads_first(): return lax.all_to_all(grads, ('xl', 'xh', 'z', 'core'), 0, 0, tiled=True)  5.49 us
  transfers between devices with their start and end apart: 35, of which 14 were waited for; matrix products, arithmetic and copies ran while one was open for 7% of the time, Pallas kernels for 7%

profile of v3, /device:TPU:1, one launch (start us, length us, event | category | flops | bytes accessed | tf_op | source)
XLA Modules:
  0.0 234.3 jit_solution(15216151719772411645)
XLA Ops:
  5.3 2.7 %collective-permute-start.1 = (bf16[2048,256]{1,0:T(8,128)(2,1)}, bf16[2048,256]{1,0:T(8,128)(2,1)}, u32[]{:S(2)}, u32[]{:S(2)}) collective-permute-start(bf16[2048,256]{1,0:T(8,128)(2,1)} %refs_0_.3), channel_id=1, source_target_pairs={{0,48},{16,0},{32,16},{48,32},{1,49},{17,1},{33,17},{49,33},{2,50}... | collective-permute-start | bytes 3145736 | tf_op jit(solution)/shard_map/ppermute | solution.py:25
  10.3 18.7 %collective-permute-done.2.refs_2_.refs_3_ = bf16[2048,256]{1,0:T(8,128)(2,1)S(1)} collective-permute-done((bf16[2048,256]{1,0:T(8,128)(2,1)}, bf16[2048,256]{1,0:T(8,128)(2,1)S(1)}, u32[]{:S(2)}, u32[]{:S(2)}) %collective-permute-start.2) | collective-permute-done | bytes 1048608 | tf_op jit(solution)/shard_map/ppermute | solution.py:25
  30.5 3.1 %collective-permute-done.refs_0_.refs_1_ = bf16[2048,256]{1,0:T(8,128)(2,1)} collective-permute-done((bf16[2048,256]{1,0:T(8,128)(2,1)}, bf16[2048,256]{1,0:T(8,128)(2,1)}, u32[]{:S(2)}, u32[]{:S(2)}) %collective-permute-start) | collective-permute-done | bytes 1048608 | tf_op jit(solution)/shard_map/ppermute | solution.py:25
  33.6 3.4 %copy_rows.2 = (bf16[2304,256]{1,0:T(8,128)(2,1)}, bf16[2304,256]{1,0:T(8,128)(2,1)}, bf16[1536,256]{1,0:T(8,128)(2,1)}) custom-call(bf16[2048,256]{1,0:T(8,128)(2,1)} %collective-permute-done.refs_0_.refs_1_, bf16[2048,256]{1,0:T(8,128)(2,1)} %collective-permute-done.1.refs_1_.refs_2_, bf16[2048,256]{1,0:T(8,128)(2,1)} %copy-done.5), custom_call_target="tpu_custom_call" | custom-call | tf_op jit(solution)/shard_map/copy_rows/pallas_call | solution.py:147
  37.5 2.6 %collective-permute-start.6 = (bf16[2304,256]{1,0:T(8,128)(2,1)}, bf16[2304,256]{1,0:T(8,128)(2,1)S(1)}, u32[]{:S(2)}, u32[]{:S(2)}) collective-permute-start(bf16[2304,256]{1,0:T(8,128)(2,1)} %get-tuple-element.62), channel_id=1, source_target_pairs={{0,48},{16,0},{32,16},{48,32},{1,49},{17,1},{33,17},{49,33},{2,50}... | collective-permute-start | bytes 3538952 | tf_op jit(solution)/shard_map/ppermute | solution.py:25
  40.0 2.3 %collective-permute-start.11 = (bf16[2048,256]{1,0:T(8,128)(2,1)}, bf16[2048,256]{1,0:T(8,128)(2,1)}, u32[]{:S(2)}, u32[]{:S(2)}) collective-permute-start(bf16[2048,256]{1,0:T(8,128)(2,1)} %refs_0_.3), channel_id=1, source_target_pairs={{0,1},{1,0},{2,3},{3,2},{4,5},{5,4},{6,7},{7,6},{8,9},{9,8},{10,11... | collective-permute-start | bytes 3145736 | tf_op jit(solution)/shard_map/ppermute | solution.py:25
  44.7 8.0 %all-to-all-start = ((bf16[32,4,16,256]{3,2,1,0:T(8,128)(2,1)}), bf16[32,4,16,256]{3,2,1,0:T(8,128)(2,1)S(1)}, u32[]{:S(2)}, u32[]{:S(2)}) async-start(bf16[32,4,16,256]{3,2,1,0:T(8,128)(2,1)} %bitcast.13), calls=%async_computation | async-start | bytes 2097152 | tf_op jit(solution)/shard_map/all_to_all | solution.py:291
  55.0 3.8 %collective-permute-start.14 = (bf16[2048,256]{1,0:T(8,128)(2,1)}, bf16[2048,256]{1,0:T(8,128)(2,1)}, u32[]{:S(2)}, u32[]{:S(2)}) collective-permute-start(bf16[2048,256]{1,0:T(8,128)(2,1)} %copy-done.5), channel_id=1, source_target_pairs={{0,1},{1,0},{2,3},{3,2},{4,5},{5,4},{6,7},{7,6},{8,9},{9,8},{10,11... | collective-permute-start | bytes 3145736 | tf_op jit(solution)/shard_map/ppermute | solution.py:25
  58.9 5.6 %collective-permute-done.5.refs_0_.refs_4_ = bf16[2304,256]{1,0:T(8,128)(2,1)S(1)} collective-permute-done((bf16[2304,256]{1,0:T(8,128)(2,1)}, bf16[2304,256]{1,0:T(8,128)(2,1)S(1)}, u32[]{:S(2)}, u32[]{:S(2)}) %collective-permute-start.5) | collective-permute-done | bytes 1179680 | tf_op jit(solution)/shard_map/ppermute | solution.py:25
  64.5 2.4 %collective-permute-start.12 = (bf16[2048,256]{1,0:T(8,128)(2,1)}, bf16[2048,256]{1,0:T(8,128)(2,1)}, u32[]{:S(2)}, u32[]{:S(2)}) collective-permute-start(bf16[2048,256]{1,0:T(8,128)(2,1)} %collective-permute-done.refs_0_.refs_1_), channel_id=1, source_target_pairs={{0,1},{1,0},{2,3},{3,2},{4,5},{5,4},{6,7},{7,6},{8,9},{9,8},{10,11... | collective-permute-start | bytes 3145736 | tf_op jit(solution)/shard_map/ppermute | solution.py:25
  66.9 5.5 %all-to-all-done = bf16[32,4,16,256]{3,2,1,0:T(8,128)(2,1)S(1)} async-done(((bf16[32,4,16,256]{3,2,1,0:T(8,128)(2,1)}), bf16[32,4,16,256]{3,2,1,0:T(8,128)(2,1)S(1)}, u32[]{:S(2)}, u32[]{:S(2)}) %all-to-all-start) | async-done | bytes 1048608 | tf_op jit(solution)/shard_map/all_to_all | solution.py:291
  75.5 2.7 %collective-permute-start.9 = (bf16[640,256]{1,0:T(8,128)(2,1)}, bf16[640,256]{1,0:T(8,128)(2,1)}, u32[]{:S(2)}, u32[]{:S(2)}) collective-permute-start(bf16[640,256]{1,0:T(8,128)(2,1)} %get-tuple-element.69), channel_id=1, source_target_pairs={{0,48},{16,0},{32,16},{48,32},{1,49},{17,1},{33,17},{49,33},{2,50}... | collective-permute-start | bytes 983048 | tf_op jit(solution)/shard_map/ppermute | solution.py:25
  78.5 7.7 %collective-permute-done.8.refs_7_ = bf16[640,256]{1,0:T(8,128)(2,1)} collective-permute-done((bf16[640,256]{1,0:T(8,128)(2,1)}, bf16[640,256]{1,0:T(8,128)(2,1)}, u32[]{:S(2)}, u32[]{:S(2)}) %collective-permute-start.8) | collective-permute-done | bytes 327712 | tf_op jit(solution)/shard_map/ppermute | solution.py:25
  92.6 10.4 %chip_sums.2 = (bf16[2,4,128,256]{3,2,1,0:T(8,128)(2,1)}, bf16[2,5,128,256]{3,2,1,0:T(8,128)(2,1)}, bf16[1,7,128,256]{3,2,1,0:T(8,128)(2,1)}, bf16[1,7,128,256]{3,2,1,0:T(8,128)(2,1)}) custom-call(s32[2,3,128]{2,1,0:T(4,128)} %pad_add_fusion.tables, s32[2]{0:T(128)} %pad_add_fusion.1.owners, s32[1]{0:T(128)} %bitcast.10.core, ...), custom_call_target="tpu_custom_call" | custom-call | flops 10000000000 | bytes 1024 | tf_op jit(solution)/shard_map/chip_sums/pallas_call | solution.py:93
  106.6 14.9 %chip_sums.3 = (bf16[2,9,128,256]{3,2,1,0:T(8,128)(2,1)}, bf16[2,9,128,256]{3,2,1,0:T(8,128)(2,1)}, bf16[2,9,128,256]{3,2,1,0:T(8,128)(2,1)}, bf16[3,7,128,256]{3,2,1,0:T(8,128)(2,1)}, bf16[3,7,128,256]{3,2,1,0:T(8,128)(2,1)}) custom-call(s32[2,3,128]{2,1,0:T(4,128)} %pad_add_fusion.tables, s32[6]{0:T(128)} %stack.60.owners, s32[1]{0:T(128)} %bitcast.10.core, ...), custom_call_target="tpu_custom_call" | custom-call | flops 17999998976 | bytes 1024 | tf_op jit(solution)/shard_map/chip_sums/pallas_call | solution.py:93
  129.9 2.7 %collective-permute-start.28 = (bf16[4,128,256]{2,1,0:T(8,128)(2,1)S(1)}, bf16[4,128,256]{2,1,0:T(8,128)(2,1)S(1)}, u32[]{:S(2)}, u32[]{:S(2)}) collective-permute-start(bf16[4,128,256]{2,1,0:T(8,128)(2,1)S(1)} %fusion.11), channel_id=1, source_target_pairs={{0,6},{2,0},{4,2},{6,4},{1,7},{3,1},{5,3},{7,5},{8,14},{10,8},{12,... | collective-permute-start | bytes 786440 | tf_op jit(solution)/shard_map/ppermute | solution.py:25
  134.5 3.5 %all-to-all-start.1 = ((bf16[4,32,16,256]{3,2,1,0:T(8,128)(2,1)}), bf16[4,32,16,256]{3,2,1,0:T(8,128)(2,1)S(1)}, u32[]{:S(2)}, u32[]{:S(2)}) async-start(bf16[4,32,16,256]{3,2,1,0:T(8,128)(2,1)} %copy.15), calls=%async_computation.1 | async-start | bytes 2097152 | tf_op jit(solution)/shard_map/all_to_all | solution.py:295
  138.0 22.9 %collective-permute-done.27 = bf16[3,128,256]{2,1,0:T(8,128)(2,1)S(1)} collective-permute-done((bf16[3,128,256]{2,1,0:T(8,128)(2,1)}, bf16[3,128,256]{2,1,0:T(8,128)(2,1)S(1)}, u32[]{:S(2)}, u32[]{:S(2)}) %collective-permute-start.27) | collective-permute-done | bytes 196640 | tf_op jit(solution)/shard_map/ppermute | solution.py:25
  161.6 2.5 %fusion.6 = bf16[9,128,256]{2,1,0:T(8,128)(2,1)} fusion(bf16[2,9,128,256]{3,2,1,0:T(8,128)(2,1)} %collective-permute-done.25, bf16[2,9,128,256]{3,2,1,0:T(8,128)(2,1)} %collective-permute-done.24, bf16[2,9,128,256]{3,2,1,0:T(8,128)(2,1)} %get-tuple-element.79), kind=kLoop, calls=%fused_computation.21 | loop fusion | flops 1769472 | bytes 2359296 | tf_op jit(solution)/shard_map/convert_element_type | solution.py:216
  168.1 2.7 %collective-permute-start.31 = (bf16[7,128,256]{2,1,0:T(8,128)(2,1)}, bf16[7,128,256]{2,1,0:T(8,128)(2,1)}, u32[]{:S(2)}, u32[]{:S(2)}) collective-permute-start(bf16[7,128,256]{2,1,0:T(8,128)(2,1)} %pad_maximum_fusion.4), channel_id=1, source_target_pairs={{0,6},{2,0},{4,2},{6,4},{1,7},{3,1},{5,3},{7,5},{8,14},{10,8},{12,... | collective-permute-start | bytes 1376264 | tf_op jit(solution)/shard_map/ppermute | solution.py:25
  171.2 6.3 %collective-permute-done.30 = bf16[7,128,256]{2,1,0:T(8,128)(2,1)} collective-permute-done((bf16[7,128,256]{2,1,0:T(8,128)(2,1)}, bf16[7,128,256]{2,1,0:T(8,128)(2,1)}, u32[]{:S(2)}, u32[]{:S(2)}) %collective-permute-start.30) | collective-permute-done | bytes 458784 | tf_op jit(solution)/shard_map/ppermute | solution.py:25
  183.0 33.7 %all_to_all.20 = bf16[128,40,128]{2,1,0:T(8,128)(2,1)S(1)} all-to-all(bf16[128,40,128]{2,1,0:T(8,128)(2,1)S(1)} %pad_maximum_fusion), channel_id=1, replica_groups=mesh['xl'=2,'y'=4,'xh'=2,'z'=4,'core'=2] {'xl','y','xh','z','core'}, dimensions={0} | all-to-all | bytes 2621440 | tf_op jit(solution)/shard_map/all_to_all | solution.py:319
  217.7 4.5 %all-to-all-start.3 = ((f32[128,2,256]{2,1,0:T(2,128)}), f32[128,2,256]{2,1,0:T(2,128)S(1)}, u32[]{:S(2)}, u32[]{:S(2)}) async-start(f32[128,2,256]{2,1,0:T(2,128)} %broadcast_in_dim.2), calls=%async_computation.3 | async-start | bytes 524288 | tf_op jit(solution)/shard_map/all_to_all | solution.py:328
  223.5 9.9 %all-to-all-done.3 = f32[128,2,256]{2,1,0:T(2,128)S(1)} async-done(((f32[128,2,256]{2,1,0:T(2,128)}), f32[128,2,256]{2,1,0:T(2,128)S(1)}, u32[]{:S(2)}, u32[]{:S(2)}) %all-to-all-start.3) | async-done | bytes 262176 | tf_op jit(solution)/shard_map/all_to_all | solution.py:328
  (115 shorter events, 49.9 us)
Async XLA Ops:
  2.4 31.1 %collective-permute-start.4 = (bf16[8,8,128,128]{3,2,1,0:T(8,128)(2,1)S(1)}, bf16[8,8,128,128]{3,2,1,0:T(8,128)(2,1)}, u32[]{:S(2)}, u32[]{:S(2)}) collective-permute-start(bf16[8,8,128,128]{3,2,1,0:T(8,128)(2,1)S(1)} %dynamic-slice_bitcast_fusion), channel_id=1, source_target_pairs={{0,1},{1,0},{2,3},{3,2},{4,5},{5,4},{6,7},{7,6},{8,9},{9,8},{10,11... | collective-permute-start | bytes 6291464 | tf_op jit(solution)/shard_map/ppermute | solution.py:25
  4.0 25.0 %collective-permute-start.2 = (bf16[2048,256]{1,0:T(8,128)(2,1)}, bf16[2048,256]{1,0:T(8,128)(2,1)S(1)}, u32[]{:S(2)}, u32[]{:S(2)}) collective-permute-start(bf16[2048,256]{1,0:T(8,128)(2,1)} %refs_0_.3), channel_id=1, source_target_pairs={{0,64},{64,0},{1,65},{65,1},{2,66},{66,2},{3,67},{67,3},{4,68},{68... | collective-permute-start | bytes 3145736 | tf_op jit(solution)/shard_map/ppermute | solution.py:25
  5.3 25.2 %collective-permute-start.1 = (bf16[2048,256]{1,0:T(8,128)(2,1)}, bf16[2048,256]{1,0:T(8,128)(2,1)}, u32[]{:S(2)}, u32[]{:S(2)}) collective-permute-start(bf16[2048,256]{1,0:T(8,128)(2,1)} %refs_0_.3), channel_id=1, source_target_pairs={{0,48},{16,0},{32,16},{48,32},{1,49},{17,1},{33,17},{49,33},{2,50}... | collective-permute-start | bytes 3145736 | tf_op jit(solution)/shard_map/ppermute | solution.py:25
  8.0 25.6 %collective-permute-start = (bf16[2048,256]{1,0:T(8,128)(2,1)}, bf16[2048,256]{1,0:T(8,128)(2,1)}, u32[]{:S(2)}, u32[]{:S(2)}) collective-permute-start(bf16[2048,256]{1,0:T(8,128)(2,1)} %refs_0_.3), channel_id=1, source_target_pairs={{0,16},{16,32},{32,48},{48,0},{1,17},{17,33},{33,49},{49,1},{2,18}... | collective-permute-start | bytes 3145736 | tf_op jit(solution)/shard_map/ppermute | solution.py:25
  37.0 27.4 %collective-permute-start.5 = (bf16[2304,256]{1,0:T(8,128)(2,1)}, bf16[2304,256]{1,0:T(8,128)(2,1)S(1)}, u32[]{:S(2)}, u32[]{:S(2)}) collective-permute-start(bf16[2304,256]{1,0:T(8,128)(2,1)} %get-tuple-element.61), channel_id=1, source_target_pairs={{0,16},{16,32},{32,48},{48,0},{1,17},{17,33},{33,49},{49,1},{2,18}... | collective-permute-start | bytes 3538952 | tf_op jit(solution)/shard_map/ppermute | solution.py:25
  37.1 17.9 %collective-permute-start.7 = (bf16[1536,256]{1,0:T(8,128)(2,1)}, bf16[1536,256]{1,0:T(8,128)(2,1)}, u32[]{:S(2)}, u32[]{:S(2)}) collective-permute-start(bf16[1536,256]{1,0:T(8,128)(2,1)} %get-tuple-element.63), channel_id=1, source_target_pairs={{0,64},{64,0},{1,65},{65,1},{2,66},{66,2},{3,67},{67,3},{4,68},{68... | collective-permute-start | bytes 2359304 | tf_op jit(solution)/shard_map/ppermute | solution.py:25
  37.5 35.0 %collective-permute-start.6 = (bf16[2304,256]{1,0:T(8,128)(2,1)}, bf16[2304,256]{1,0:T(8,128)(2,1)S(1)}, u32[]{:S(2)}, u32[]{:S(2)}) collective-permute-start(bf16[2304,256]{1,0:T(8,128)(2,1)} %get-tuple-element.62), channel_id=1, source_target_pairs={{0,48},{16,0},{32,16},{48,32},{1,49},{17,1},{33,17},{49,33},{2,50}... | collective-permute-start | bytes 3538952 | tf_op jit(solution)/shard_map/ppermute | solution.py:25
  40.0 32.5 %collective-permute-start.11 = (bf16[2048,256]{1,0:T(8,128)(2,1)}, bf16[2048,256]{1,0:T(8,128)(2,1)}, u32[]{:S(2)}, u32[]{:S(2)}) collective-permute-start(bf16[2048,256]{1,0:T(8,128)(2,1)} %refs_0_.3), channel_id=1, source_target_pairs={{0,1},{1,0},{2,3},{3,2},{4,5},{5,4},{6,7},{7,6},{8,9},{9,8},{10,11... | collective-permute-start | bytes 3145736 | tf_op jit(solution)/shard_map/ppermute | solution.py:25
  44.7 27.7 %all-to-all-start = ((bf16[32,4,16,256]{3,2,1,0:T(8,128)(2,1)}), bf16[32,4,16,256]{3,2,1,0:T(8,128)(2,1)S(1)}, u32[]{:S(2)}, u32[]{:S(2)}) async-start(bf16[32,4,16,256]{3,2,1,0:T(8,128)(2,1)} %bitcast.13), calls=%async_computation | async-start | bytes 2097152 | tf_op jit(solution)/shard_map/all_to_all | solution.py:291
  52.8 22.7 %collective-permute-start.13 = (bf16[2048,256]{1,0:T(8,128)(2,1)}, bf16[2048,256]{1,0:T(8,128)(2,1)}, u32[]{:S(2)}, u32[]{:S(2)}) collective-permute-start(bf16[2048,256]{1,0:T(8,128)(2,1)} %collective-permute-done.1.refs_1_.refs_2_), channel_id=1, source_target_pairs={{0,1},{1,0},{2,3},{3,2},{4,5},{5,4},{6,7},{7,6},{8,9},{9,8},{10,11... | collective-permute-start | bytes 3145736 | tf_op jit(solution)/shard_map/ppermute | solution.py:25
  55.0 20.5 %collective-permute-start.14 = (bf16[2048,256]{1,0:T(8,128)(2,1)}, bf16[2048,256]{1,0:T(8,128)(2,1)}, u32[]{:S(2)}, u32[]{:S(2)}) collective-permute-start(bf16[2048,256]{1,0:T(8,128)(2,1)} %copy-done.5), channel_id=1, source_target_pairs={{0,1},{1,0},{2,3},{3,2},{4,5},{5,4},{6,7},{7,6},{8,9},{9,8},{10,11... | collective-permute-start | bytes 3145736 | tf_op jit(solution)/shard_map/ppermute | solution.py:25
  64.5 13.7 %collective-permute-start.12 = (bf16[2048,256]{1,0:T(8,128)(2,1)}, bf16[2048,256]{1,0:T(8,128)(2,1)}, u32[]{:S(2)}, u32[]{:S(2)}) collective-permute-start(bf16[2048,256]{1,0:T(8,128)(2,1)} %collective-permute-done.refs_0_.refs_1_), channel_id=1, source_target_pairs={{0,1},{1,0},{2,3},{3,2},{4,5},{5,4},{6,7},{7,6},{8,9},{9,8},{10,11... | collective-permute-start | bytes 3145736 | tf_op jit(solution)/shard_map/ppermute | solution.py:25
  72.4 20.2 %collective-permute-start.15 = (bf16[2304,256]{1,0:T(8,128)(2,1)S(1)}, bf16[2304,256]{1,0:T(8,128)(2,1)}, u32[]{:S(2)}, u32[]{:S(2)}) collective-permute-start(bf16[2304,256]{1,0:T(8,128)(2,1)S(1)} %collective-permute-done.5.refs_0_.refs_4_), channel_id=1, source_target_pairs={{0,1},{1,0},{2,3},{3,2},{4,5},{5,4},{6,7},{7,6},{8,9},{9,8},{10,11... | collective-permute-start | bytes 3538952 | tf_op jit(solution)/shard_map/ppermute | solution.py:25
  72.6 20.1 %collective-permute-start.16 = (bf16[2304,256]{1,0:T(8,128)(2,1)S(1)}, bf16[2304,256]{1,0:T(8,128)(2,1)}, u32[]{:S(2)}, u32[]{:S(2)}) collective-permute-start(bf16[2304,256]{1,0:T(8,128)(2,1)S(1)} %collective-permute-done.6.refs_1_.refs_5_), channel_id=1, source_target_pairs={{0,1},{1,0},{2,3},{3,2},{4,5},{5,4},{6,7},{7,6},{8,9},{9,8},{10,11... | collective-permute-start | bytes 3538952 | tf_op jit(solution)/shard_map/ppermute | solution.py:25
  103.1 18.4 %collective-permute-start.23 = (bf16[1,7,128,256]{3,2,1,0:T(8,128)(2,1)}, bf16[1,7,128,256]{3,2,1,0:T(8,128)(2,1)S(1)}, u32[]{:S(2)}, u32[]{:S(2)}) collective-permute-start(bf16[1,7,128,256]{3,2,1,0:T(8,128)(2,1)} %get-tuple-element.73), channel_id=1, source_target_pairs={{0,8},{8,0},{1,9},{9,1},{2,10},{10,2},{3,11},{11,3},{4,12},{12,4},... | collective-permute-start | bytes 1376264 | tf_op jit(solution)/shard_map/ppermute | solution.py:25
  103.9 17.6 %collective-permute-start.21 = (bf16[2,4,128,256]{3,2,1,0:T(8,128)(2,1)}, bf16[2,4,128,256]{3,2,1,0:T(8,128)(2,1)S(1)}, u32[]{:S(2)}, u32[]{:S(2)}) collective-permute-start(bf16[2,4,128,256]{3,2,1,0:T(8,128)(2,1)} %get-tuple-element.71), channel_id=1, source_target_pairs={{0,2},{2,4},{4,6},{6,0},{1,3},{3,5},{5,7},{7,1},{8,10},{10,12},{12... | collective-permute-start | bytes 1572872 | tf_op jit(solution)/shard_map/ppermute | solution.py:25
  104.5 17.1 %collective-permute-start.22 = (bf16[2,5,128,256]{3,2,1,0:T(8,128)(2,1)}, bf16[2,5,128,256]{3,2,1,0:T(8,128)(2,1)S(1)}, u32[]{:S(2)}, u32[]{:S(2)}) collective-permute-start(bf16[2,5,128,256]{3,2,1,0:T(8,128)(2,1)} %get-tuple-element.72), channel_id=1, source_target_pairs={{0,6},{2,0},{4,2},{6,4},{1,7},{3,1},{5,3},{7,5},{8,14},{10,8},{12,... | collective-permute-start | bytes 1966088 | tf_op jit(solution)/shard_map/ppermute | solution.py:25
  123.7 37.2 %collective-permute-start.25 = (bf16[2,9,128,256]{3,2,1,0:T(8,128)(2,1)}, bf16[2,9,128,256]{3,2,1,0:T(8,128)(2,1)}, u32[]{:S(2)}, u32[]{:S(2)}) collective-permute-start(bf16[2,9,128,256]{3,2,1,0:T(8,128)(2,1)} %fusion.5), channel_id=1, source_target_pairs={{0,6},{2,0},{4,2},{6,4},{1,7},{3,1},{5,3},{7,5},{8,14},{10,8},{12,... | collective-permute-start | bytes 3538952 | tf_op jit(solution)/shard_map/ppermute | solution.py:25
  125.7 35.3 %collective-permute-start.26 = (bf16[3,7,128,256]{3,2,1,0:T(8,128)(2,1)}, bf16[3,7,128,256]{3,2,1,0:T(8,128)(2,1)}, u32[]{:S(2)}, u32[]{:S(2)}) collective-permute-start(bf16[3,7,128,256]{3,2,1,0:T(8,128)(2,1)} %get-tuple-element.84), channel_id=1, source_target_pairs={{0,8},{8,0},{1,9},{9,1},{2,10},{10,2},{3,11},{11,3},{4,12},{12,4},... | collective-permute-start | bytes 4128776 | tf_op jit(solution)/shard_map/ppermute | solution.py:25
  129.9 31.1 %collective-permute-start.24 = (bf16[2,9,128,256]{3,2,1,0:T(8,128)(2,1)}, bf16[2,9,128,256]{3,2,1,0:T(8,128)(2,1)}, u32[]{:S(2)}, u32[]{:S(2)}) collective-permute-start(bf16[2,9,128,256]{3,2,1,0:T(8,128)(2,1)} %fusion.7), channel_id=1, source_target_pairs={{0,2},{2,4},{4,6},{6,0},{1,3},{3,5},{5,7},{7,1},{8,10},{10,12},{12... | collective-permute-start | bytes 3538952 | tf_op jit(solution)/shard_map/ppermute | solution.py:25
  129.9 31.0 %collective-permute-start.28 = (bf16[4,128,256]{2,1,0:T(8,128)(2,1)S(1)}, bf16[4,128,256]{2,1,0:T(8,128)(2,1)S(1)}, u32[]{:S(2)}, u32[]{:S(2)}) collective-permute-start(bf16[4,128,256]{2,1,0:T(8,128)(2,1)S(1)} %fusion.11), channel_id=1, source_target_pairs={{0,6},{2,0},{4,2},{6,4},{1,7},{3,1},{5,3},{7,5},{8,14},{10,8},{12,... | collective-permute-start | bytes 786440 | tf_op jit(solution)/shard_map/ppermute | solution.py:25
  133.4 27.5 %collective-permute-start.27 = (bf16[3,128,256]{2,1,0:T(8,128)(2,1)}, bf16[3,128,256]{2,1,0:T(8,128)(2,1)S(1)}, u32[]{:S(2)}, u32[]{:S(2)}) collective-permute-start(bf16[3,128,256]{2,1,0:T(8,128)(2,1)} %fusion.13), channel_id=1, source_target_pairs={{0,2},{2,4},{4,6},{6,0},{1,3},{3,5},{5,7},{7,1},{8,10},{10,12},{12... | collective-permute-start | bytes 589832 | tf_op jit(solution)/shard_map/ppermute | solution.py:25
  134.5 36.3 %all-to-all-start.1 = ((bf16[4,32,16,256]{3,2,1,0:T(8,128)(2,1)}), bf16[4,32,16,256]{3,2,1,0:T(8,128)(2,1)S(1)}, u32[]{:S(2)}, u32[]{:S(2)}) async-start(bf16[4,32,16,256]{3,2,1,0:T(8,128)(2,1)} %copy.15), calls=%async_computation.1 | async-start | bytes 2097152 | tf_op jit(solution)/shard_map/all_to_all | solution.py:295
  217.7 15.7 %all-to-all-start.3 = ((f32[128,2,256]{2,1,0:T(2,128)}), f32[128,2,256]{2,1,0:T(2,128)S(1)}, u32[]{:S(2)}, u32[]{:S(2)}) async-start(f32[128,2,256]{2,1,0:T(2,128)} %broadcast_in_dim.2), calls=%async_computation.3 | async-start | bytes 524288 | tf_op jit(solution)/shard_map/all_to_all | solution.py:328
  (22 other events, 338.6 us)

commit v4 on v3

--- a/solution.py
+++ b/solution.py
@@ -10,7 +10,7 @@
 BS = 128
 WIDTH = 256
 OWNER_BLOCKS = 16
-LOW = 9
+LOW = 8
 SIDE_FIRST = 10
 TURNS = 8
 PEERS = 8
@@ -25,15 +25,13 @@
     return lax.ppermute(value, axis, ring(lax.axis_size(axis), step))
 
 
-def load_slab(layout, pieces, slab, sems):
-    copies = []
-    for n, (piece, start, rows, place) in enumerate(layout):
-        source = pieces[piece].at[pl.ds(start, rows)]
-        copy = pltpu.make_async_copy(source, slab.at[pl.ds(place, rows)], sems.at[n])
-        copy.start()
-        copies.append(copy)
-    for copy in copies:
-        copy.wait()
+def slab_copies(layout, pieces, slab, sems):
+    return [
+        pltpu.make_async_copy(
+            pieces[piece].at[pl.ds(start, rows)], slab.at[pl.ds(place, rows)], sems.at[n]
+        )
+        for n, (piece, start, rows, place) in enumerate(layout)
+    ]
 
 
 def chip_kernel(
@@ -44,7 +42,10 @@
 
     @pl.when(step == 0)
     def _():
-        load_slab(layout, pieces, slab, sems)
+        for copy in slab_copies(layout, pieces, slab, sems):
+            copy.start()
+        for copy in slab_copies(layout, pieces, slab, sems)[: len(layout) // 2]:
+            copy.wait()
 
     sums[...] = jnp.zeros_like(sums)
 
@@ -56,6 +57,12 @@
     slots = [turn * 16 + owners[step] * 2 + core[0] for turn in range(TURNS)]
     for turn, slot in enumerate(slots):
         sums[tables[0, 1, slot]] = product(0, slot, adj_ref[turn, 0, 0])
+
+    @pl.when(step == 0)
+    def _():
+        for copy in slab_copies(layout, pieces, slab, sems)[len(layout) // 2 :]:
+            copy.wait()
+
     for turn, slot in enumerate(slots):
         row = tables[1, 1, slot]
         term = product(1, slot, other_adj_ref[turn, 0]).astype(jnp.float32)
@@ -209,6 +216,46 @@
     return layout, pieces, shared, others
 
 
+def add_via_kernel(up_in, down_in, via_a, via_b, up, down, *refs):
+    part = via_a.shape[1]
+    held, (sems,) = refs[:-1], refs[-1:]
+    targets = up.at[:, pl.ds(0, part)], down.at[:, pl.ds(part, via_b.shape[1])]
+    sources = up_in.at[:, pl.ds(0, part)], down_in.at[:, pl.ds(part, via_b.shape[1])]
+    loads = [
+        pltpu.make_async_copy(source, buffer, sems.at[n])
+        for n, (source, buffer) in enumerate(zip((*sources, via_a, via_b), held))
+    ]
+    for load in loads:
+        load.start()
+    stores = []
+    for n in range(2):
+        loads[n].wait()
+        loads[n + 2].wait()
+        total = held[n][...].astype(jnp.float32) + held[n + 2][...].astype(jnp.float32)
+        held[n][...] = total.astype(jnp.bfloat16)
+        stores.append(pltpu.make_async_copy(held[n], targets[n], sems.at[4 + n]))
+        stores[n].start()
+    for store in stores:
+        store.wait()
+
+
+def add_via(up, down, via_a, via_b):
+    any_spec = pl.BlockSpec(memory_space=pl.ANY)
+    return pl.pallas_call(
+        add_via_kernel,
+        out_shape=[jax.ShapeDtypeStruct(x.shape, x.dtype) for x in (up, down)],
+        in_specs=[any_spec] * 4,
+        out_specs=[any_spec] * 2,
+        scratch_shapes=[
+            *[pltpu.VMEM(x.shape, x.dtype) for x in (via_a, via_b, via_a, via_b)],
+            pltpu.SemaphoreType.DMA((6,)),
+        ],
+        input_output_aliases={0: 0, 1: 1},
+        compiler_params=pltpu.CompilerParams(vmem_limit_bytes=60 * 1024 * 1024),
+        name="add_via",
+    )(up, down, via_a, via_b)
+
+
 def add(*terms):
     total = terms[0].astype(jnp.float32)
     for term in terms[1:]:
@@ -216,32 +263,41 @@
     return total.astype(jnp.bfloat16)
 
 
-def reduce_to_owner(far, near):
+def reduce_to_owner(far, near, others):
     far_a, far_b, keep, give = far
     via_a = permute(far_a, "z", 1)
     via_b = permute(far_b, "z", -1)
     came = permute(give, "xh", 1)
     via_a, via_b, came, near = together(via_a, via_b, came, near)
     cut = came.shape[1] // 2
-    high_a = permute(add(keep[0, :cut], came[0, :cut]), "z", 1)
-    high_b = permute(add(keep[0, cut:], came[0, cut:]), "z", -1)
+    high_a, high_b = add(keep[0, :cut], came[0, :cut]), add(keep[0, cut:], came[0, cut:])
+    sums = high_a, high_b
+    high_a, high_b = permute(high_a, "z", 1), permute(high_b, "z", -1)
     up, down, own, keep, give = near
-    part = via_a.shape[1]
-    up = lax.dynamic_update_slice(up, add(up[:, :part], via_a), (0, 0, 0, 0))
-    down = lax.dynamic_update_slice(down, add(down[:, part:], via_b), (0, part, 0, 0))
+    up, down = add_via(up, down, via_a, via_b)
+    others = others((up, sums))
     came = permute(give, "xh", 1)
     up, down, came, high_a, high_b = together(
         permute(up, "z", 1), permute(down, "z", -1), came, high_a, high_b
     )
-    low_side = permute(add(own[1], up[1], down[1]), "xh", 1)
-    high = [add(keep[n], came[n]) for n in range(2)]
-    high_up = jnp.concatenate([add(high[0][:cut], high_a), high[0][cut:]])
-    high_down = jnp.concatenate([high[1][:cut], add(high[1][cut:], high_b)])
-    low_side, high_up, high_down = together(
-        low_side, permute(high_up, "z", 1), permute(high_down, "z", -1)
-    )
-    high = add(keep[2], came[2], high_up, high_down)
-    return jnp.concatenate([add(own[0], up[0], down[0], low_side), high]).reshape(-1, WIDTH)
+    low = add(own[1], up[1], down[1])
+    low_side = permute(low, "xh", 1)
+    (keep, came), _ = lax.optimization_barrier(((keep, came), low))
+    rest = came.shape[1] - cut
+    high_up = add(keep[0], came[0], jnp.pad(high_a, ((0, rest), (0, 0), (0, 0))))
+    high_down = add(keep[1], came[1], jnp.pad(high_b, ((cut, 0), (0, 0), (0, 0))))
+    (own, up, down, keep, came), _ = lax.optimization_barrier(
+        ((own, up, down, keep, came), (high_up, high_down))
+    )
+    low_side, high_up, high_down, low, high = together(
+        low_side,
+        permute(high_up, "z", 1),
+        permute(high_down, "z", -1),
+        add(own[0], up[0], down[0]),
+        add(keep[2], came[2]),
+    )
+    high = add(high, high_up, high_down)
+    return jnp.concatenate([add(low, low_side), high]).reshape(-1, WIDTH), others
 
 
 def derivative(preact, grad_rows):
@@ -304,8 +360,7 @@
     far = products((layout, pieces), (2,))
 
     near = products((layout, pieces), (1, 3, 0))
-    agg = reduce_to_owner(far, near)
-    grad_row = grads_last(grads, near)
+    agg, grad_row = reduce_to_owner(far, near, functools.partial(grads_last, grads))
 
     preact = jnp.dot(agg, weight, preferred_element_type=jnp.float32)
     out_row = jax.nn.silu(preact).astype(jnp.bfloat16)

time: 235 us -> 231 us (0.983)
  other arithmetic: 16.9 us -> 7.78 us
  waiting for transfers between devices: 86.2 us -> 93.6 us
  Pallas kernels: 30.8 us -> 33.6 us
  starting transfers between devices: 54.2 us -> 51.5 us
  blocking collectives: 33.7 us -> 31.1 us
    all_to_all x1, waiting for transfers between devices: 0.01 us -> 10.6 us  [grads_last(): grads = lax.all_to_all(grads, 'y', 0, 0, tiled=True)]
    dynamic_update_slice x2 -> x0, other arithmetic: 4.15 us -> none  [the longest x1 2.19 us: reduce_to_owner(): lax.dynamic_update_slice(down, add(down[:, part:], via_b), (0, part, 0, 0))]
    convert_element_type x8 -> x7, other arithmetic: 7.89 us -> 4.55 us  [add(): return total.astype(jnp.bfloat16)]
    ppermute x32, waiting for transfers between devices: 70.7 us -> 67.6 us  [permute(): return lax.ppermute(value, axis, ring(lax.axis_size(axis), step))]
    ppermute x32, starting transfers between devices: 38.1 us -> 35.5 us  [permute(): return lax.ppermute(value, axis, ring(lax.axis_size(axis), step))]
    all_to_all x1, blocking collectives: 33.7 us -> 31.1 us  [on_device(): came = lax.all_to_all(sent, AXES, split_axis=0, concat_axis=0, tiled=True)]
    pallas_call x0 -> x1, Pallas kernels: none -> 2.51 us  [add_via(): pl.pallas_call(add_via_kernel, out_shape=[jax.ShapeDtypeStruct(x.shape, x...]
  transfers between devices with their start and end apart: 35 -> 35, of which waited for: 14 -> 17; matrix products, arithmetic and copies ran while one was open for 7% -> 4% of each run, Pallas kernels for 7% -> 9%
where the time goes in v4:
time: 231 us
  waiting for transfers between devices  93.6 us (41%)
  starting transfers between devices  51.5 us (22%)
  Pallas kernels  33.6 us (15%)
  blocking collectives  31.1 us (13%)
  local copies, waits for them, and re-layouts  9.63 us (4%)
  other arithmetic  7.78 us (3%)
    ppermute x32, waiting for transfers between devices, permute(): return lax.ppermute(value, axis, ring(lax.axis_size(axis), step))  67.6 us
    ppermute x32, starting transfers between devices, permute(): return lax.ppermute(value, axis, ring(lax.axis_size(axis), step))  35.5 us
    all_to_all x1, blocking collectives, on_device(): came = lax.all_to_all(sent, AXES, split_axis=0, concat_axis=0, tiled=True)  31.1 us
    pallas_call x2, Pallas kernels, chip_sums(): pl.pallas_call(functools.partial(chip_kernel, layout, len(pieces), stores...  25.6 us
    all_to_all x1, waiting for transfers between devices, grads_last(): grads = lax.all_to_all(grads, 'y', 0, 0, tiled=True)  10.6 us
    all_to_all x1, waiting for transfers between devices, on_device(): lax.all_to_all(spread, AXES, split_axis=0, concat_axis=0, tiled=True)  9.94 us
    all_to_all x1, starting transfers between devices, grads_first(): return lax.all_to_all(grads, ('xl', 'xh', 'z', 'core'), 0, 0, tiled=True)  8.04 us
    pallas_call x2, Pallas kernels, copy_rows(): pl.pallas_call(functools.partial(copy_rows_kernel, plans, len(sources)),...  5.5 us
  transfers between devices with their start and end apart: 35, of which 17 were waited for; matrix products, arithmetic and copies ran while one was open for 4% of the time, Pallas kernels for 9%

profile of v4, /device:TPU:1, one launch (start us, length us, event | category | flops | bytes accessed | tf_op | source)
XLA Modules:
  0.0 230.6 jit_solution(15764488454829995890)
XLA Ops:
  5.3 2.7 %collective-permute-start.1 = (bf16[2048,256]{1,0:T(8,128)(2,1)}, bf16[2048,256]{1,0:T(8,128)(2,1)}, u32[]{:S(2)}, u32[]{:S(2)}) collective-permute-start(bf16[2048,256]{1,0:T(8,128)(2,1)} %refs_0_.3), channel_id=1, source_target_pairs={{0,48},{16,0},{32,16},{48,32},{1,49},{17,1},{33,17},{49,33},{2,50}... | collective-permute-start | bytes 3145736 | tf_op jit(solution)/shard_map/ppermute | solution.py:25
  10.3 18.7 %collective-permute-done.2.refs_2_.refs_3_ = bf16[2048,256]{1,0:T(8,128)(2,1)S(1)} collective-permute-done((bf16[2048,256]{1,0:T(8,128)(2,1)}, bf16[2048,256]{1,0:T(8,128)(2,1)S(1)}, u32[]{:S(2)}, u32[]{:S(2)}) %collective-permute-start.2) | collective-permute-done | bytes 1048608 | tf_op jit(solution)/shard_map/ppermute | solution.py:25
  30.5 3.1 %collective-permute-done.refs_0_.refs_1_ = bf16[2048,256]{1,0:T(8,128)(2,1)} collective-permute-done((bf16[2048,256]{1,0:T(8,128)(2,1)}, bf16[2048,256]{1,0:T(8,128)(2,1)}, u32[]{:S(2)}, u32[]{:S(2)}) %collective-permute-start) | collective-permute-done | bytes 1048608 | tf_op jit(solution)/shard_map/ppermute | solution.py:25
  33.6 3.5 %copy_rows.2 = (bf16[2304,256]{1,0:T(8,128)(2,1)}, bf16[2304,256]{1,0:T(8,128)(2,1)}, bf16[1536,256]{1,0:T(8,128)(2,1)}) custom-call(bf16[2048,256]{1,0:T(8,128)(2,1)} %collective-permute-done.refs_0_.refs_1_, bf16[2048,256]{1,0:T(8,128)(2,1)} %collective-permute-done.1.refs_1_.refs_2_, bf16[2048,256]{1,0:T(8,128)(2,1)} %copy-done.4), custom_call_target="tpu_custom_call" | custom-call | tf_op jit(solution)/shard_map/copy_rows/pallas_call | solution.py:154
  37.5 2.6 %collective-permute-start.6 = (bf16[2304,256]{1,0:T(8,128)(2,1)}, bf16[2304,256]{1,0:T(8,128)(2,1)S(1)}, u32[]{:S(2)}, u32[]{:S(2)}) collective-permute-start(bf16[2304,256]{1,0:T(8,128)(2,1)} %get-tuple-element.73), channel_id=1, source_target_pairs={{0,48},{16,0},{32,16},{48,32},{1,49},{17,1},{33,17},{49,33},{2,50}... | collective-permute-start | bytes 3538952 | tf_op jit(solution)/shard_map/ppermute | solution.py:25
  40.1 2.3 %collective-permute-start.11 = (bf16[2048,256]{1,0:T(8,128)(2,1)}, bf16[2048,256]{1,0:T(8,128)(2,1)}, u32[]{:S(2)}, u32[]{:S(2)}) collective-permute-start(bf16[2048,256]{1,0:T(8,128)(2,1)} %refs_0_.3), channel_id=1, source_target_pairs={{0,1},{1,0},{2,3},{3,2},{4,5},{5,4},{6,7},{7,6},{8,9},{9,8},{10,11... | collective-permute-start | bytes 3145736 | tf_op jit(solution)/shard_map/ppermute | solution.py:25
  42.5 2.4 %copy.16 = bf16[2,16,4,16,256]{4,3,2,1,0:T(8,128)(2,1)} copy(bf16[2,16,4,16,256]{4,3,1,2,0:T(8,128)(2,1)} %bitcast.86) | data formatting | bytes 2097152 | tf_op jit(solution)/shard_map/transpose | solution.py:346
  44.8 8.0 %all-to-all-start = ((bf16[32,4,16,256]{3,2,1,0:T(8,128)(2,1)}), bf16[32,4,16,256]{3,2,1,0:T(8,128)(2,1)S(1)}, u32[]{:S(2)}, u32[]{:S(2)}) async-start(bf16[32,4,16,256]{3,2,1,0:T(8,128)(2,1)} %bitcast.13), calls=%async_computation | async-start | bytes 2097152 | tf_op jit(solution)/shard_map/all_to_all | solution.py:347
  55.1 3.8 %collective-permute-start.14 = (bf16[2048,256]{1,0:T(8,128)(2,1)}, bf16[2048,256]{1,0:T(8,128)(2,1)}, u32[]{:S(2)}, u32[]{:S(2)}) collective-permute-start(bf16[2048,256]{1,0:T(8,128)(2,1)} %copy-done.4), channel_id=1, source_target_pairs={{0,1},{1,0},{2,3},{3,2},{4,5},{5,4},{6,7},{7,6},{8,9},{9,8},{10,11... | collective-permute-start | bytes 3145736 | tf_op jit(solution)/shard_map/ppermute | solution.py:25
  58.9 5.6 %collective-permute-done.5.refs_0_.refs_4_ = bf16[2304,256]{1,0:T(8,128)(2,1)S(1)} collective-permute-done((bf16[2304,256]{1,0:T(8,128)(2,1)}, bf16[2304,256]{1,0:T(8,128)(2,1)S(1)}, u32[]{:S(2)}, u32[]{:S(2)}) %collective-permute-start.5) | collective-permute-done | bytes 1179680 | tf_op jit(solution)/shard_map/ppermute | solution.py:25
  64.6 2.4 %collective-permute-start.12 = (bf16[2048,256]{1,0:T(8,128)(2,1)}, bf16[2048,256]{1,0:T(8,128)(2,1)}, u32[]{:S(2)}, u32[]{:S(2)}) collective-permute-start(bf16[2048,256]{1,0:T(8,128)(2,1)} %collective-permute-done.refs_0_.refs_1_), channel_id=1, source_target_pairs={{0,1},{1,0},{2,3},{3,2},{4,5},{5,4},{6,7},{7,6},{8,9},{9,8},{10,11... | collective-permute-start | bytes 3145736 | tf_op jit(solution)/shard_map/ppermute | solution.py:25
  67.0 5.5 %all-to-all-done = bf16[32,4,16,256]{3,2,1,0:T(8,128)(2,1)S(1)} async-done(((bf16[32,4,16,256]{3,2,1,0:T(8,128)(2,1)}), bf16[32,4,16,256]{3,2,1,0:T(8,128)(2,1)S(1)}, u32[]{:S(2)}, u32[]{:S(2)}) %all-to-all-start) | async-done | bytes 1048608 | tf_op jit(solution)/shard_map/all_to_all | solution.py:347
  75.6 2.7 %collective-permute-start.9 = (bf16[640,256]{1,0:T(8,128)(2,1)}, bf16[640,256]{1,0:T(8,128)(2,1)}, u32[]{:S(2)}, u32[]{:S(2)}) collective-permute-start(bf16[640,256]{1,0:T(8,128)(2,1)} %get-tuple-element.80), channel_id=1, source_target_pairs={{0,48},{16,0},{32,16},{48,32},{1,49},{17,1},{33,17},{49,33},{2,50}... | collective-permute-start | bytes 983048 | tf_op jit(solution)/shard_map/ppermute | solution.py:25
  78.6 7.7 %collective-permute-done.8.refs_7_ = bf16[640,256]{1,0:T(8,128)(2,1)} collective-permute-done((bf16[640,256]{1,0:T(8,128)(2,1)}, bf16[640,256]{1,0:T(8,128)(2,1)}, u32[]{:S(2)}, u32[]{:S(2)}) %collective-permute-start.8) | collective-permute-done | bytes 327712 | tf_op jit(solution)/shard_map/ppermute | solution.py:25
  92.7 10.3 %chip_sums.2 = (bf16[2,4,128,256]{3,2,1,0:T(8,128)(2,1)}, bf16[2,4,128,256]{3,2,1,0:T(8,128)(2,1)}, bf16[1,8,128,256]{3,2,1,0:T(8,128)(2,1)}, bf16[1,8,128,256]{3,2,1,0:T(8,128)(2,1)}) custom-call(s32[2,3,128]{2,1,0:T(4,128)} %pad_add_fusion.tables, s32[2]{0:T(128)} %pad_add_fusion.1.owners, s32[1]{0:T(128)} %bitcast.10.core, ...), custom_call_target="tpu_custom_call" | custom-call | flops 10000000000 | bytes 1024 | tf_op jit(solution)/shard_map/chip_sums/pallas_call | solution.py:100
  106.6 15.2 %chip_sums.3 = (bf16[2,8,128,256]{3,2,1,0:T(8,128)(2,1)}, bf16[2,8,128,256]{3,2,1,0:T(8,128)(2,1)}, bf16[2,8,128,256]{3,2,1,0:T(8,128)(2,1)}, bf16[3,8,128,256]{3,2,1,0:T(8,128)(2,1)}, bf16[3,8,128,256]{3,2,1,0:T(8,128)(2,1)}) custom-call(s32[2,3,128]{2,1,0:T(4,128)} %pad_add_fusion.tables, s32[6]{0:T(128)} %stack.60.owners, s32[1]{0:T(128)} %bitcast.10.core, ...), custom_call_target="tpu_custom_call" | custom-call | flops 17999998976 | bytes 1024 | tf_op jit(solution)/shard_map/chip_sums/pallas_call | solution.py:100
  125.0 2.5 %add_via.1 = (bf16[2,8,128,256]{3,2,1,0:T(8,128)(2,1)}, bf16[2,8,128,256]{3,2,1,0:T(8,128)(2,1)}) custom-call(bf16[2,8,128,256]{3,2,1,0:T(8,128)(2,1)} %get-tuple-element.91.up_in, bf16[2,8,128,256]{3,2,1,0:T(8,128)(2,1)} %get-tuple-element.92.down_in, bf16[2,4,128,256]{3,2,1,0:T(8,128)(2,1)} %copy-done.7, ...), custom_call_target="tpu_custom_call", output_to_operand_aliasing={{0}: (0, {}), {1}: (1, {})} | custom-call | tf_op jit(solution)/shard_map/add_via/pallas_call | solution.py:244
  129.4 3.5 %all-to-all-start.1 = ((bf16[4,32,16,256]{3,2,1,0:T(8,128)(2,1)}), bf16[4,32,16,256]{3,2,1,0:T(8,128)(2,1)S(1)}, u32[]{:S(2)}, u32[]{:S(2)}) async-start(bf16[4,32,16,256]{3,2,1,0:T(8,128)(2,1)} %copy.17), calls=%async_computation.1 | async-start | bytes 2097152 | tf_op jit(solution)/shard_map/all_to_all | solution.py:351
  136.2 10.6 %all-to-all-done.1 = bf16[4,32,16,256]{3,2,1,0:T(8,128)(2,1)S(1)} async-done(((bf16[4,32,16,256]{3,2,1,0:T(8,128)(2,1)}), bf16[4,32,16,256]{3,2,1,0:T(8,128)(2,1)S(1)}, u32[]{:S(2)}, u32[]{:S(2)}) %all-to-all-start.1) | async-done | bytes 1048608 | tf_op jit(solution)/shard_map/all_to_all | solution.py:351
  147.2 15.2 %collective-permute-done.28 = bf16[4,128,256]{2,1,0:T(8,128)(2,1)S(1)} collective-permute-done((bf16[4,128,256]{2,1,0:T(8,128)(2,1)}, bf16[4,128,256]{2,1,0:T(8,128)(2,1)S(1)}, u32[]{:S(2)}, u32[]{:S(2)}) %collective-permute-start.28) | collective-permute-done | bytes 262176 | tf_op jit(solution)/shard_map/ppermute | solution.py:25
  169.4 7.4 %collective-permute-done.31 = bf16[8,128,256]{2,1,0:T(8,128)(2,1)S(1)} collective-permute-done((bf16[8,128,256]{2,1,0:T(8,128)(2,1)S(1)}, bf16[8,128,256]{2,1,0:T(8,128)(2,1)S(1)}, u32[]{:S(2)}, u32[]{:S(2)}) %collective-permute-start.31) | collective-permute-done | bytes 524320 | tf_op jit(solution)/shard_map/ppermute | solution.py:25
  181.8 31.1 %all_to_all.20 = bf16[128,40,128]{2,1,0:T(8,128)(2,1)S(1)} all-to-all(bf16[128,40,128]{2,1,0:T(8,128)(2,1)S(1)} %pad_maximum_fusion), channel_id=1, replica_groups=mesh['xl'=2,'y'=4,'xh'=2,'z'=4,'core'=2] {'xl','y','xh','z','core'}, dimensions={0} | all-to-all | bytes 2621440 | tf_op jit(solution)/shard_map/all_to_all | solution.py:374
  213.9 4.5 %all-to-all-start.3 = ((f32[128,2,256]{2,1,0:T(2,128)}), f32[128,2,256]{2,1,0:T(2,128)S(1)}, u32[]{:S(2)}, u32[]{:S(2)}) async-start(f32[128,2,256]{2,1,0:T(2,128)} %broadcast_in_dim.2), calls=%async_computation.3 | async-start | bytes 524288 | tf_op jit(solution)/shard_map/all_to_all | solution.py:383
  219.7 9.9 %all-to-all-done.3 = f32[128,2,256]{2,1,0:T(2,128)S(1)} async-done(((f32[128,2,256]{2,1,0:T(2,128)}), f32[128,2,256]{2,1,0:T(2,128)S(1)}, u32[]{:S(2)}, u32[]{:S(2)}) %all-to-all-start.3) | async-done | bytes 262176 | tf_op jit(solution)/shard_map/all_to_all | solution.py:383
  (109 shorter events, 47.6 us)
Async XLA Ops:
  2.4 31.1 %collective-permute-start.4 = (bf16[8,8,128,128]{3,2,1,0:T(8,128)(2,1)S(1)}, bf16[8,8,128,128]{3,2,1,0:T(8,128)(2,1)}, u32[]{:S(2)}, u32[]{:S(2)}) collective-permute-start(bf16[8,8,128,128]{3,2,1,0:T(8,128)(2,1)S(1)} %dynamic-slice_bitcast_fusion), channel_id=1, source_target_pairs={{0,1},{1,0},{2,3},{3,2},{4,5},{5,4},{6,7},{7,6},{8,9},{9,8},{10,11... | collective-permute-start | bytes 6291464 | tf_op jit(solution)/shard_map/ppermute | solution.py:25
  4.0 25.0 %collective-permute-start.2 = (bf16[2048,256]{1,0:T(8,128)(2,1)}, bf16[2048,256]{1,0:T(8,128)(2,1)S(1)}, u32[]{:S(2)}, u32[]{:S(2)}) collective-permute-start(bf16[2048,256]{1,0:T(8,128)(2,1)} %refs_0_.3), channel_id=1, source_target_pairs={{0,64},{64,0},{1,65},{65,1},{2,66},{66,2},{3,67},{67,3},{4,68},{68... | collective-permute-start | bytes 3145736 | tf_op jit(solution)/shard_map/ppermute | solution.py:25
  5.3 25.2 %collective-permute-start.1 = (bf16[2048,256]{1,0:T(8,128)(2,1)}, bf16[2048,256]{1,0:T(8,128)(2,1)}, u32[]{:S(2)}, u32[]{:S(2)}) collective-permute-start(bf16[2048,256]{1,0:T(8,128)(2,1)} %refs_0_.3), channel_id=1, source_target_pairs={{0,48},{16,0},{32,16},{48,32},{1,49},{17,1},{33,17},{49,33},{2,50}... | collective-permute-start | bytes 3145736 | tf_op jit(solution)/shard_map/ppermute | solution.py:25
  8.0 25.6 %collective-permute-start = (bf16[2048,256]{1,0:T(8,128)(2,1)}, bf16[2048,256]{1,0:T(8,128)(2,1)}, u32[]{:S(2)}, u32[]{:S(2)}) collective-permute-start(bf16[2048,256]{1,0:T(8,128)(2,1)} %refs_0_.3), channel_id=1, source_target_pairs={{0,16},{16,32},{32,48},{48,0},{1,17},{17,33},{33,49},{49,1},{2,18}... | collective-permute-start | bytes 3145736 | tf_op jit(solution)/shard_map/ppermute | solution.py:25
  37.1 27.4 %collective-permute-start.5 = (bf16[2304,256]{1,0:T(8,128)(2,1)}, bf16[2304,256]{1,0:T(8,128)(2,1)S(1)}, u32[]{:S(2)}, u32[]{:S(2)}) collective-permute-start(bf16[2304,256]{1,0:T(8,128)(2,1)} %get-tuple-element.72), channel_id=1, source_target_pairs={{0,16},{16,32},{32,48},{48,0},{1,17},{17,33},{33,49},{49,1},{2,18}... | collective-permute-start | bytes 3538952 | tf_op jit(solution)/shard_map/ppermute | solution.py:25
  37.2 17.9 %collective-permute-start.7 = (bf16[1536,256]{1,0:T(8,128)(2,1)}, bf16[1536,256]{1,0:T(8,128)(2,1)}, u32[]{:S(2)}, u32[]{:S(2)}) collective-permute-start(bf16[1536,256]{1,0:T(8,128)(2,1)} %get-tuple-element.74), channel_id=1, source_target_pairs={{0,64},{64,0},{1,65},{65,1},{2,66},{66,2},{3,67},{67,3},{4,68},{68... | collective-permute-start | bytes 2359304 | tf_op jit(solution)/shard_map/ppermute | solution.py:25
  37.5 35.0 %collective-permute-start.6 = (bf16[2304,256]{1,0:T(8,128)(2,1)}, bf16[2304,256]{1,0:T(8,128)(2,1)S(1)}, u32[]{:S(2)}, u32[]{:S(2)}) collective-permute-start(bf16[2304,256]{1,0:T(8,128)(2,1)} %get-tuple-element.73), channel_id=1, source_target_pairs={{0,48},{16,0},{32,16},{48,32},{1,49},{17,1},{33,17},{49,33},{2,50}... | collective-permute-start | bytes 3538952 | tf_op jit(solution)/shard_map/ppermute | solution.py:25
  40.1 32.5 %collective-permute-start.11 = (bf16[2048,256]{1,0:T(8,128)(2,1)}, bf16[2048,256]{1,0:T(8,128)(2,1)}, u32[]{:S(2)}, u32[]{:S(2)}) collective-permute-start(bf16[2048,256]{1,0:T(8,128)(2,1)} %refs_0_.3), channel_id=1, source_target_pairs={{0,1},{1,0},{2,3},{3,2},{4,5},{5,4},{6,7},{7,6},{8,9},{9,8},{10,11... | collective-permute-start | bytes 3145736 | tf_op jit(solution)/shard_map/ppermute | solution.py:25
  44.8 27.7 %all-to-all-start = ((bf16[32,4,16,256]{3,2,1,0:T(8,128)(2,1)}), bf16[32,4,16,256]{3,2,1,0:T(8,128)(2,1)S(1)}, u32[]{:S(2)}, u32[]{:S(2)}) async-start(bf16[32,4,16,256]{3,2,1,0:T(8,128)(2,1)} %bitcast.13), calls=%async_computation | async-start | bytes 2097152 | tf_op jit(solution)/shard_map/all_to_all | solution.py:347
  52.9 22.7 %collective-permute-start.13 = (bf16[2048,256]{1,0:T(8,128)(2,1)}, bf16[2048,256]{1,0:T(8,128)(2,1)}, u32[]{:S(2)}, u32[]{:S(2)}) collective-permute-start(bf16[2048,256]{1,0:T(8,128)(2,1)} %collective-permute-done.1.refs_1_.refs_2_), channel_id=1, source_target_pairs={{0,1},{1,0},{2,3},{3,2},{4,5},{5,4},{6,7},{7,6},{8,9},{9,8},{10,11... | collective-permute-start | bytes 3145736 | tf_op jit(solution)/shard_map/ppermute | solution.py:25
  55.1 20.5 %collective-permute-start.14 = (bf16[2048,256]{1,0:T(8,128)(2,1)}, bf16[2048,256]{1,0:T(8,128)(2,1)}, u32[]{:S(2)}, u32[]{:S(2)}) collective-permute-start(bf16[2048,256]{1,0:T(8,128)(2,1)} %copy-done.4), channel_id=1, source_target_pairs={{0,1},{1,0},{2,3},{3,2},{4,5},{5,4},{6,7},{7,6},{8,9},{9,8},{10,11... | collective-permute-start | bytes 3145736 | tf_op jit(solution)/shard_map/ppermute | solution.py:25
  64.6 13.7 %collective-permute-start.12 = (bf16[2048,256]{1,0:T(8,128)(2,1)}, bf16[2048,256]{1,0:T(8,128)(2,1)}, u32[]{:S(2)}, u32[]{:S(2)}) collective-permute-start(bf16[2048,256]{1,0:T(8,128)(2,1)} %collective-permute-done.refs_0_.refs_1_), channel_id=1, source_target_pairs={{0,1},{1,0},{2,3},{3,2},{4,5},{5,4},{6,7},{7,6},{8,9},{9,8},{10,11... | collective-permute-start | bytes 3145736 | tf_op jit(solution)/shard_map/ppermute | solution.py:25
  72.5 20.2 %collective-permute-start.15 = (bf16[2304,256]{1,0:T(8,128)(2,1)S(1)}, bf16[2304,256]{1,0:T(8,128)(2,1)}, u32[]{:S(2)}, u32[]{:S(2)}) collective-permute-start(bf16[2304,256]{1,0:T(8,128)(2,1)S(1)} %collective-permute-done.5.refs_0_.refs_4_), channel_id=1, source_target_pairs={{0,1},{1,0},{2,3},{3,2},{4,5},{5,4},{6,7},{7,6},{8,9},{9,8},{10,11... | collective-permute-start | bytes 3538952 | tf_op jit(solution)/shard_map/ppermute | solution.py:25
  72.6 20.1 %collective-permute-start.16 = (bf16[2304,256]{1,0:T(8,128)(2,1)S(1)}, bf16[2304,256]{1,0:T(8,128)(2,1)}, u32[]{:S(2)}, u32[]{:S(2)}) collective-permute-start(bf16[2304,256]{1,0:T(8,128)(2,1)S(1)} %collective-permute-done.6.refs_1_.refs_5_), channel_id=1, source_target_pairs={{0,1},{1,0},{2,3},{3,2},{4,5},{5,4},{6,7},{7,6},{8,9},{9,8},{10,11... | collective-permute-start | bytes 3538952 | tf_op jit(solution)/shard_map/ppermute | solution.py:25
  103.1 18.7 %collective-permute-start.21 = (bf16[2,4,128,256]{3,2,1,0:T(8,128)(2,1)}, bf16[2,4,128,256]{3,2,1,0:T(8,128)(2,1)S(1)}, u32[]{:S(2)}, u32[]{:S(2)}) collective-permute-start(bf16[2,4,128,256]{3,2,1,0:T(8,128)(2,1)} %get-tuple-element.82), channel_id=1, source_target_pairs={{0,2},{2,4},{4,6},{6,0},{1,3},{3,5},{5,7},{7,1},{8,10},{10,12},{12... | collective-permute-start | bytes 1572872 | tf_op jit(solution)/shard_map/ppermute | solution.py:25
  103.9 18.0 %collective-permute-start.22 = (bf16[2,4,128,256]{3,2,1,0:T(8,128)(2,1)}, bf16[2,4,128,256]{3,2,1,0:T(8,128)(2,1)S(1)}, u32[]{:S(2)}, u32[]{:S(2)}) collective-permute-start(bf16[2,4,128,256]{3,2,1,0:T(8,128)(2,1)} %get-tuple-element.83), channel_id=1, source_target_pairs={{0,6},{2,0},{4,2},{6,4},{1,7},{3,1},{5,3},{7,5},{8,14},{10,8},{12,... | collective-permute-start | bytes 1572872 | tf_op jit(solution)/shard_map/ppermute | solution.py:25
  105.8 16.0 %collective-permute-start.23 = (bf16[1,8,128,256]{3,2,1,0:T(8,128)(2,1)}, bf16[1,8,128,256]{3,2,1,0:T(8,128)(2,1)S(1)}, u32[]{:S(2)}, u32[]{:S(2)}) collective-permute-start(bf16[1,8,128,256]{3,2,1,0:T(8,128)(2,1)} %get-tuple-element.84), channel_id=1, source_target_pairs={{0,8},{8,0},{1,9},{9,1},{2,10},{10,2},{3,11},{11,3},{4,12},{12,4},... | collective-permute-start | bytes 1572872 | tf_op jit(solution)/shard_map/ppermute | solution.py:25
  122.8 40.9 %collective-permute-start.26 = (bf16[3,8,128,256]{3,2,1,0:T(8,128)(2,1)}, bf16[3,8,128,256]{3,2,1,0:T(8,128)(2,1)S(1)}, u32[]{:S(2)}, u32[]{:S(2)}) collective-permute-start(bf16[3,8,128,256]{3,2,1,0:T(8,128)(2,1)} %get-tuple-element.97), channel_id=1, source_target_pairs={{0,8},{8,0},{1,9},{9,1},{2,10},{10,2},{3,11},{11,3},{4,12},{12,4},... | collective-permute-start | bytes 4718600 | tf_op jit(solution)/shard_map/ppermute | solution.py:25
  129.4 17.3 %all-to-all-start.1 = ((bf16[4,32,16,256]{3,2,1,0:T(8,128)(2,1)}), bf16[4,32,16,256]{3,2,1,0:T(8,128)(2,1)S(1)}, u32[]{:S(2)}, u32[]{:S(2)}) async-start(bf16[4,32,16,256]{3,2,1,0:T(8,128)(2,1)} %copy.17), calls=%async_computation.1 | async-start | bytes 2097152 | tf_op jit(solution)/shard_map/all_to_all | solution.py:351
  133.0 30.7 %collective-permute-start.25 = (bf16[2,8,128,256]{3,2,1,0:T(8,128)(2,1)}, bf16[2,8,128,256]{3,2,1,0:T(8,128)(2,1)}, u32[]{:S(2)}, u32[]{:S(2)}) collective-permute-start(bf16[2,8,128,256]{3,2,1,0:T(8,128)(2,1)} %get-tuple-element.96), channel_id=1, source_target_pairs={{0,6},{2,0},{4,2},{6,4},{1,7},{3,1},{5,3},{7,5},{8,14},{10,8},{12,... | collective-permute-start | bytes 3145736 | tf_op jit(solution)/shard_map/ppermute | solution.py:25
  133.2 30.5 %collective-permute-start.24 = (bf16[2,8,128,256]{3,2,1,0:T(8,128)(2,1)}, bf16[2,8,128,256]{3,2,1,0:T(8,128)(2,1)}, u32[]{:S(2)}, u32[]{:S(2)}) collective-permute-start(bf16[2,8,128,256]{3,2,1,0:T(8,128)(2,1)} %get-tuple-element.95), channel_id=1, source_target_pairs={{0,2},{2,4},{4,6},{6,0},{1,3},{3,5},{5,7},{7,1},{8,10},{10,12},{12... | collective-permute-start | bytes 3145736 | tf_op jit(solution)/shard_map/ppermute | solution.py:25
  134.7 27.7 %collective-permute-start.28 = (bf16[4,128,256]{2,1,0:T(8,128)(2,1)}, bf16[4,128,256]{2,1,0:T(8,128)(2,1)S(1)}, u32[]{:S(2)}, u32[]{:S(2)}) collective-permute-start(bf16[4,128,256]{2,1,0:T(8,128)(2,1)} %get-tuple-element.128), channel_id=1, source_target_pairs={{0,6},{2,0},{4,2},{6,4},{1,7},{3,1},{5,3},{7,5},{8,14},{10,8},{12,... | collective-permute-start | bytes 786440 | tf_op jit(solution)/shard_map/ppermute | solution.py:25
  136.0 27.7 %collective-permute-start.27 = (bf16[4,128,256]{2,1,0:T(8,128)(2,1)S(1)}, bf16[4,128,256]{2,1,0:T(8,128)(2,1)S(1)}, u32[]{:S(2)}, u32[]{:S(2)}) collective-permute-start(bf16[4,128,256]{2,1,0:T(8,128)(2,1)S(1)} %get-tuple-element.129), channel_id=1, source_target_pairs={{0,2},{2,4},{4,6},{6,0},{1,3},{3,5},{5,7},{7,1},{8,10},{10,12},{12... | collective-permute-start | bytes 786440 | tf_op jit(solution)/shard_map/ppermute | solution.py:25
  213.9 15.7 %all-to-all-start.3 = ((f32[128,2,256]{2,1,0:T(2,128)}), f32[128,2,256]{2,1,0:T(2,128)S(1)}, u32[]{:S(2)}, u32[]{:S(2)}) async-start(f32[128,2,256]{2,1,0:T(2,128)} %broadcast_in_dim.2), calls=%async_computation.3 | async-start | bytes 524288 | tf_op jit(solution)/shard_map/all_to_all | solution.py:383
  (22 other events, 337.3 us)

commit v5 on v4

--- a/solution.py
+++ b/solution.py
@@ -65,7 +65,7 @@
 
     for turn, slot in enumerate(slots):
         row = tables[1, 1, slot]
-        term = product(1, slot, other_adj_ref[turn, 0]).astype(jnp.float32)
+        term = product(1, slot, other_adj_ref[turn, 0, 0]).astype(jnp.float32)
         sums[row] = (sums[row].astype(jnp.float32) + term).astype(jnp.bfloat16)
 
     for out, (first, last, start, stop, every) in zip(outs, stores):
@@ -105,7 +105,7 @@
             grid=(steps,),
             in_specs=[
                 pl.BlockSpec((TURNS, 1, 1, BS, BS), lambda g, tb, ow, co: (0, ow[g], co[0], 0, 0)),
-                pl.BlockSpec((TURNS, 1, BS, BS), lambda g, tb, ow, co: (0, ow[g], 0, 0)),
+                pl.BlockSpec((TURNS, 1, 1, BS, BS), lambda g, tb, ow, co: (0, ow[g], co[0], 0, 0)),
                 *[pl.BlockSpec(memory_space=pl.ANY)] * len(pieces),
             ],
             out_specs=specs,
@@ -334,7 +334,6 @@
         return jnp.stack(chips).astype(jnp.int32)
 
     adj = adj_blocks.reshape(TURNS, PEERS, 2, BS, BS)
-    other_adj = lax.dynamic_index_in_dim(adj, 1 - core, 2, keepdims=False)
 
     def tied(value, *others):
         return lax.optimization_barrier((value, others))[0]
@@ -352,7 +351,7 @@
         grads = grads.reshape(4, 2, 16, sub_rows, feat_width).transpose(1, 0, 2, 3, 4)
         return grads.reshape(local_rows, feat_width)
 
-    layout, pieces, (theirs, other_adj), grads = gather(features, (mine, other_adj), grads_first)
+    layout, pieces, (theirs, other_adj), grads = gather(features, (mine, adj), grads_first)
     tables = jnp.stack([mine, theirs.at[0].add(CB)])
     products = functools.partial(
         chip_sums, tables=tables, owners=owners, core=core.reshape(1), adj=adj, other_adj=other_adj

time: 231 us -> 230 us (level)
  no operation moved by 1% of the time
where the time goes in v5:
time: 230 us
  waiting for transfers between devices  93.1 us (40%)
  starting transfers between devices  51.3 us (22%)
  Pallas kernels  33.7 us (15%)
  blocking collectives  31.1 us (14%)
  local copies, waits for them, and re-layouts  8.74 us (4%)
  other arithmetic  8.48 us (4%)
    ppermute x32, waiting for transfers between devices, permute(): return lax.ppermute(value, axis, ring(lax.axis_size(axis), step))  66.8 us
    ppermute x32, starting transfers between devices, permute(): return lax.ppermute(value, axis, ring(lax.axis_size(axis), step))  35.3 us
    all_to_all x1, blocking collectives, on_device(): came = lax.all_to_all(sent, AXES, split_axis=0, concat_axis=0, tiled=True)  31.1 us
    pallas_call x2, Pallas kernels, chip_sums(): pl.pallas_call(functools.partial(chip_kernel, layout, len(pieces), stores...  25.5 us
    all_to_all x1, waiting for transfers between devices, grads_last(): grads = lax.all_to_all(grads, 'y', 0, 0, tiled=True)  10.8 us
    all_to_all x1, waiting for transfers between devices, on_device(): lax.all_to_all(spread, AXES, split_axis=0, concat_axis=0, tiled=True)  9.94 us
    all_to_all x1, starting transfers between devices, grads_first(): return lax.all_to_all(grads, ('xl', 'xh', 'z', 'core'), 0, 0, tiled=True)  8.04 us
    pallas_call x2, Pallas kernels, copy_rows(): pl.pallas_call(functools.partial(copy_rows_kernel, plans, len(sources)),...  5.53 us
  transfers between devices with their start and end apart: 35, of which 17 were waited for; matrix products, arithmetic and copies ran while one was open for 4% of the time, Pallas kernels for 9%

profile of v5, /device:TPU:1, one launch (start us, length us, event | category | flops | bytes accessed | tf_op | source)
XLA Modules:
  0.0 229.7 jit_solution(12792289377237481825)
XLA Ops:
  3.5 2.7 %collective-permute-start.1 = (bf16[2048,256]{1,0:T(8,128)(2,1)}, bf16[2048,256]{1,0:T(8,128)(2,1)S(1)}, u32[]{:S(2)}, u32[]{:S(2)}) collective-permute-start(bf16[2048,256]{1,0:T(8,128)(2,1)} %refs_0_.3), channel_id=1, source_target_pairs={{0,48},{16,0},{32,16},{48,32},{1,49},{17,1},{33,17},{49,33},{2,50}... | collective-permute-start | bytes 3145736 | tf_op jit(solution)/shard_map/ppermute | solution.py:25
  9.2 17.9 %collective-permute-done.2.refs_2_.refs_3_ = bf16[2048,256]{1,0:T(8,128)(2,1)S(1)} collective-permute-done((bf16[2048,256]{1,0:T(8,128)(2,1)}, bf16[2048,256]{1,0:T(8,128)(2,1)S(1)}, u32[]{:S(2)}, u32[]{:S(2)}) %collective-permute-start.2) | collective-permute-done | bytes 1048608 | tf_op jit(solution)/shard_map/ppermute | solution.py:25
  28.7 3.0 %collective-permute-done.refs_0_.refs_1_ = bf16[2048,256]{1,0:T(8,128)(2,1)S(1)} collective-permute-done((bf16[2048,256]{1,0:T(8,128)(2,1)}, bf16[2048,256]{1,0:T(8,128)(2,1)S(1)}, u32[]{:S(2)}, u32[]{:S(2)}) %collective-permute-start) | collective-permute-done | bytes 1048608 | tf_op jit(solution)/shard_map/ppermute | solution.py:25
  32.6 3.5 %copy_rows.2 = (bf16[2304,256]{1,0:T(8,128)(2,1)}, bf16[2304,256]{1,0:T(8,128)(2,1)}, bf16[1536,256]{1,0:T(8,128)(2,1)}) custom-call(bf16[2048,256]{1,0:T(8,128)(2,1)} %copy-done.6, bf16[2048,256]{1,0:T(8,128)(2,1)} %copy-done.5, bf16[2048,256]{1,0:T(8,128)(2,1)} %copy-done.4), custom_call_target="tpu_custom_call" | custom-call | tf_op jit(solution)/shard_map/copy_rows/pallas_call | solution.py:154
  36.6 2.6 %collective-permute-start.6 = (bf16[2304,256]{1,0:T(8,128)(2,1)}, bf16[2304,256]{1,0:T(8,128)(2,1)S(1)}, u32[]{:S(2)}, u32[]{:S(2)}) collective-permute-start(bf16[2304,256]{1,0:T(8,128)(2,1)} %get-tuple-element.73), channel_id=1, source_target_pairs={{0,48},{16,0},{32,16},{48,32},{1,49},{17,1},{33,17},{49,33},{2,50}... | collective-permute-start | bytes 3538952 | tf_op jit(solution)/shard_map/ppermute | solution.py:25
  39.2 2.3 %collective-permute-start.11 = (bf16[2048,256]{1,0:T(8,128)(2,1)}, bf16[2048,256]{1,0:T(8,128)(2,1)}, u32[]{:S(2)}, u32[]{:S(2)}) collective-permute-start(bf16[2048,256]{1,0:T(8,128)(2,1)} %refs_0_.3), channel_id=1, source_target_pairs={{0,1},{1,0},{2,3},{3,2},{4,5},{5,4},{6,7},{7,6},{8,9},{9,8},{10,11... | collective-permute-start | bytes 3145736 | tf_op jit(solution)/shard_map/ppermute | solution.py:25
  41.5 2.3 %copy.16 = bf16[2,16,4,16,256]{4,3,2,1,0:T(8,128)(2,1)} copy(bf16[2,16,4,16,256]{4,3,1,2,0:T(8,128)(2,1)} %bitcast.81) | data formatting | bytes 2097152 | tf_op jit(solution)/shard_map/transpose | solution.py:345
  43.8 8.0 %all-to-all-start = ((bf16[32,4,16,256]{3,2,1,0:T(8,128)(2,1)}), bf16[32,4,16,256]{3,2,1,0:T(8,128)(2,1)S(1)}, u32[]{:S(2)}, u32[]{:S(2)}) async-start(bf16[32,4,16,256]{3,2,1,0:T(8,128)(2,1)} %bitcast.12), calls=%async_computation | async-start | bytes 2097152 | tf_op jit(solution)/shard_map/all_to_all | solution.py:346
  54.2 3.8 %collective-permute-start.14 = (bf16[2048,256]{1,0:T(8,128)(2,1)}, bf16[2048,256]{1,0:T(8,128)(2,1)}, u32[]{:S(2)}, u32[]{:S(2)}) collective-permute-start(bf16[2048,256]{1,0:T(8,128)(2,1)} %copy-done.4), channel_id=1, source_target_pairs={{0,1},{1,0},{2,3},{3,2},{4,5},{5,4},{6,7},{7,6},{8,9},{9,8},{10,11... | collective-permute-start | bytes 3145736 | tf_op jit(solution)/shard_map/ppermute | solution.py:25
  58.0 5.6 %collective-permute-done.5.refs_0_.refs_4_ = bf16[2304,256]{1,0:T(8,128)(2,1)S(1)} collective-permute-done((bf16[2304,256]{1,0:T(8,128)(2,1)}, bf16[2304,256]{1,0:T(8,128)(2,1)S(1)}, u32[]{:S(2)}, u32[]{:S(2)}) %collective-permute-start.5) | collective-permute-done | bytes 1179680 | tf_op jit(solution)/shard_map/ppermute | solution.py:25
  63.6 2.4 %collective-permute-start.12 = (bf16[2048,256]{1,0:T(8,128)(2,1)}, bf16[2048,256]{1,0:T(8,128)(2,1)}, u32[]{:S(2)}, u32[]{:S(2)}) collective-permute-start(bf16[2048,256]{1,0:T(8,128)(2,1)} %copy-done.6), channel_id=1, source_target_pairs={{0,1},{1,0},{2,3},{3,2},{4,5},{5,4},{6,7},{7,6},{8,9},{9,8},{10,11... | collective-permute-start | bytes 3145736 | tf_op jit(solution)/shard_map/ppermute | solution.py:25
  66.0 5.5 %all-to-all-done = bf16[32,4,16,256]{3,2,1,0:T(8,128)(2,1)S(1)} async-done(((bf16[32,4,16,256]{3,2,1,0:T(8,128)(2,1)}), bf16[32,4,16,256]{3,2,1,0:T(8,128)(2,1)S(1)}, u32[]{:S(2)}, u32[]{:S(2)}) %all-to-all-start) | async-done | bytes 1048608 | tf_op jit(solution)/shard_map/all_to_all | solution.py:346
  74.7 2.7 %collective-permute-start.9 = (bf16[640,256]{1,0:T(8,128)(2,1)}, bf16[640,256]{1,0:T(8,128)(2,1)}, u32[]{:S(2)}, u32[]{:S(2)}) collective-permute-start(bf16[640,256]{1,0:T(8,128)(2,1)} %get-tuple-element.80), channel_id=1, source_target_pairs={{0,48},{16,0},{32,16},{48,32},{1,49},{17,1},{33,17},{49,33},{2,50}... | collective-permute-start | bytes 983048 | tf_op jit(solution)/shard_map/ppermute | solution.py:25
  77.6 7.7 %collective-permute-done.8.refs_7_ = bf16[640,256]{1,0:T(8,128)(2,1)} collective-permute-done((bf16[640,256]{1,0:T(8,128)(2,1)}, bf16[640,256]{1,0:T(8,128)(2,1)}, u32[]{:S(2)}, u32[]{:S(2)}) %collective-permute-start.8) | collective-permute-done | bytes 327712 | tf_op jit(solution)/shard_map/ppermute | solution.py:25
  91.8 10.3 %chip_sums.2 = (bf16[2,4,128,256]{3,2,1,0:T(8,128)(2,1)}, bf16[2,4,128,256]{3,2,1,0:T(8,128)(2,1)}, bf16[1,8,128,256]{3,2,1,0:T(8,128)(2,1)}, bf16[1,8,128,256]{3,2,1,0:T(8,128)(2,1)}) custom-call(s32[2,3,128]{2,1,0:T(4,128)} %pad_add_fusion.tables, s32[2]{0:T(128)} %pad_add_fusion.1.owners, s32[1]{0:T(128)} %bitcast.9.core, ...), custom_call_target="tpu_custom_call" | custom-call | flops 10000000000 | bytes 1024 | tf_op jit(solution)/shard_map/chip_sums/pallas_call | solution.py:100
  105.6 15.2 %chip_sums.3 = (bf16[2,8,128,256]{3,2,1,0:T(8,128)(2,1)}, bf16[2,8,128,256]{3,2,1,0:T(8,128)(2,1)}, bf16[2,8,128,256]{3,2,1,0:T(8,128)(2,1)}, bf16[3,8,128,256]{3,2,1,0:T(8,128)(2,1)}, bf16[3,8,128,256]{3,2,1,0:T(8,128)(2,1)}) custom-call(s32[2,3,128]{2,1,0:T(4,128)} %pad_add_fusion.tables, s32[6]{0:T(128)} %stack.60.owners, s32[1]{0:T(128)} %bitcast.9.core, ...), custom_call_target="tpu_custom_call" | custom-call | flops 17999998976 | bytes 1024 | tf_op jit(solution)/shard_map/chip_sums/pallas_call | solution.py:100
  124.0 2.6 %add_via.1 = (bf16[2,8,128,256]{3,2,1,0:T(8,128)(2,1)}, bf16[2,8,128,256]{3,2,1,0:T(8,128)(2,1)}) custom-call(bf16[2,8,128,256]{3,2,1,0:T(8,128)(2,1)} %get-tuple-element.91.up_in, bf16[2,8,128,256]{3,2,1,0:T(8,128)(2,1)} %get-tuple-element.92.down_in, bf16[2,4,128,256]{3,2,1,0:T(8,128)(2,1)} %copy-done.9, ...), custom_call_target="tpu_custom_call", output_to_operand_aliasing={{0}: (0, {}), {1}: (1, {})} | custom-call | tf_op jit(solution)/shard_map/add_via/pallas_call | solution.py:244
  128.6 3.5 %all-to-all-start.1 = ((bf16[4,32,16,256]{3,2,1,0:T(8,128)(2,1)}), bf16[4,32,16,256]{3,2,1,0:T(8,128)(2,1)S(1)}, u32[]{:S(2)}, u32[]{:S(2)}) async-start(bf16[4,32,16,256]{3,2,1,0:T(8,128)(2,1)} %copy.17), calls=%async_computation.1 | async-start | bytes 2097152 | tf_op jit(solution)/shard_map/all_to_all | solution.py:350
  135.1 10.8 %all-to-all-done.1 = bf16[4,32,16,256]{3,2,1,0:T(8,128)(2,1)S(1)} async-done(((bf16[4,32,16,256]{3,2,1,0:T(8,128)(2,1)}), bf16[4,32,16,256]{3,2,1,0:T(8,128)(2,1)S(1)}, u32[]{:S(2)}, u32[]{:S(2)}) %all-to-all-start.1) | async-done | bytes 1048608 | tf_op jit(solution)/shard_map/all_to_all | solution.py:350
  146.4 15.0 %collective-permute-done.28 = bf16[4,128,256]{2,1,0:T(8,128)(2,1)S(1)} collective-permute-done((bf16[4,128,256]{2,1,0:T(8,128)(2,1)}, bf16[4,128,256]{2,1,0:T(8,128)(2,1)S(1)}, u32[]{:S(2)}, u32[]{:S(2)}) %collective-permute-start.28) | collective-permute-done | bytes 262176 | tf_op jit(solution)/shard_map/ppermute | solution.py:25
  168.5 7.4 %collective-permute-done.31 = bf16[8,128,256]{2,1,0:T(8,128)(2,1)S(1)} collective-permute-done((bf16[8,128,256]{2,1,0:T(8,128)(2,1)S(1)}, bf16[8,128,256]{2,1,0:T(8,128)(2,1)S(1)}, u32[]{:S(2)}, u32[]{:S(2)}) %collective-permute-start.31) | collective-permute-done | bytes 524320 | tf_op jit(solution)/shard_map/ppermute | solution.py:25
  181.0 31.1 %all_to_all.20 = bf16[128,40,128]{2,1,0:T(8,128)(2,1)S(1)} all-to-all(bf16[128,40,128]{2,1,0:T(8,128)(2,1)S(1)} %pad_maximum_fusion), channel_id=1, replica_groups=mesh['xl'=2,'y'=4,'xh'=2,'z'=4,'core'=2] {'xl','y','xh','z','core'}, dimensions={0} | all-to-all | bytes 2621440 | tf_op jit(solution)/shard_map/all_to_all | solution.py:373
  213.1 4.5 %all-to-all-start.3 = ((f32[128,2,256]{2,1,0:T(2,128)}), f32[128,2,256]{2,1,0:T(2,128)S(1)}, u32[]{:S(2)}, u32[]{:S(2)}) async-start(f32[128,2,256]{2,1,0:T(2,128)} %broadcast_in_dim.2), calls=%async_computation.3 | async-start | bytes 524288 | tf_op jit(solution)/shard_map/all_to_all | solution.py:382
  218.8 9.9 %all-to-all-done.3 = f32[128,2,256]{2,1,0:T(2,128)S(1)} async-done(((f32[128,2,256]{2,1,0:T(2,128)}), f32[128,2,256]{2,1,0:T(2,128)S(1)}, u32[]{:S(2)}, u32[]{:S(2)}) %all-to-all-start.3) | async-done | bytes 262176 | tf_op jit(solution)/shard_map/all_to_all | solution.py:382
  (108 shorter events, 47.5 us)
Async XLA Ops:
  0.6 31.0 %collective-permute-start.4 = (bf16[8,8,2,128,128]{4,3,2,1,0:T(8,128)(2,1)}, bf16[8,8,2,128,128]{4,3,2,1,0:T(8,128)(2,1)}, u32[]{:S(2)}, u32[]{:S(2)}) collective-permute-start(bf16[8,8,2,128,128]{4,3,2,1,0:T(8,128)(2,1)} %bitcast.84), channel_id=1, source_target_pairs={{0,1},{1,0},{2,3},{3,2},{4,5},{5,4},{6,7},{7,6},{8,9},{9,8},{10,11... | collective-permute-start | bytes 12582920 | tf_op jit(solution)/shard_map/ppermute | solution.py:25
  2.1 24.9 %collective-permute-start.2 = (bf16[2048,256]{1,0:T(8,128)(2,1)}, bf16[2048,256]{1,0:T(8,128)(2,1)S(1)}, u32[]{:S(2)}, u32[]{:S(2)}) collective-permute-start(bf16[2048,256]{1,0:T(8,128)(2,1)} %refs_0_.3), channel_id=1, source_target_pairs={{0,64},{64,0},{1,65},{65,1},{2,66},{66,2},{3,67},{67,3},{4,68},{68... | collective-permute-start | bytes 3145736 | tf_op jit(solution)/shard_map/ppermute | solution.py:25
  3.5 25.2 %collective-permute-start.1 = (bf16[2048,256]{1,0:T(8,128)(2,1)}, bf16[2048,256]{1,0:T(8,128)(2,1)S(1)}, u32[]{:S(2)}, u32[]{:S(2)}) collective-permute-start(bf16[2048,256]{1,0:T(8,128)(2,1)} %refs_0_.3), channel_id=1, source_target_pairs={{0,48},{16,0},{32,16},{48,32},{1,49},{17,1},{33,17},{49,33},{2,50}... | collective-permute-start | bytes 3145736 | tf_op jit(solution)/shard_map/ppermute | solution.py:25
  6.2 25.5 %collective-permute-start = (bf16[2048,256]{1,0:T(8,128)(2,1)}, bf16[2048,256]{1,0:T(8,128)(2,1)S(1)}, u32[]{:S(2)}, u32[]{:S(2)}) collective-permute-start(bf16[2048,256]{1,0:T(8,128)(2,1)} %refs_0_.3), channel_id=1, source_target_pairs={{0,16},{16,32},{32,48},{48,0},{1,17},{17,33},{33,49},{49,1},{2,18}... | collective-permute-start | bytes 3145736 | tf_op jit(solution)/shard_map/ppermute | solution.py:25
  36.2 27.4 %collective-permute-start.5 = (bf16[2304,256]{1,0:T(8,128)(2,1)}, bf16[2304,256]{1,0:T(8,128)(2,1)S(1)}, u32[]{:S(2)}, u32[]{:S(2)}) collective-permute-start(bf16[2304,256]{1,0:T(8,128)(2,1)} %get-tuple-element.72), channel_id=1, source_target_pairs={{0,16},{16,32},{32,48},{48,0},{1,17},{17,33},{33,49},{49,1},{2,18}... | collective-permute-start | bytes 3538952 | tf_op jit(solution)/shard_map/ppermute | solution.py:25
  36.3 17.9 %collective-permute-start.7 = (bf16[1536,256]{1,0:T(8,128)(2,1)}, bf16[1536,256]{1,0:T(8,128)(2,1)}, u32[]{:S(2)}, u32[]{:S(2)}) collective-permute-start(bf16[1536,256]{1,0:T(8,128)(2,1)} %get-tuple-element.74), channel_id=1, source_target_pairs={{0,64},{64,0},{1,65},{65,1},{2,66},{66,2},{3,67},{67,3},{4,68},{68... | collective-permute-start | bytes 2359304 | tf_op jit(solution)/shard_map/ppermute | solution.py:25
  36.6 35.0 %collective-permute-start.6 = (bf16[2304,256]{1,0:T(8,128)(2,1)}, bf16[2304,256]{1,0:T(8,128)(2,1)S(1)}, u32[]{:S(2)}, u32[]{:S(2)}) collective-permute-start(bf16[2304,256]{1,0:T(8,128)(2,1)} %get-tuple-element.73), channel_id=1, source_target_pairs={{0,48},{16,0},{32,16},{48,32},{1,49},{17,1},{33,17},{49,33},{2,50}... | collective-permute-start | bytes 3538952 | tf_op jit(solution)/shard_map/ppermute | solution.py:25
  39.2 32.5 %collective-permute-start.11 = (bf16[2048,256]{1,0:T(8,128)(2,1)}, bf16[2048,256]{1,0:T(8,128)(2,1)}, u32[]{:S(2)}, u32[]{:S(2)}) collective-permute-start(bf16[2048,256]{1,0:T(8,128)(2,1)} %refs_0_.3), channel_id=1, source_target_pairs={{0,1},{1,0},{2,3},{3,2},{4,5},{5,4},{6,7},{7,6},{8,9},{9,8},{10,11... | collective-permute-start | bytes 3145736 | tf_op jit(solution)/shard_map/ppermute | solution.py:25
  43.8 27.7 %all-to-all-start = ((bf16[32,4,16,256]{3,2,1,0:T(8,128)(2,1)}), bf16[32,4,16,256]{3,2,1,0:T(8,128)(2,1)S(1)}, u32[]{:S(2)}, u32[]{:S(2)}) async-start(bf16[32,4,16,256]{3,2,1,0:T(8,128)(2,1)} %bitcast.12), calls=%async_computation | async-start | bytes 2097152 | tf_op jit(solution)/shard_map/all_to_all | solution.py:346
  51.9 22.7 %collective-permute-start.13 = (bf16[2048,256]{1,0:T(8,128)(2,1)}, bf16[2048,256]{1,0:T(8,128)(2,1)}, u32[]{:S(2)}, u32[]{:S(2)}) collective-permute-start(bf16[2048,256]{1,0:T(8,128)(2,1)} %copy-done.5), channel_id=1, source_target_pairs={{0,1},{1,0},{2,3},{3,2},{4,5},{5,4},{6,7},{7,6},{8,9},{9,8},{10,11... | collective-permute-start | bytes 3145736 | tf_op jit(solution)/shard_map/ppermute | solution.py:25
  54.2 20.5 %collective-permute-start.14 = (bf16[2048,256]{1,0:T(8,128)(2,1)}, bf16[2048,256]{1,0:T(8,128)(2,1)}, u32[]{:S(2)}, u32[]{:S(2)}) collective-permute-start(bf16[2048,256]{1,0:T(8,128)(2,1)} %copy-done.4), channel_id=1, source_target_pairs={{0,1},{1,0},{2,3},{3,2},{4,5},{5,4},{6,7},{7,6},{8,9},{9,8},{10,11... | collective-permute-start | bytes 3145736 | tf_op jit(solution)/shard_map/ppermute | solution.py:25
  63.6 13.7 %collective-permute-start.12 = (bf16[2048,256]{1,0:T(8,128)(2,1)}, bf16[2048,256]{1,0:T(8,128)(2,1)}, u32[]{:S(2)}, u32[]{:S(2)}) collective-permute-start(bf16[2048,256]{1,0:T(8,128)(2,1)} %copy-done.6), channel_id=1, source_target_pairs={{0,1},{1,0},{2,3},{3,2},{4,5},{5,4},{6,7},{7,6},{8,9},{9,8},{10,11... | collective-permute-start | bytes 3145736 | tf_op jit(solution)/shard_map/ppermute | solution.py:25
  71.5 20.2 %collective-permute-start.15 = (bf16[2304,256]{1,0:T(8,128)(2,1)S(1)}, bf16[2304,256]{1,0:T(8,128)(2,1)}, u32[]{:S(2)}, u32[]{:S(2)}) collective-permute-start(bf16[2304,256]{1,0:T(8,128)(2,1)S(1)} %collective-permute-done.5.refs_0_.refs_4_), channel_id=1, source_target_pairs={{0,1},{1,0},{2,3},{3,2},{4,5},{5,4},{6,7},{7,6},{8,9},{9,8},{10,11... | collective-permute-start | bytes 3538952 | tf_op jit(solution)/shard_map/ppermute | solution.py:25
  71.7 20.1 %collective-permute-start.16 = (bf16[2304,256]{1,0:T(8,128)(2,1)S(1)}, bf16[2304,256]{1,0:T(8,128)(2,1)}, u32[]{:S(2)}, u32[]{:S(2)}) collective-permute-start(bf16[2304,256]{1,0:T(8,128)(2,1)S(1)} %collective-permute-done.6.refs_1_.refs_5_), channel_id=1, source_target_pairs={{0,1},{1,0},{2,3},{3,2},{4,5},{5,4},{6,7},{7,6},{8,9},{9,8},{10,11... | collective-permute-start | bytes 3538952 | tf_op jit(solution)/shard_map/ppermute | solution.py:25
  102.1 18.7 %collective-permute-start.21 = (bf16[2,4,128,256]{3,2,1,0:T(8,128)(2,1)}, bf16[2,4,128,256]{3,2,1,0:T(8,128)(2,1)S(1)}, u32[]{:S(2)}, u32[]{:S(2)}) collective-permute-start(bf16[2,4,128,256]{3,2,1,0:T(8,128)(2,1)} %get-tuple-element.82), channel_id=1, source_target_pairs={{0,2},{2,4},{4,6},{6,0},{1,3},{3,5},{5,7},{7,1},{8,10},{10,12},{12... | collective-permute-start | bytes 1572872 | tf_op jit(solution)/shard_map/ppermute | solution.py:25
  102.9 17.9 %collective-permute-start.22 = (bf16[2,4,128,256]{3,2,1,0:T(8,128)(2,1)}, bf16[2,4,128,256]{3,2,1,0:T(8,128)(2,1)S(1)}, u32[]{:S(2)}, u32[]{:S(2)}) collective-permute-start(bf16[2,4,128,256]{3,2,1,0:T(8,128)(2,1)} %get-tuple-element.83), channel_id=1, source_target_pairs={{0,6},{2,0},{4,2},{6,4},{1,7},{3,1},{5,3},{7,5},{8,14},{10,8},{12,... | collective-permute-start | bytes 1572872 | tf_op jit(solution)/shard_map/ppermute | solution.py:25
  104.9 16.0 %collective-permute-start.23 = (bf16[1,8,128,256]{3,2,1,0:T(8,128)(2,1)}, bf16[1,8,128,256]{3,2,1,0:T(8,128)(2,1)S(1)}, u32[]{:S(2)}, u32[]{:S(2)}) collective-permute-start(bf16[1,8,128,256]{3,2,1,0:T(8,128)(2,1)} %get-tuple-element.84), channel_id=1, source_target_pairs={{0,8},{8,0},{1,9},{9,1},{2,10},{10,2},{3,11},{11,3},{4,12},{12,4},... | collective-permute-start | bytes 1572872 | tf_op jit(solution)/shard_map/ppermute | solution.py:25
  121.8 41.0 %collective-permute-start.26 = (bf16[3,8,128,256]{3,2,1,0:T(8,128)(2,1)}, bf16[3,8,128,256]{3,2,1,0:T(8,128)(2,1)S(1)}, u32[]{:S(2)}, u32[]{:S(2)}) collective-permute-start(bf16[3,8,128,256]{3,2,1,0:T(8,128)(2,1)} %get-tuple-element.97), channel_id=1, source_target_pairs={{0,8},{8,0},{1,9},{9,1},{2,10},{10,2},{3,11},{11,3},{4,12},{12,4},... | collective-permute-start | bytes 4718600 | tf_op jit(solution)/shard_map/ppermute | solution.py:25
  128.6 17.3 %all-to-all-start.1 = ((bf16[4,32,16,256]{3,2,1,0:T(8,128)(2,1)}), bf16[4,32,16,256]{3,2,1,0:T(8,128)(2,1)S(1)}, u32[]{:S(2)}, u32[]{:S(2)}) async-start(bf16[4,32,16,256]{3,2,1,0:T(8,128)(2,1)} %copy.17), calls=%async_computation.1 | async-start | bytes 2097152 | tf_op jit(solution)/shard_map/all_to_all | solution.py:350
  132.1 30.8 %collective-permute-start.25 = (bf16[2,8,128,256]{3,2,1,0:T(8,128)(2,1)}, bf16[2,8,128,256]{3,2,1,0:T(8,128)(2,1)}, u32[]{:S(2)}, u32[]{:S(2)}) collective-permute-start(bf16[2,8,128,256]{3,2,1,0:T(8,128)(2,1)} %get-tuple-element.96), channel_id=1, source_target_pairs={{0,6},{2,0},{4,2},{6,4},{1,7},{3,1},{5,3},{7,5},{8,14},{10,8},{12,... | collective-permute-start | bytes 3145736 | tf_op jit(solution)/shard_map/ppermute | solution.py:25
  132.2 30.7 %collective-permute-start.24 = (bf16[2,8,128,256]{3,2,1,0:T(8,128)(2,1)}, bf16[2,8,128,256]{3,2,1,0:T(8,128)(2,1)}, u32[]{:S(2)}, u32[]{:S(2)}) collective-permute-start(bf16[2,8,128,256]{3,2,1,0:T(8,128)(2,1)} %get-tuple-element.95), channel_id=1, source_target_pairs={{0,2},{2,4},{4,6},{6,0},{1,3},{3,5},{5,7},{7,1},{8,10},{10,12},{12... | collective-permute-start | bytes 3145736 | tf_op jit(solution)/shard_map/ppermute | solution.py:25
  133.6 27.7 %collective-permute-start.28 = (bf16[4,128,256]{2,1,0:T(8,128)(2,1)}, bf16[4,128,256]{2,1,0:T(8,128)(2,1)S(1)}, u32[]{:S(2)}, u32[]{:S(2)}) collective-permute-start(bf16[4,128,256]{2,1,0:T(8,128)(2,1)} %get-tuple-element.128), channel_id=1, source_target_pairs={{0,6},{2,0},{4,2},{6,4},{1,7},{3,1},{5,3},{7,5},{8,14},{10,8},{12,... | collective-permute-start | bytes 786440 | tf_op jit(solution)/shard_map/ppermute | solution.py:25
  135.1 27.7 %collective-permute-start.27 = (bf16[4,128,256]{2,1,0:T(8,128)(2,1)S(1)}, bf16[4,128,256]{2,1,0:T(8,128)(2,1)S(1)}, u32[]{:S(2)}, u32[]{:S(2)}) collective-permute-start(bf16[4,128,256]{2,1,0:T(8,128)(2,1)S(1)} %get-tuple-element.129), channel_id=1, source_target_pairs={{0,2},{2,4},{4,6},{6,0},{1,3},{3,5},{5,7},{7,1},{8,10},{10,12},{12... | collective-permute-start | bytes 786440 | tf_op jit(solution)/shard_map/ppermute | solution.py:25
  213.1 15.7 %all-to-all-start.3 = ((f32[128,2,256]{2,1,0:T(2,128)}), f32[128,2,256]{2,1,0:T(2,128)S(1)}, u32[]{:S(2)}, u32[]{:S(2)}) async-start(f32[128,2,256]{2,1,0:T(2,128)} %broadcast_in_dim.2), calls=%async_computation.3 | async-start | bytes 524288 | tf_op jit(solution)/shard_map/all_to_all | solution.py:382
  (22 other events, 324.6 us)

commit v6 on v5

--- a/solution.py
+++ b/solution.py
@@ -346,7 +346,7 @@
         return lax.all_to_all(grads, ("xl", "xh", "z", "core"), 0, 0, tiled=True)
 
     def grads_last(grads, after):
-        grads = tied(grads, after).transpose(1, 0, 2, 3)
+        grads = tied(grads.transpose(1, 0, 2, 3), after)
         grads = lax.all_to_all(grads, "y", 0, 0, tiled=True)
         grads = grads.reshape(4, 2, 16, sub_rows, feat_width).transpose(1, 0, 2, 3, 4)
         return grads.reshape(local_rows, feat_width)

time: 230 us -> 230 us (level)
  no operation moved by 1% of the time
where the time goes in v6:
time: 230 us
  waiting for transfers between devices  93 us (40%)
  starting transfers between devices  51.4 us (22%)
  Pallas kernels  33.7 us (15%)
  blocking collectives  31.1 us (14%)
  local copies, waits for them, and re-layouts  8.74 us (4%)
  other arithmetic  8.48 us (4%)
    ppermute x32, waiting for transfers between devices, permute(): return lax.ppermute(value, axis, ring(lax.axis_size(axis), step))  66.8 us
    ppermute x32, starting transfers between devices, permute(): return lax.ppermute(value, axis, ring(lax.axis_size(axis), step))  35.3 us
    all_to_all x1, blocking collectives, on_device(): came = lax.all_to_all(sent, AXES, split_axis=0, concat_axis=0, tiled=True)  31.1 us
    pallas_call x2, Pallas kernels, chip_sums(): pl.pallas_call(functools.partial(chip_kernel, layout, len(pieces), stores...  25.5 us
    all_to_all x1, waiting for transfers between devices, grads_last(): grads = lax.all_to_all(grads, 'y', 0, 0, tiled=True)  10.8 us
    all_to_all x1, waiting for transfers between devices, on_device(): lax.all_to_all(spread, AXES, split_axis=0, concat_axis=0, tiled=True)  9.94 us
    all_to_all x1, starting transfers between devices, grads_first(): return lax.all_to_all(grads, ('xl', 'xh', 'z', 'core'), 0, 0, tiled=True)  8.04 us
    pallas_call x2, Pallas kernels, copy_rows(): pl.pallas_call(functools.partial(copy_rows_kernel, plans, len(sources)),...  5.53 us
  transfers between devices with their start and end apart: 35, of which 17 were waited for; matrix products, arithmetic and copies ran while one was open for 4% of the time, Pallas kernels for 9%

profile of v6, /device:TPU:1, one launch (start us, length us, event | category | flops | bytes accessed | tf_op | source)
XLA Modules:
  0.0 229.7 jit_solution(12792289377237481825)
XLA Ops:
  3.5 2.7 %collective-permute-start.1 = (bf16[2048,256]{1,0:T(8,128)(2,1)}, bf16[2048,256]{1,0:T(8,128)(2,1)S(1)}, u32[]{:S(2)}, u32[]{:S(2)}) collective-permute-start(bf16[2048,256]{1,0:T(8,128)(2,1)} %refs_0_.3), channel_id=1, source_target_pairs={{0,48},{16,0},{32,16},{48,32},{1,49},{17,1},{33,17},{49,33},{2,50}... | collective-permute-start | bytes 3145736 | tf_op jit(solution)/shard_map/ppermute | solution.py:25
  9.2 17.9 %collective-permute-done.2.refs_2_.refs_3_ = bf16[2048,256]{1,0:T(8,128)(2,1)S(1)} collective-permute-done((bf16[2048,256]{1,0:T(8,128)(2,1)}, bf16[2048,256]{1,0:T(8,128)(2,1)S(1)}, u32[]{:S(2)}, u32[]{:S(2)}) %collective-permute-start.2) | collective-permute-done | bytes 1048608 | tf_op jit(solution)/shard_map/ppermute | solution.py:25
  28.7 3.0 %collective-permute-done.refs_0_.refs_1_ = bf16[2048,256]{1,0:T(8,128)(2,1)S(1)} collective-permute-done((bf16[2048,256]{1,0:T(8,128)(2,1)}, bf16[2048,256]{1,0:T(8,128)(2,1)S(1)}, u32[]{:S(2)}, u32[]{:S(2)}) %collective-permute-start) | collective-permute-done | bytes 1048608 | tf_op jit(solution)/shard_map/ppermute | solution.py:25
  32.6 3.5 %copy_rows.2 = (bf16[2304,256]{1,0:T(8,128)(2,1)}, bf16[2304,256]{1,0:T(8,128)(2,1)}, bf16[1536,256]{1,0:T(8,128)(2,1)}) custom-call(bf16[2048,256]{1,0:T(8,128)(2,1)} %copy-done.6, bf16[2048,256]{1,0:T(8,128)(2,1)} %copy-done.5, bf16[2048,256]{1,0:T(8,128)(2,1)} %copy-done.4), custom_call_target="tpu_custom_call" | custom-call | tf_op jit(solution)/shard_map/copy_rows/pallas_call | solution.py:154
  36.6 2.6 %collective-permute-start.6 = (bf16[2304,256]{1,0:T(8,128)(2,1)}, bf16[2304,256]{1,0:T(8,128)(2,1)S(1)}, u32[]{:S(2)}, u32[]{:S(2)}) collective-permute-start(bf16[2304,256]{1,0:T(8,128)(2,1)} %get-tuple-element.73), channel_id=1, source_target_pairs={{0,48},{16,0},{32,16},{48,32},{1,49},{17,1},{33,17},{49,33},{2,50}... | collective-permute-start | bytes 3538952 | tf_op jit(solution)/shard_map/ppermute | solution.py:25
  39.2 2.3 %collective-permute-start.11 = (bf16[2048,256]{1,0:T(8,128)(2,1)}, bf16[2048,256]{1,0:T(8,128)(2,1)}, u32[]{:S(2)}, u32[]{:S(2)}) collective-permute-start(bf16[2048,256]{1,0:T(8,128)(2,1)} %refs_0_.3), channel_id=1, source_target_pairs={{0,1},{1,0},{2,3},{3,2},{4,5},{5,4},{6,7},{7,6},{8,9},{9,8},{10,11... | collective-permute-start | bytes 3145736 | tf_op jit(solution)/shard_map/ppermute | solution.py:25
  41.5 2.3 %copy.16 = bf16[2,16,4,16,256]{4,3,2,1,0:T(8,128)(2,1)} copy(bf16[2,16,4,16,256]{4,3,1,2,0:T(8,128)(2,1)} %bitcast.81) | data formatting | bytes 2097152 | tf_op jit(solution)/shard_map/transpose | solution.py:345
  43.8 8.0 %all-to-all-start = ((bf16[32,4,16,256]{3,2,1,0:T(8,128)(2,1)}), bf16[32,4,16,256]{3,2,1,0:T(8,128)(2,1)S(1)}, u32[]{:S(2)}, u32[]{:S(2)}) async-start(bf16[32,4,16,256]{3,2,1,0:T(8,128)(2,1)} %bitcast.12), calls=%async_computation | async-start | bytes 2097152 | tf_op jit(solution)/shard_map/all_to_all | solution.py:346
  54.2 3.8 %collective-permute-start.14 = (bf16[2048,256]{1,0:T(8,128)(2,1)}, bf16[2048,256]{1,0:T(8,128)(2,1)}, u32[]{:S(2)}, u32[]{:S(2)}) collective-permute-start(bf16[2048,256]{1,0:T(8,128)(2,1)} %copy-done.4), channel_id=1, source_target_pairs={{0,1},{1,0},{2,3},{3,2},{4,5},{5,4},{6,7},{7,6},{8,9},{9,8},{10,11... | collective-permute-start | bytes 3145736 | tf_op jit(solution)/shard_map/ppermute | solution.py:25
  58.0 5.6 %collective-permute-done.5.refs_0_.refs_4_ = bf16[2304,256]{1,0:T(8,128)(2,1)S(1)} collective-permute-done((bf16[2304,256]{1,0:T(8,128)(2,1)}, bf16[2304,256]{1,0:T(8,128)(2,1)S(1)}, u32[]{:S(2)}, u32[]{:S(2)}) %collective-permute-start.5) | collective-permute-done | bytes 1179680 | tf_op jit(solution)/shard_map/ppermute | solution.py:25
  63.6 2.4 %collective-permute-start.12 = (bf16[2048,256]{1,0:T(8,128)(2,1)}, bf16[2048,256]{1,0:T(8,128)(2,1)}, u32[]{:S(2)}, u32[]{:S(2)}) collective-permute-start(bf16[2048,256]{1,0:T(8,128)(2,1)} %copy-done.6), channel_id=1, source_target_pairs={{0,1},{1,0},{2,3},{3,2},{4,5},{5,4},{6,7},{7,6},{8,9},{9,8},{10,11... | collective-permute-start | bytes 3145736 | tf_op jit(solution)/shard_map/ppermute | solution.py:25
  66.0 5.5 %all-to-all-done = bf16[32,4,16,256]{3,2,1,0:T(8,128)(2,1)S(1)} async-done(((bf16[32,4,16,256]{3,2,1,0:T(8,128)(2,1)}), bf16[32,4,16,256]{3,2,1,0:T(8,128)(2,1)S(1)}, u32[]{:S(2)}, u32[]{:S(2)}) %all-to-all-start) | async-done | bytes 1048608 | tf_op jit(solution)/shard_map/all_to_all | solution.py:346
  74.7 2.7 %collective-permute-start.9 = (bf16[640,256]{1,0:T(8,128)(2,1)}, bf16[640,256]{1,0:T(8,128)(2,1)}, u32[]{:S(2)}, u32[]{:S(2)}) collective-permute-start(bf16[640,256]{1,0:T(8,128)(2,1)} %get-tuple-element.80), channel_id=1, source_target_pairs={{0,48},{16,0},{32,16},{48,32},{1,49},{17,1},{33,17},{49,33},{2,50}... | collective-permute-start | bytes 983048 | tf_op jit(solution)/shard_map/ppermute | solution.py:25
  77.6 7.7 %collective-permute-done.8.refs_7_ = bf16[640,256]{1,0:T(8,128)(2,1)} collective-permute-done((bf16[640,256]{1,0:T(8,128)(2,1)}, bf16[640,256]{1,0:T(8,128)(2,1)}, u32[]{:S(2)}, u32[]{:S(2)}) %collective-permute-start.8) | collective-permute-done | bytes 327712 | tf_op jit(solution)/shard_map/ppermute | solution.py:25
  91.8 10.3 %chip_sums.2 = (bf16[2,4,128,256]{3,2,1,0:T(8,128)(2,1)}, bf16[2,4,128,256]{3,2,1,0:T(8,128)(2,1)}, bf16[1,8,128,256]{3,2,1,0:T(8,128)(2,1)}, bf16[1,8,128,256]{3,2,1,0:T(8,128)(2,1)}) custom-call(s32[2,3,128]{2,1,0:T(4,128)} %pad_add_fusion.tables, s32[2]{0:T(128)} %pad_add_fusion.1.owners, s32[1]{0:T(128)} %bitcast.9.core, ...), custom_call_target="tpu_custom_call" | custom-call | flops 10000000000 | bytes 1024 | tf_op jit(solution)/shard_map/chip_sums/pallas_call | solution.py:100
  105.6 15.2 %chip_sums.3 = (bf16[2,8,128,256]{3,2,1,0:T(8,128)(2,1)}, bf16[2,8,128,256]{3,2,1,0:T(8,128)(2,1)}, bf16[2,8,128,256]{3,2,1,0:T(8,128)(2,1)}, bf16[3,8,128,256]{3,2,1,0:T(8,128)(2,1)}, bf16[3,8,128,256]{3,2,1,0:T(8,128)(2,1)}) custom-call(s32[2,3,128]{2,1,0:T(4,128)} %pad_add_fusion.tables, s32[6]{0:T(128)} %stack.60.owners, s32[1]{0:T(128)} %bitcast.9.core, ...), custom_call_target="tpu_custom_call" | custom-call | flops 17999998976 | bytes 1024 | tf_op jit(solution)/shard_map/chip_sums/pallas_call | solution.py:100
  124.0 2.6 %add_via.1 = (bf16[2,8,128,256]{3,2,1,0:T(8,128)(2,1)}, bf16[2,8,128,256]{3,2,1,0:T(8,128)(2,1)}) custom-call(bf16[2,8,128,256]{3,2,1,0:T(8,128)(2,1)} %get-tuple-element.91.up_in, bf16[2,8,128,256]{3,2,1,0:T(8,128)(2,1)} %get-tuple-element.92.down_in, bf16[2,4,128,256]{3,2,1,0:T(8,128)(2,1)} %copy-done.9, ...), custom_call_target="tpu_custom_call", output_to_operand_aliasing={{0}: (0, {}), {1}: (1, {})} | custom-call | tf_op jit(solution)/shard_map/add_via/pallas_call | solution.py:244
  128.6 3.5 %all-to-all-start.1 = ((bf16[4,32,16,256]{3,2,1,0:T(8,128)(2,1)}), bf16[4,32,16,256]{3,2,1,0:T(8,128)(2,1)S(1)}, u32[]{:S(2)}, u32[]{:S(2)}) async-start(bf16[4,32,16,256]{3,2,1,0:T(8,128)(2,1)} %copy.17), calls=%async_computation.1 | async-start | bytes 2097152 | tf_op jit(solution)/shard_map/all_to_all | solution.py:350
  135.1 10.8 %all-to-all-done.1 = bf16[4,32,16,256]{3,2,1,0:T(8,128)(2,1)S(1)} async-done(((bf16[4,32,16,256]{3,2,1,0:T(8,128)(2,1)}), bf16[4,32,16,256]{3,2,1,0:T(8,128)(2,1)S(1)}, u32[]{:S(2)}, u32[]{:S(2)}) %all-to-all-start.1) | async-done | bytes 1048608 | tf_op jit(solution)/shard_map/all_to_all | solution.py:350
  146.4 15.0 %collective-permute-done.28 = bf16[4,128,256]{2,1,0:T(8,128)(2,1)S(1)} collective-permute-done((bf16[4,128,256]{2,1,0:T(8,128)(2,1)}, bf16[4,128,256]{2,1,0:T(8,128)(2,1)S(1)}, u32[]{:S(2)}, u32[]{:S(2)}) %collective-permute-start.28) | collective-permute-done | bytes 262176 | tf_op jit(solution)/shard_map/ppermute | solution.py:25
  168.5 7.4 %collective-permute-done.31 = bf16[8,128,256]{2,1,0:T(8,128)(2,1)S(1)} collective-permute-done((bf16[8,128,256]{2,1,0:T(8,128)(2,1)S(1)}, bf16[8,128,256]{2,1,0:T(8,128)(2,1)S(1)}, u32[]{:S(2)}, u32[]{:S(2)}) %collective-permute-start.31) | collective-permute-done | bytes 524320 | tf_op jit(solution)/shard_map/ppermute | solution.py:25
  181.0 31.1 %all_to_all.20 = bf16[128,40,128]{2,1,0:T(8,128)(2,1)S(1)} all-to-all(bf16[128,40,128]{2,1,0:T(8,128)(2,1)S(1)} %pad_maximum_fusion), channel_id=1, replica_groups=mesh['xl'=2,'y'=4,'xh'=2,'z'=4,'core'=2] {'xl','y','xh','z','core'}, dimensions={0} | all-to-all | bytes 2621440 | tf_op jit(solution)/shard_map/all_to_all | solution.py:373
  213.1 4.5 %all-to-all-start.3 = ((f32[128,2,256]{2,1,0:T(2,128)}), f32[128,2,256]{2,1,0:T(2,128)S(1)}, u32[]{:S(2)}, u32[]{:S(2)}) async-start(f32[128,2,256]{2,1,0:T(2,128)} %broadcast_in_dim.2), calls=%async_computation.3 | async-start | bytes 524288 | tf_op jit(solution)/shard_map/all_to_all | solution.py:382
  218.8 9.9 %all-to-all-done.3 = f32[128,2,256]{2,1,0:T(2,128)S(1)} async-done(((f32[128,2,256]{2,1,0:T(2,128)}), f32[128,2,256]{2,1,0:T(2,128)S(1)}, u32[]{:S(2)}, u32[]{:S(2)}) %all-to-all-start.3) | async-done | bytes 262176 | tf_op jit(solution)/shard_map/all_to_all | solution.py:382
  (108 shorter events, 47.6 us)
Async XLA Ops:
  0.6 31.0 %collective-permute-start.4 = (bf16[8,8,2,128,128]{4,3,2,1,0:T(8,128)(2,1)}, bf16[8,8,2,128,128]{4,3,2,1,0:T(8,128)(2,1)}, u32[]{:S(2)}, u32[]{:S(2)}) collective-permute-start(bf16[8,8,2,128,128]{4,3,2,1,0:T(8,128)(2,1)} %bitcast.84), channel_id=1, source_target_pairs={{0,1},{1,0},{2,3},{3,2},{4,5},{5,4},{6,7},{7,6},{8,9},{9,8},{10,11... | collective-permute-start | bytes 12582920 | tf_op jit(solution)/shard_map/ppermute | solution.py:25
  2.1 24.9 %collective-permute-start.2 = (bf16[2048,256]{1,0:T(8,128)(2,1)}, bf16[2048,256]{1,0:T(8,128)(2,1)S(1)}, u32[]{:S(2)}, u32[]{:S(2)}) collective-permute-start(bf16[2048,256]{1,0:T(8,128)(2,1)} %refs_0_.3), channel_id=1, source_target_pairs={{0,64},{64,0},{1,65},{65,1},{2,66},{66,2},{3,67},{67,3},{4,68},{68... | collective-permute-start | bytes 3145736 | tf_op jit(solution)/shard_map/ppermute | solution.py:25
  3.5 25.2 %collective-permute-start.1 = (bf16[2048,256]{1,0:T(8,128)(2,1)}, bf16[2048,256]{1,0:T(8,128)(2,1)S(1)}, u32[]{:S(2)}, u32[]{:S(2)}) collective-permute-start(bf16[2048,256]{1,0:T(8,128)(2,1)} %refs_0_.3), channel_id=1, source_target_pairs={{0,48},{16,0},{32,16},{48,32},{1,49},{17,1},{33,17},{49,33},{2,50}... | collective-permute-start | bytes 3145736 | tf_op jit(solution)/shard_map/ppermute | solution.py:25
  6.2 25.5 %collective-permute-start = (bf16[2048,256]{1,0:T(8,128)(2,1)}, bf16[2048,256]{1,0:T(8,128)(2,1)S(1)}, u32[]{:S(2)}, u32[]{:S(2)}) collective-permute-start(bf16[2048,256]{1,0:T(8,128)(2,1)} %refs_0_.3), channel_id=1, source_target_pairs={{0,16},{16,32},{32,48},{48,0},{1,17},{17,33},{33,49},{49,1},{2,18}... | collective-permute-start | bytes 3145736 | tf_op jit(solution)/shard_map/ppermute | solution.py:25
  36.2 27.4 %collective-permute-start.5 = (bf16[2304,256]{1,0:T(8,128)(2,1)}, bf16[2304,256]{1,0:T(8,128)(2,1)S(1)}, u32[]{:S(2)}, u32[]{:S(2)}) collective-permute-start(bf16[2304,256]{1,0:T(8,128)(2,1)} %get-tuple-element.72), channel_id=1, source_target_pairs={{0,16},{16,32},{32,48},{48,0},{1,17},{17,33},{33,49},{49,1},{2,18}... | collective-permute-start | bytes 3538952 | tf_op jit(solution)/shard_map/ppermute | solution.py:25
  36.3 17.9 %collective-permute-start.7 = (bf16[1536,256]{1,0:T(8,128)(2,1)}, bf16[1536,256]{1,0:T(8,128)(2,1)}, u32[]{:S(2)}, u32[]{:S(2)}) collective-permute-start(bf16[1536,256]{1,0:T(8,128)(2,1)} %get-tuple-element.74), channel_id=1, source_target_pairs={{0,64},{64,0},{1,65},{65,1},{2,66},{66,2},{3,67},{67,3},{4,68},{68... | collective-permute-start | bytes 2359304 | tf_op jit(solution)/shard_map/ppermute | solution.py:25
  36.6 35.0 %collective-permute-start.6 = (bf16[2304,256]{1,0:T(8,128)(2,1)}, bf16[2304,256]{1,0:T(8,128)(2,1)S(1)}, u32[]{:S(2)}, u32[]{:S(2)}) collective-permute-start(bf16[2304,256]{1,0:T(8,128)(2,1)} %get-tuple-element.73), channel_id=1, source_target_pairs={{0,48},{16,0},{32,16},{48,32},{1,49},{17,1},{33,17},{49,33},{2,50}... | collective-permute-start | bytes 3538952 | tf_op jit(solution)/shard_map/ppermute | solution.py:25
  39.2 32.5 %collective-permute-start.11 = (bf16[2048,256]{1,0:T(8,128)(2,1)}, bf16[2048,256]{1,0:T(8,128)(2,1)}, u32[]{:S(2)}, u32[]{:S(2)}) collective-permute-start(bf16[2048,256]{1,0:T(8,128)(2,1)} %refs_0_.3), channel_id=1, source_target_pairs={{0,1},{1,0},{2,3},{3,2},{4,5},{5,4},{6,7},{7,6},{8,9},{9,8},{10,11... | collective-permute-start | bytes 3145736 | tf_op jit(solution)/shard_map/ppermute | solution.py:25
  43.8 27.7 %all-to-all-start = ((bf16[32,4,16,256]{3,2,1,0:T(8,128)(2,1)}), bf16[32,4,16,256]{3,2,1,0:T(8,128)(2,1)S(1)}, u32[]{:S(2)}, u32[]{:S(2)}) async-start(bf16[32,4,16,256]{3,2,1,0:T(8,128)(2,1)} %bitcast.12), calls=%async_computation | async-start | bytes 2097152 | tf_op jit(solution)/shard_map/all_to_all | solution.py:346
  51.9 22.7 %collective-permute-start.13 = (bf16[2048,256]{1,0:T(8,128)(2,1)}, bf16[2048,256]{1,0:T(8,128)(2,1)}, u32[]{:S(2)}, u32[]{:S(2)}) collective-permute-start(bf16[2048,256]{1,0:T(8,128)(2,1)} %copy-done.5), channel_id=1, source_target_pairs={{0,1},{1,0},{2,3},{3,2},{4,5},{5,4},{6,7},{7,6},{8,9},{9,8},{10,11... | collective-permute-start | bytes 3145736 | tf_op jit(solution)/shard_map/ppermute | solution.py:25
  54.2 20.5 %collective-permute-start.14 = (bf16[2048,256]{1,0:T(8,128)(2,1)}, bf16[2048,256]{1,0:T(8,128)(2,1)}, u32[]{:S(2)}, u32[]{:S(2)}) collective-permute-start(bf16[2048,256]{1,0:T(8,128)(2,1)} %copy-done.4), channel_id=1, source_target_pairs={{0,1},{1,0},{2,3},{3,2},{4,5},{5,4},{6,7},{7,6},{8,9},{9,8},{10,11... | collective-permute-start | bytes 3145736 | tf_op jit(solution)/shard_map/ppermute | solution.py:25
  63.6 13.7 %collective-permute-start.12 = (bf16[2048,256]{1,0:T(8,128)(2,1)}, bf16[2048,256]{1,0:T(8,128)(2,1)}, u32[]{:S(2)}, u32[]{:S(2)}) collective-permute-start(bf16[2048,256]{1,0:T(8,128)(2,1)} %copy-done.6), channel_id=1, source_target_pairs={{0,1},{1,0},{2,3},{3,2},{4,5},{5,4},{6,7},{7,6},{8,9},{9,8},{10,11... | collective-permute-start | bytes 3145736 | tf_op jit(solution)/shard_map/ppermute | solution.py:25
  71.5 20.2 %collective-permute-start.15 = (bf16[2304,256]{1,0:T(8,128)(2,1)S(1)}, bf16[2304,256]{1,0:T(8,128)(2,1)}, u32[]{:S(2)}, u32[]{:S(2)}) collective-permute-start(bf16[2304,256]{1,0:T(8,128)(2,1)S(1)} %collective-permute-done.5.refs_0_.refs_4_), channel_id=1, source_target_pairs={{0,1},{1,0},{2,3},{3,2},{4,5},{5,4},{6,7},{7,6},{8,9},{9,8},{10,11... | collective-permute-start | bytes 3538952 | tf_op jit(solution)/shard_map/ppermute | solution.py:25
  71.7 20.1 %collective-permute-start.16 = (bf16[2304,256]{1,0:T(8,128)(2,1)S(1)}, bf16[2304,256]{1,0:T(8,128)(2,1)}, u32[]{:S(2)}, u32[]{:S(2)}) collective-permute-start(bf16[2304,256]{1,0:T(8,128)(2,1)S(1)} %collective-permute-done.6.refs_1_.refs_5_), channel_id=1, source_target_pairs={{0,1},{1,0},{2,3},{3,2},{4,5},{5,4},{6,7},{7,6},{8,9},{9,8},{10,11... | collective-permute-start | bytes 3538952 | tf_op jit(solution)/shard_map/ppermute | solution.py:25
  102.1 18.7 %collective-permute-start.21 = (bf16[2,4,128,256]{3,2,1,0:T(8,128)(2,1)}, bf16[2,4,128,256]{3,2,1,0:T(8,128)(2,1)S(1)}, u32[]{:S(2)}, u32[]{:S(2)}) collective-permute-start(bf16[2,4,128,256]{3,2,1,0:T(8,128)(2,1)} %get-tuple-element.82), channel_id=1, source_target_pairs={{0,2},{2,4},{4,6},{6,0},{1,3},{3,5},{5,7},{7,1},{8,10},{10,12},{12... | collective-permute-start | bytes 1572872 | tf_op jit(solution)/shard_map/ppermute | solution.py:25
  102.9 17.9 %collective-permute-start.22 = (bf16[2,4,128,256]{3,2,1,0:T(8,128)(2,1)}, bf16[2,4,128,256]{3,2,1,0:T(8,128)(2,1)S(1)}, u32[]{:S(2)}, u32[]{:S(2)}) collective-permute-start(bf16[2,4,128,256]{3,2,1,0:T(8,128)(2,1)} %get-tuple-element.83), channel_id=1, source_target_pairs={{0,6},{2,0},{4,2},{6,4},{1,7},{3,1},{5,3},{7,5},{8,14},{10,8},{12,... | collective-permute-start | bytes 1572872 | tf_op jit(solution)/shard_map/ppermute | solution.py:25
  104.9 16.0 %collective-permute-start.23 = (bf16[1,8,128,256]{3,2,1,0:T(8,128)(2,1)}, bf16[1,8,128,256]{3,2,1,0:T(8,128)(2,1)S(1)}, u32[]{:S(2)}, u32[]{:S(2)}) collective-permute-start(bf16[1,8,128,256]{3,2,1,0:T(8,128)(2,1)} %get-tuple-element.84), channel_id=1, source_target_pairs={{0,8},{8,0},{1,9},{9,1},{2,10},{10,2},{3,11},{11,3},{4,12},{12,4},... | collective-permute-start | bytes 1572872 | tf_op jit(solution)/shard_map/ppermute | solution.py:25
  121.8 41.0 %collective-permute-start.26 = (bf16[3,8,128,256]{3,2,1,0:T(8,128)(2,1)}, bf16[3,8,128,256]{3,2,1,0:T(8,128)(2,1)S(1)}, u32[]{:S(2)}, u32[]{:S(2)}) collective-permute-start(bf16[3,8,128,256]{3,2,1,0:T(8,128)(2,1)} %get-tuple-element.97), channel_id=1, source_target_pairs={{0,8},{8,0},{1,9},{9,1},{2,10},{10,2},{3,11},{11,3},{4,12},{12,4},... | collective-permute-start | bytes 4718600 | tf_op jit(solution)/shard_map/ppermute | solution.py:25
  128.6 17.3 %all-to-all-start.1 = ((bf16[4,32,16,256]{3,2,1,0:T(8,128)(2,1)}), bf16[4,32,16,256]{3,2,1,0:T(8,128)(2,1)S(1)}, u32[]{:S(2)}, u32[]{:S(2)}) async-start(bf16[4,32,16,256]{3,2,1,0:T(8,128)(2,1)} %copy.17), calls=%async_computation.1 | async-start | bytes 2097152 | tf_op jit(solution)/shard_map/all_to_all | solution.py:350
  132.1 30.7 %collective-permute-start.25 = (bf16[2,8,128,256]{3,2,1,0:T(8,128)(2,1)}, bf16[2,8,128,256]{3,2,1,0:T(8,128)(2,1)}, u32[]{:S(2)}, u32[]{:S(2)}) collective-permute-start(bf16[2,8,128,256]{3,2,1,0:T(8,128)(2,1)} %get-tuple-element.96), channel_id=1, source_target_pairs={{0,6},{2,0},{4,2},{6,4},{1,7},{3,1},{5,3},{7,5},{8,14},{10,8},{12,... | collective-permute-start | bytes 3145736 | tf_op jit(solution)/shard_map/ppermute | solution.py:25
  132.2 30.7 %collective-permute-start.24 = (bf16[2,8,128,256]{3,2,1,0:T(8,128)(2,1)}, bf16[2,8,128,256]{3,2,1,0:T(8,128)(2,1)}, u32[]{:S(2)}, u32[]{:S(2)}) collective-permute-start(bf16[2,8,128,256]{3,2,1,0:T(8,128)(2,1)} %get-tuple-element.95), channel_id=1, source_target_pairs={{0,2},{2,4},{4,6},{6,0},{1,3},{3,5},{5,7},{7,1},{8,10},{10,12},{12... | collective-permute-start | bytes 3145736 | tf_op jit(solution)/shard_map/ppermute | solution.py:25
  133.6 27.7 %collective-permute-start.28 = (bf16[4,128,256]{2,1,0:T(8,128)(2,1)}, bf16[4,128,256]{2,1,0:T(8,128)(2,1)S(1)}, u32[]{:S(2)}, u32[]{:S(2)}) collective-permute-start(bf16[4,128,256]{2,1,0:T(8,128)(2,1)} %get-tuple-element.128), channel_id=1, source_target_pairs={{0,6},{2,0},{4,2},{6,4},{1,7},{3,1},{5,3},{7,5},{8,14},{10,8},{12,... | collective-permute-start | bytes 786440 | tf_op jit(solution)/shard_map/ppermute | solution.py:25
  135.1 27.7 %collective-permute-start.27 = (bf16[4,128,256]{2,1,0:T(8,128)(2,1)S(1)}, bf16[4,128,256]{2,1,0:T(8,128)(2,1)S(1)}, u32[]{:S(2)}, u32[]{:S(2)}) collective-permute-start(bf16[4,128,256]{2,1,0:T(8,128)(2,1)S(1)} %get-tuple-element.129), channel_id=1, source_target_pairs={{0,2},{2,4},{4,6},{6,0},{1,3},{3,5},{5,7},{7,1},{8,10},{10,12},{12... | collective-permute-start | bytes 786440 | tf_op jit(solution)/shard_map/ppermute | solution.py:25
  213.1 15.7 %all-to-all-start.3 = ((f32[128,2,256]{2,1,0:T(2,128)}), f32[128,2,256]{2,1,0:T(2,128)S(1)}, u32[]{:S(2)}, u32[]{:S(2)}) async-start(f32[128,2,256]{2,1,0:T(2,128)} %broadcast_in_dim.2), calls=%async_computation.3 | async-start | bytes 524288 | tf_op jit(solution)/shard_map/all_to_all | solution.py:382
  (22 other events, 324.5 us)
